TPU v7x, 32 devices: a whole 2x2x4 slice. The times are simulated.
32 devices in a mesh: var: 4 (over y, x), patch: 8 (over z, core).
Axes of the slice: x: 2, y: 2, z: 4, core: 2. Of those that a mesh axis runs over, the one named last changes fastest.
Arguments:
- field_patches: bfloat16 [48, 4, 8, 2048], P('var', None, 'patch'), may hold values from -6 to 6
- var_ids: int32 [48], replicated, may hold values from 0 to 47, each once
- lead_bucket: int32 [8], P('patch'), may hold values from 0 to 7
- patch_weight: bfloat16 [48, 4, 1024], P('var'), may hold values from -3 to 3
- var_embed: bfloat16 [48, 1024], replicated, may hold values from -6 to 6
- agg_query: bfloat16 [1024], replicated, may hold values from -6 to 6
- agg_key: bfloat16 [1024, 1024], replicated, may hold values from -0.1875 to 0.1875
- agg_value: bfloat16 [1024, 1024], replicated, may hold values from -0.1875 to 0.1875
- agg_out: bfloat16 [1024, 1024], replicated, may hold values from -0.375 to 0.375
- lead_table: bfloat16 [8, 1024], replicated, may hold values from -3 to 3
- ln1_gain: bfloat16 [1024], replicated, may hold values from 0.099609375 to 1.8984375
- attn_qkv: bfloat16 [1024, 3072], replicated, may hold values from -0.25 to 0.25
- attn_out: bfloat16 [1024, 1024], replicated, may hold values from -1.5 to 1.5
- ln2_gain: bfloat16 [1024], replicated, may hold values from 0.099609375 to 1.8984375
- mlp_in: bfloat16 [1024, 4096], replicated, may hold values from -0.1875 to 0.1875
- mlp_in_bias: bfloat16 [4096], replicated, may hold values from -3 to 3
- mlp_out: bfloat16 [4096, 1024], replicated, may hold values from -0.125 to 0.125
- cotangent: bfloat16 [8, 2048, 1024], P('patch', 'var'), may hold values from -6 to 6
Outputs:
- output: bfloat16 [8, 2048, 1024], P('patch', 'var')
- field_grad: float32 [48, 4, 8, 2048], P('var', None, 'patch')
- patch_weight_grad: float32 [48, 4, 1024], P('var')
- var_embed_grad: float32 [48, 1024], P('var')
- agg_query_grad: float32 [1024], P('var')
- agg_key_grad: float32 [1024, 1024], P('var')
- agg_value_grad: float32 [1024, 1024], P('var')
- agg_out_grad: float32 [1024, 1024], P('var')
- lead_table_grad: float32 [8, 1024], P('var')
- ln1_gain_grad: float32 [1024], P('var')
- attn_qkv_grad: float32 [1024, 3072], P('var')
- attn_out_grad: float32 [1024, 1024], P('var')
- ln2_gain_grad: float32 [1024], P('var')
- mlp_in_grad: float32 [1024, 4096], P('var')
- mlp_in_bias_grad: float32 [4096], P('var')
- mlp_out_grad: float32 [4096, 1024], P('var')
Inputs may be any that keep to these rules, and one draw needn't show every extreme that they name: var_ids names each of the 48 variables once.
All inputs are finite; a program needn't handle non-finite values.
Results may differ from a plain program's by a relative error of at most 0.02.
Values may be sent and summed in bfloat16 or wider, within the bound.
No kernel may reach another device: no remote copies, remote signals or barrier semaphores. Data moves between devices by JAX's collectives and lax.ppermute only.
A program may use at most 256 MiB of HBM per device.

v0:
```python
from functools import partial

import jax
import jax.numpy as jnp
from jax import lax
from jax.sharding import PartitionSpec as P

HEADS = 16


highest = lax.Precision.HIGHEST
epsilon = 1e-05


def layer_norm(inputs, gain_vector):
    centered = inputs - jnp.mean(inputs, axis=-1, keepdims=True)
    inverse = lax.rsqrt(jnp.mean(centered * centered, axis=-1, keepdims=True) + epsilon)
    normed = centered * inverse
    return (normed * gain_vector.astype(jnp.float32), normed, inverse)


def norm_back(grad_rows, normed, inverse, gain_vector):
    grad_gain = jnp.sum(grad_rows * normed, axis=0)
    grad_normed = grad_rows * gain_vector.astype(jnp.float32)
    first_mean = jnp.mean(grad_normed, axis=-1, keepdims=True)
    second_mean = jnp.mean(grad_normed * normed, axis=-1, keepdims=True)
    return (inverse * (grad_normed - first_mean - normed * second_mean), grad_gain)


def front_terms(pixels_low, weight_rows, embed_rows, query_keys, value_weight):
    channels = pixels_low.shape[0]
    pixels = pixels_low.astype(jnp.float32)
    key_pixels = jnp.einsum(
        "vcd,dh->vch", weight_rows.astype(jnp.float32), query_keys, precision=highest
    )
    key_embeds = jnp.dot(embed_rows.astype(jnp.float32), query_keys, precision=highest)
    scores = (
        jnp.einsum("vcr,vch->vhr", pixels, key_pixels, precision=highest) + key_embeds[:, :, None]
    )
    stacked = jnp.concatenate([weight_rows, embed_rows[:, None, :]], axis=1)
    projected = jnp.einsum("vkd,de->vke", stacked, value_weight, preferred_element_type=jnp.float32)
    extended = jnp.concatenate(
        [pixels, jnp.ones((channels, 1, pixels.shape[2]), jnp.float32)], axis=1
    )
    return (key_pixels, scores, stacked, projected, extended)


def value_sums(soft, extended, projected):
    heads_here = soft.shape[1]
    weighted = soft[:, None, :, :] * extended[:, :, None, :]
    per_head = projected.reshape(projected.shape[0], projected.shape[1], heads_here, -1)
    summed = jnp.einsum("vkhr,vkhe->her", weighted, per_head, precision=highest)
    return summed.reshape(-1, summed.shape[2])


def front_back(
    key_pixels,
    scores,
    stacked,
    projected,
    extended,
    query_keys,
    value_weight,
    log_rows,
    delta_rows,
    grad_rows,
):
    channels, kinds = (extended.shape[0], extended.shape[1])
    heads_here = scores.shape[1]
    soft = jnp.exp(scores - log_rows[None])
    per_head = projected.reshape(channels, kinds, heads_here, -1)
    grad_heads = grad_rows.astype(jnp.float32).reshape(heads_here, -1, grad_rows.shape[1])
    through = jnp.einsum("vkhe,her->vkhr", per_head, grad_heads, precision=highest)
    grad_soft = jnp.sum(extended[:, :, None, :] * through, axis=1)
    grad_scores = soft * (grad_soft - delta_rows[None])
    weighted = soft[:, None, :, :] * extended[:, :, None, :]
    grad_projected = jnp.einsum("vkhr,her->vkhe", weighted, grad_heads, precision=highest).reshape(
        channels, kinds, -1
    )
    grad_extended = jnp.sum(soft[:, None, :, :] * through, axis=2)
    pixels = extended[:, :-1]
    grad_pixels = grad_extended[:, :-1] + jnp.einsum(
        "vhr,vch->vcr", grad_scores, key_pixels, precision=highest
    )
    grad_keypix = jnp.einsum("vhr,vcr->vch", grad_scores, pixels, precision=highest)
    grad_keyemb = jnp.sum(grad_scores, axis=2)
    grad_stacked = jnp.einsum(
        "vke,de->vkd", grad_projected, value_weight.astype(jnp.float32), precision=highest
    )
    stacked_wide = stacked.astype(jnp.float32)
    grad_value = jnp.einsum("vkd,vke->de", stacked_wide, grad_projected, precision=highest)
    grad_weights = grad_stacked[:, :-1] + jnp.einsum(
        "vch,dh->vcd", grad_keypix, query_keys, precision=highest
    )
    grad_embeds = grad_stacked[:, -1] + jnp.dot(grad_keyemb, query_keys.T, precision=highest)
    grad_query_keys = jnp.einsum(
        "vcd,vch->dh", stacked_wide[:, :-1], grad_keypix, precision=highest
    )
    grad_query_keys = grad_query_keys + jnp.dot(
        stacked_wide[:, -1].T, grad_keyemb, precision=highest
    )
    return (grad_pixels, grad_weights, grad_embeds, grad_value, grad_query_keys)


def attend_item(inputs, block_rows):
    query_all, key_all, value_all = inputs
    group_heads, length, head_dim = query_all.shape
    count_blocks = length // block_rows
    blocks = query_all.reshape(group_heads, count_blocks, block_rows, head_dim).transpose(
        1, 0, 2, 3
    )

    def one_block(carried, query_block):
        scores = (
            jnp.einsum("hqd,hkd->hqk", query_block, key_all, preferred_element_type=jnp.float32)
            * 0.125
        )
        row_top = jnp.max(scores, axis=-1, keepdims=True)
        exponent = jnp.exp(scores - row_top)
        row_total = jnp.sum(exponent, axis=-1, keepdims=True)
        weights_low = (exponent / row_total).astype(jnp.bfloat16)
        mixed_rows = jnp.einsum(
            "hqk,hkd->hqd", weights_low, value_all, preferred_element_type=jnp.float32
        )
        return (carried, (mixed_rows.astype(jnp.bfloat16), (row_top + jnp.log(row_total))[..., 0]))

    unused, (mixed_rows, log_sums) = lax.scan(one_block, jnp.float32(0.0), blocks)
    mixed_rows = mixed_rows.transpose(1, 0, 2, 3).reshape(group_heads, length, head_dim)
    log_sums = log_sums.transpose(1, 0, 2).reshape(group_heads, length)
    return (mixed_rows, log_sums)


def attend_back(inputs, block_rows):
    query_all, key_all, value_all, grad_all, lse_all = inputs
    group_heads, length, head_dim = query_all.shape
    count_blocks = length // block_rows
    query_blocks = query_all.reshape(group_heads, count_blocks, block_rows, head_dim).transpose(
        1, 0, 2, 3
    )
    grad_blocks = grad_all.reshape(group_heads, count_blocks, block_rows, head_dim).transpose(
        1, 0, 2, 3
    )
    lse_blocks = lse_all.reshape(group_heads, count_blocks, block_rows).transpose(1, 0, 2)

    def one_block(carried, pieces):
        query_block, grad_block, lse_block = pieces
        grad_keys, grad_values = carried
        scores = (
            jnp.einsum("hqd,hkd->hqk", query_block, key_all, preferred_element_type=jnp.float32)
            * 0.125
        )
        weights_full = jnp.exp(scores - lse_block[..., None])
        grad_weights = jnp.einsum(
            "hqd,hkd->hqk", grad_block, value_all, preferred_element_type=jnp.float32
        )
        row_delta = jnp.sum(weights_full * grad_weights, axis=-1, keepdims=True)
        grad_scores = (weights_full * (grad_weights - row_delta)).astype(jnp.bfloat16)
        grad_query = (
            jnp.einsum("hqk,hkd->hqd", grad_scores, key_all, preferred_element_type=jnp.float32)
            * 0.125
        )
        grad_keys = (
            grad_keys
            + jnp.einsum(
                "hqk,hqd->hkd", grad_scores, query_block, preferred_element_type=jnp.float32
            )
            * 0.125
        )
        grad_values = grad_values + jnp.einsum(
            "hqk,hqd->hkd",
            weights_full.astype(jnp.bfloat16),
            grad_block,
            preferred_element_type=jnp.float32,
        )
        return ((grad_keys, grad_values), grad_query.astype(jnp.bfloat16))

    zeros_rows = jnp.zeros(key_all.shape, jnp.float32)
    (grad_keys, grad_values), grad_query = lax.scan(
        one_block, (zeros_rows, zeros_rows), (query_blocks, grad_blocks, lse_blocks)
    )
    grad_query = grad_query.transpose(1, 0, 2, 3).reshape(group_heads, length, head_dim)
    return (grad_query, grad_keys, grad_values)


def body(
    field_patches,
    var_ids,
    lead_bucket,
    patch_weight,
    var_embed,
    agg_query,
    agg_key,
    agg_value,
    agg_out,
    lead_table,
    ln1_gain,
    attn_qkv,
    attn_out,
    ln2_gain,
    mlp_in,
    mlp_in_bias,
    mlp_out,
    cotangent,
):
    groups = lax.axis_size("var")
    member = lax.axis_index("var")
    local_vars, pixel_count, samples_here, seq_len = field_patches.shape
    width = agg_key.shape[0]
    lead_count = lead_table.shape[0]
    vocab = var_embed.shape[0]
    quarter = seq_len // groups
    row_count = samples_here * quarter
    head_dim = width // HEADS
    head_groups = HEADS // 4
    block_rows = min(512, quarter)
    query_heads = agg_query.reshape(HEADS, head_dim)
    query_keys = (
        jnp.einsum(
            "dhc,hc->dh",
            agg_key.reshape(width, HEADS, head_dim),
            query_heads,
            preferred_element_type=jnp.float32,
        )
        * 0.125
    )
    ids_here = lax.dynamic_slice_in_dim(var_ids, member * local_vars, local_vars)
    front_rows = samples_here * seq_len
    pixel_rows = field_patches.reshape(local_vars, pixel_count, front_rows)
    table_pick = (ids_here[:, None] == jnp.arange(vocab, dtype=jnp.int32)[None, :]).astype(
        jnp.bfloat16
    )
    embed_rows = jnp.dot(table_pick, var_embed, preferred_element_type=jnp.float32).astype(
        jnp.bfloat16
    )
    key_pixels, scores, stacked, projected, extended = front_terms(
        pixel_rows, patch_weight, embed_rows, query_keys, agg_value
    )
    row_top = jnp.max(scores, axis=0)
    soft = jnp.exp(scores - row_top[None])
    row_total = jnp.sum(soft, axis=0)
    sums = value_sums(soft, extended, projected)
    parts = (
        lax.all_to_all(
            row_top.reshape(1, HEADS, samples_here, seq_len),
            "var",
            split_axis=3,
            concat_axis=0,
            tiled=True,
        ),
        lax.all_to_all(
            row_total.reshape(1, HEADS, samples_here, seq_len),
            "var",
            split_axis=3,
            concat_axis=0,
            tiled=True,
        ),
        lax.all_to_all(
            sums.reshape(1, width, samples_here, seq_len),
            "var",
            split_axis=3,
            concat_axis=0,
            tiled=True,
        ),
    )
    top_all = jnp.max(parts[0], axis=0)
    scale = jnp.exp(parts[0] - top_all[None])
    total_all = jnp.sum(scale * parts[1], axis=0)
    sums_all = jnp.sum(
        parts[2].reshape(groups, HEADS, head_dim, samples_here, quarter) * scale[:, :, None], axis=0
    )
    attended = sums_all.reshape(HEADS, head_dim, row_count) / total_all
    log_sums = (top_all + jnp.log(total_all)).reshape(HEADS, row_count)
    attended = attended.reshape(width, row_count)
    att_low = attended.astype(jnp.bfloat16)
    agg_rows = jnp.einsum("dr,de->re", att_low, agg_out, preferred_element_type=jnp.float32)
    lead_pick = (lead_bucket[:, None] == jnp.arange(lead_count, dtype=jnp.int32)[None, :]).astype(
        jnp.float32
    )
    lead_rows = jnp.dot(lead_pick, lead_table.astype(jnp.float32), precision=highest)
    resid_zero = (agg_rows.reshape(samples_here, quarter, width) + lead_rows[:, None, :]).reshape(
        row_count, width
    )
    normed_one, plain_one, inverse_one = layer_norm(resid_zero, ln1_gain)
    hidden_one = normed_one.astype(jnp.bfloat16)
    projections = jnp.dot(hidden_one, attn_qkv, preferred_element_type=jnp.float32)
    queries = projections[:, :width].astype(jnp.bfloat16).reshape(samples_here, quarter, width)
    key_local = (
        projections[:, width : 2 * width].astype(jnp.bfloat16).reshape(samples_here, quarter, width)
    )
    value_local = (
        projections[:, 2 * width :].astype(jnp.bfloat16).reshape(samples_here, quarter, width)
    )

    def to_items(tensor, length):
        shaped = tensor.reshape(samples_here, length, head_groups, 4, head_dim).transpose(
            0, 2, 3, 1, 4
        )
        return shaped.reshape(samples_here * head_groups, 4, length, head_dim)

    def from_items(tensor, length):
        shaped = tensor.reshape(samples_here, head_groups, 4, length, head_dim).transpose(
            0, 3, 1, 2, 4
        )
        return shaped.reshape(samples_here * length, width)

    key_full, value_full = (
        lax.all_gather(key_local, "var", axis=1, tiled=True),
        lax.all_gather(value_local, "var", axis=1, tiled=True),
    )
    query_items = to_items(queries, quarter)
    key_items = to_items(key_full, seq_len)
    value_items = to_items(value_full, seq_len)
    mixed_items, lse_items = lax.map(
        partial(attend_item, block_rows=block_rows), (query_items, key_items, value_items)
    )
    mixed = from_items(mixed_items, quarter)
    resid_one = resid_zero + jnp.dot(mixed, attn_out, preferred_element_type=jnp.float32)
    normed_two, plain_two, inverse_two = layer_norm(resid_one, ln2_gain)
    hidden_two = normed_two.astype(jnp.bfloat16)
    inner = jnp.dot(hidden_two, mlp_in, preferred_element_type=jnp.float32) + mlp_in_bias.astype(
        jnp.float32
    )
    activated = jax.nn.gelu(inner, approximate=False).astype(jnp.bfloat16)
    branch_mlp = jnp.dot(activated, mlp_out, preferred_element_type=jnp.float32)
    output = (resid_one + branch_mlp).astype(jnp.bfloat16).reshape(samples_here, quarter, width)
    grad_out = cotangent.reshape(row_count, width)
    grad_mlp_out = jnp.einsum("rf,rd->fd", activated, grad_out, preferred_element_type=jnp.float32)
    grad_act = jnp.einsum("rd,fd->rf", grad_out, mlp_out, preferred_element_type=jnp.float32)
    unused, gelu_back = jax.vjp(partial(jax.nn.gelu, approximate=False), inner)
    grad_inner = gelu_back(grad_act)[0].astype(jnp.bfloat16)
    grad_mlp_in = jnp.einsum(
        "rd,rf->df", hidden_two, grad_inner, preferred_element_type=jnp.float32
    )
    grad_bias = jnp.sum(grad_inner.astype(jnp.float32), axis=0)
    grad_hidden_two = jnp.einsum(
        "rf,df->rd", grad_inner, mlp_in, preferred_element_type=jnp.float32
    )
    grad_norm_two, grad_gain_two = norm_back(grad_hidden_two, plain_two, inverse_two, ln2_gain)
    grad_resid_one = grad_out.astype(jnp.float32) + grad_norm_two
    grad_branch = grad_resid_one.astype(jnp.bfloat16)
    grad_attn_out = jnp.einsum("rd,re->de", mixed, grad_branch, preferred_element_type=jnp.float32)
    grad_mixed = jnp.einsum(
        "re,de->rd", grad_branch, attn_out, preferred_element_type=jnp.float32
    ).astype(jnp.bfloat16)
    grad_query_items, grad_key_items, grad_value_items = lax.map(
        partial(attend_back, block_rows=block_rows),
        (
            query_items,
            key_items,
            value_items,
            to_items(grad_mixed.reshape(samples_here, quarter, width), quarter),
            lse_items,
        ),
    )
    grad_queries = from_items(grad_query_items, quarter)
    grad_keys_full = from_items(grad_key_items, seq_len).reshape(samples_here, seq_len, width)
    grad_values_full = from_items(grad_value_items, seq_len).reshape(samples_here, seq_len, width)
    grad_keys, grad_values = (
        lax.psum_scatter(grad_keys_full, "var", scatter_dimension=1, tiled=True),
        lax.psum_scatter(grad_values_full, "var", scatter_dimension=1, tiled=True),
    )
    grad_key_rows = grad_keys.reshape(row_count, width).astype(jnp.bfloat16)
    grad_value_rows = grad_values.reshape(row_count, width).astype(jnp.bfloat16)
    grad_proj = jnp.concatenate([grad_queries, grad_key_rows, grad_value_rows], axis=1)
    grad_qkv = jnp.einsum("rd,re->de", hidden_one, grad_proj, preferred_element_type=jnp.float32)
    grad_hidden_one = jnp.einsum(
        "re,de->rd", grad_proj, attn_qkv, preferred_element_type=jnp.float32
    )
    grad_norm_one, grad_gain_one = norm_back(grad_hidden_one, plain_one, inverse_one, ln1_gain)
    grad_resid_zero = grad_resid_one + grad_norm_one
    sample_sums = jnp.sum(grad_resid_zero.reshape(samples_here, quarter, width), axis=1)
    grad_lead = jnp.dot(lead_pick.T, sample_sums, precision=highest)
    grad_agg = grad_resid_zero.astype(jnp.bfloat16)
    grad_agg_out = jnp.einsum("dr,re->de", att_low, grad_agg, preferred_element_type=jnp.float32)
    grad_att = jnp.einsum(
        "re,de->dr", grad_agg, agg_out, preferred_element_type=jnp.float32
    ).astype(jnp.bfloat16)
    deltas = jnp.sum(
        (grad_att.astype(jnp.float32) * attended).reshape(HEADS, head_dim, row_count), axis=1
    )
    grad_rows = lax.all_gather(
        grad_att.reshape(width, samples_here, quarter), "var", axis=2, tiled=True
    ).reshape(width, front_rows)
    log_rows, delta_rows = (
        lax.all_gather(log_sums.reshape(HEADS, samples_here, quarter), "var", axis=2, tiled=True),
        lax.all_gather(deltas.reshape(HEADS, samples_here, quarter), "var", axis=2, tiled=True),
    )
    log_rows = log_rows.reshape(HEADS, front_rows)
    delta_rows = delta_rows.reshape(HEADS, front_rows)
    grad_pixels, grad_weights, grad_embeds, grad_value, grad_query_keys = front_back(
        key_pixels,
        scores,
        stacked,
        projected,
        extended,
        query_keys,
        agg_value,
        log_rows,
        delta_rows,
        grad_rows,
    )
    grad_table = jnp.dot(table_pick.astype(jnp.float32).T, grad_embeds, precision=highest)
    grad_query = (
        jnp.einsum(
            "dhc,dh->hc",
            agg_key.astype(jnp.float32).reshape(width, HEADS, head_dim),
            grad_query_keys,
            precision=highest,
        ).reshape(width)
        * 0.125
    )
    field_grad = grad_pixels.reshape(local_vars, pixel_count, samples_here, seq_len)
    grad_patch = lax.dynamic_update_slice_in_dim(
        jnp.zeros((vocab, pixel_count, width), jnp.float32), grad_weights, member * local_vars, 0
    )
    width_part = width // groups
    parts_in = (
        lax.psum_scatter(grad_qkv, "var", scatter_dimension=0, tiled=True),
        lax.psum_scatter(grad_attn_out, "var", scatter_dimension=0, tiled=True),
        lax.psum_scatter(grad_mlp_in, "var", scatter_dimension=0, tiled=True),
        lax.psum_scatter(grad_mlp_out, "var", scatter_dimension=0, tiled=True),
        lax.psum_scatter(grad_lead, "var", scatter_dimension=0, tiled=True),
        lax.psum_scatter(grad_agg_out, "var", scatter_dimension=0, tiled=True),
        lax.psum_scatter(grad_value, "var", scatter_dimension=0, tiled=True),
        lax.psum_scatter(grad_query_keys, "var", scatter_dimension=0, tiled=True),
        lax.psum_scatter(grad_table, "var", scatter_dimension=0, tiled=True),
        lax.psum_scatter(grad_patch, "var", scatter_dimension=0, tiled=True),
        lax.psum_scatter(grad_gain_one, "var", scatter_dimension=0, tiled=True),
        lax.psum_scatter(grad_gain_two, "var", scatter_dimension=0, tiled=True),
        lax.psum_scatter(grad_query, "var", scatter_dimension=0, tiled=True),
        lax.psum_scatter(grad_bias, "var", scatter_dimension=0, tiled=True),
    )
    totals = lax.psum(
        (
            parts_in[0],
            parts_in[1],
            parts_in[2],
            parts_in[3],
            parts_in[4],
            parts_in[5],
            parts_in[6],
            parts_in[7],
            parts_in[8],
            parts_in[9],
            parts_in[10],
            parts_in[11],
            parts_in[12],
            parts_in[13],
        ),
        "patch",
    )
    (
        sum_qkv,
        sum_attn_out,
        sum_mlp_in,
        sum_mlp_out,
        sum_lead,
        sum_agg_out,
        sum_value,
        sum_query_keys,
        sum_table,
        sum_patch,
        sum_gain_one,
        sum_gain_two,
        sum_query,
        sum_bias,
    ) = totals
    sum_key = (sum_query_keys[:, :, None] * query_heads.astype(jnp.float32)[None] * 0.125).reshape(
        width_part, width
    )
    return (
        output,
        field_grad,
        sum_patch,
        sum_table,
        sum_query,
        sum_key,
        sum_value,
        sum_agg_out,
        sum_lead,
        sum_gain_one,
        sum_qkv,
        sum_attn_out,
        sum_gain_two,
        sum_mlp_in,
        sum_bias,
        sum_mlp_out,
    )


def solution(mesh):
    placed = (
        P("var", None, "patch", None),
        P(),
        P("patch"),
        P("var", None, None),
        P(),
        P(),
        P(),
        P(),
        P(),
        P(),
        P(),
        P(),
        P(),
        P(),
        P(),
        P(),
        P(),
        P("patch", "var", None),
    )
    return jax.shard_map(
        body,
        mesh=mesh,
        in_specs=placed,
        out_specs=(
            P("patch", "var", None),
            P("var", None, "patch", None),
            P("var", None, None),
            P("var", None),
            P("var"),
            P("var", None),
            P("var", None),
            P("var", None),
            P("var", None),
            P("var"),
            P("var", None),
            P("var", None),
            P("var"),
            P("var", None),
            P("var"),
            P("var", None),
        ),
        check_vma=False,
    )
```

profile of v0, /device:TPU:0, one launch (start us, length us, event | category | flops | bytes accessed | tf_op | source)
XLA Modules:
  0.0 1969.9 jit_solution(5483503065119961382)
XLA Ops:
  20.4 10.3 reduce.9
  47.7 11.3 reduce.11
  65.5 11.4 fusion.58
  76.9 20.7 %copy.155 = f32[1,1024,1,2048]{1,2,0,3:T(1,128)} copy(f32[1,1024,1,2048]{3,1,2,0:T(8,128)} %bitcast.298) | data formatting | bytes 16777216 | tf_op jit(solution)/shard_map/reshape;reshape | solution.py:258
  125.4 70.6 %all-to-all-done = f32[1,1024,1,2048]{1,2,0,3:T(1,128)} async-done(((f32[1,1024,1,2048]{1,2,0,3:T(1,128)}), f32[1,1024,1,2048]{1,2,0,3:T(1,128)}, u32[]{:S(2)}, u32[]{:S(2)}) %all-to-all-start) | async-done | bytes 8388640 | tf_op jit(solution)/shard_map/all_to_all | solution.py:257
  196.0 20.8 %copy.156 = f32[1,1024,1,4,512]{4,3,1,2,0:T(4,128)} copy(f32[1,1024,1,4,512]{1,2,4,3,0:T(1,128)} %bitcast.23) | data formatting | bytes 16777216 | tf_op jit(solution)/shard_map/all_to_all | solution.py:257
  220.2 7.6 fusion.61
  245.2 49.8 %all-gather.9.cloned.1.call-done = bf16[2048,1024]{1,0:T(8,128)(2,1)} async-done(((bf16[512,1024]{1,0:T(8,128)(2,1)}), bf16[2048,1024]{1,0:T(8,128)(2,1)}) %all-gather.9.cloned.1.call-update) | async-done | bytes 4194320 | tf_op jit(solution)/shard_map/all_gather | solution.py:307
  301.4 48.7 %all-gather.11.cloned.1.call-done = bf16[2048,1024]{1,0:T(8,128)(2,1)} async-done(((bf16[512,1024]{1,0:T(8,128)(2,1)}), bf16[2048,1024]{1,0:T(8,128)(2,1)}) %all-gather.11.cloned.1.call-update) | async-done | bytes 4194320 | tf_op jit(solution)/shard_map/all_gather | solution.py:308
  356.7 47.8 %while.10 = (s32[]{:T(128)}, bf16[4,4,512,64]{2,3,1,0:T(8,128)(2,1)S(1)}, f32[4,4,512]{2,1,0:T(4,128)S(1)}, bf16[4,4,512,64]{2,3,1,0:T(8,128)(2,1)}, bf16[4,4,20...) while((s32[]{:T(128)}, bf16[4,4,512,64]{2,3,1,0:T(8,128)(2,1)S(1)}, ...), condition=%wide.region_10.11_spmd, body=%wide.region_7.10_spmd.sunk | while | flops 1111619584 | bytes 53020752 | solution.py:313
  409.7 25.8 %multiply_convert_fusion.1 = (bf16[512,4096]{1,0:T(8,128)(2,1)}, f32[512,4096]{1,0:T(8,128)}, f32[512,4096]{1,0:T(8,128)}) fusion(f32[4096]{0:T(1024)S(1)} %copy-done.66, bf16[1024,4096]{1,0:T(8,128)(2,1)S(1)} %copy-done.88, f32[512,1024]{1,0:T(8,128)S(1)} %get-tuple-element.307, f32[1024]{0:T(1024)S(1)} %copy-done.64, f32[512]{0:T(512)S(1)} %add_rsqrt_fusion, ...), kind=kOutput, calls=%fused_computation.72 | convolution fusion | flops 4435476480 | bytes 31481856 | tf_op jit(solution)/shard_map/dot_general | solution.py:320
  435.5 14.0 convert_reduce_fusion
  449.6 9.8 multiply_reduce_fusion.2
  465.3 150.1 %while.27 = (s32[]{:T(128)}, bf16[4,4,512,64]{2,3,1,0:T(8,128)(2,1)}, f32[4,4,2048,64]{2,3,1,0:T(8,128)}, f32[4,4,2048,64]{2,3,1,0:T(8,128)}, bf16[4,4,512,64]{2...) while((s32[]{:T(128)}, ...), condition=%wide.region_17.18_spmd, body=%wide.region_15.17_spmd.sunk | while | flops 2735470592 | bytes 168096896 | solution.py:345
  469.0 9.5 multiply_reduce_fusion.14
  478.4 7.9 multiply_convert_fusion.9
  490.5 7.0 fusion.211
  506.5 9.5 multiply_reduce_fusion.14
  515.9 7.9 multiply_convert_fusion.9
  528.0 7.0 fusion.211
  544.0 9.5 multiply_reduce_fusion.14
  553.5 7.9 multiply_convert_fusion.9
  565.6 7.0 fusion.211
  581.5 9.5 multiply_reduce_fusion.14
  591.0 7.9 multiply_convert_fusion.9
  603.1 7.0 fusion.211
  616.3 85.6 %reduce-scatter.14.cloned.1.call-done = f32[1,512,1024]{1,2,0:T(8,128)} async-done(((f32[1,2048,1024]{1,2,0:T(8,128)}), f32[1,512,1024]{1,2,0:T(8,128)}) %reduce-scatter.14.cloned.1.call-update) | async-done | bytes 2097168 | tf_op jit(solution)/shard_map/reduce_scatter | solution.py:360
  703.7 87.9 %reduce-scatter.12.cloned.1.call-done = f32[1,512,1024]{1,2,0:T(8,128)} async-done(((f32[1,2048,1024]{1,2,0:T(8,128)}), f32[1,512,1024]{1,2,0:T(8,128)}) %reduce-scatter.12.cloned.1.call-update) | async-done | bytes 2097168 | tf_op jit(solution)/shard_map/reduce_scatter | solution.py:359
  793.4 8.9 multiply_reduce_fusion.3
  807.9 19.6 all-gather.2
  837.7 10.5 all-gather.4
  848.2 16.4 all-gather.13.cloned.1.call-done
  864.6 6.8 copy.169
  871.4 10.4 fusion.54
  919.1 13.3 fusion.132
  933.7 10.5 fusion.85
  945.4 10.4 fusion.79
  965.2 25.0 %fusion = f32[16,1024]{1,0:T(8,128)S(1)} fusion(f32[48,1024]{1,0:T(8,128)S(1)} %fusion.114), kind=kCustom, calls=%all-reduce-scatter | all-reduce-scatter fusion | flops 65537 | bytes 262656
  992.9 17.9 all-reduce.11
  1016.5 14.2 reduce-scatter.24.cloned.1.call-done
  1030.6 56.6 %reduce-scatter.20.cloned.1.call-done = f32[256,1024]{1,0:T(8,128)} async-done(((f32[1024,1024]{1,0:T(8,128)}), f32[256,1024]{1,0:T(8,128)}) %reduce-scatter.20.cloned.1.call-update) | async-done | bytes 1048592 | tf_op jit(solution)/shard_map/reduce_scatter | solution.py:423
  1087.2 56.1 %reduce-scatter.18.cloned.1.call-done = f32[256,1024]{1,0:T(8,128)} async-done(((f32[1024,1024]{1,0:T(8,128)}), f32[256,1024]{1,0:T(8,128)}) %reduce-scatter.18.cloned.1.call-update) | async-done | bytes 1048592 | tf_op jit(solution)/shard_map/reduce_scatter | solution.py:424
  1143.3 157.2 %reduce-scatter.26.cloned.1.call-done = f32[256,4096]{1,0:T(8,128)} async-done(((f32[1024,4096]{1,0:T(8,128)}), f32[256,4096]{1,0:T(8,128)}) %reduce-scatter.26.cloned.1.call-update) | async-done | bytes 4194320 | tf_op jit(solution)/shard_map/reduce_scatter | solution.py:420
  1300.5 157.1 %reduce-scatter.28.cloned.1.call-done = f32[1024,1024]{1,0:T(8,128)} async-done(((f32[4096,1024]{1,0:T(8,128)}), f32[1024,1024]{1,0:T(8,128)}) %reduce-scatter.28.cloned.1.call-update) | async-done | bytes 4194320 | tf_op jit(solution)/shard_map/reduce_scatter | solution.py:421
  1457.5 124.1 %reduce-scatter.22.cloned.1.call-done = f32[256,3072]{1,0:T(8,128)} async-done(((f32[1024,3072]{1,0:T(8,128)}), f32[256,3072]{1,0:T(8,128)}) %reduce-scatter.22.cloned.1.call-update) | async-done | bytes 3145744 | tf_op jit(solution)/shard_map/reduce_scatter | solution.py:418
  1582.4 10.8 fusion.78
  1595.4 43.0 %all-reduce.18.cloned.1.call-done = (f32[12,1024]{1,0:T(8,128)}, f32[256]{0:T(256)}, f32[256,16]{0,1:T(8,128)}, f32[2,1024]{1,0:T(2,128)}, f32[256]{0:T(256)}, /*index=5*/f32[256]{0:T(256)}, f32[1024]{0:T(1024)}) async-done(((f32[12,1024]{1,0:T(8,128)}, f32[256]{0:T(256)}, f32[256,16]{0,1:T(8,128)}, f32[2,1024]{1,0:T(2,128)}, f32[256]{0:T(256)}, /*index=5*/f32[256]{0:T(256)}, f32[1024]{0:T(1024)}), ...) | async-done | bytes 80912 | tf_op jit(solution)/shard_map/psum | solution.py:433
  1640.6 302.7 %all-reduce.20.cloned.1.call-done = (f32[12,4,1024]{2,1,0:T(4,128)}, f32[256,1024]{1,0:T(8,128)}, f32[256,1024]{1,0:T(8,128)}, f32[256,3072]{1,0:T(8,128)}, f32[...) async-done(((f32[12,4,1024]{2,1,0:T(4,128)}, f32[256,1024]{1,0:T(8,128)}, f32[256,1024]{1,0:T(8,128)}, f32[256,3072]{1,0:T(8,128)}, ...) | async-done | bytes 14876688 | tf_op jit(solution)/shard_map/psum | solution.py:433
  (390 shorter events, 307.1 us)
Async XLA Ops:
  7.2 226.2 %copy-start = (bf16[1024,1024]{1,0:T(8,128)(2,1)S(1)}, bf16[1024,1024]{1,0:T(8,128)(2,1)}, u32[]{:S(2)}) copy-start(bf16[1024,1024]{1,0:T(8,128)(2,1)} %param.30) | copy-start | bytes 6291460
  11.7 29.5 %copy-start.38 = (bf16[12,1024]{1,0:T(8,128)(2,1)}, bf16[12,1024]{1,0:T(8,128)(2,1)S(1)}, u32[]{:S(2)}) copy-start(bf16[12,1024]{1,0:T(8,128)(2,1)S(1)} %convolution_convert_fusion.3) | copy-start | bytes 73732
  15.1 27.2 %copy-start.23 = (bf16[12,4,1,2048]{3,0,1,2:T(8,128)(2,1)}, bf16[12,4,1,2048]{3,0,1,2:T(8,128)(2,1)S(1)}, u32[]{:S(2)}) copy-start(bf16[12,4,1,2048]{3,0,1,2:T(8,128)(2,1)S(1)} %copy.224) | copy-start | bytes 589828
  33.0 28.3 %all-to-all-start.1 = ((f32[4,1,8192]{2,1,0:T(1,128)}), f32[4,1,8192]{2,1,0:T(1,128)}, u32[]{:S(2)}, u32[]{:S(2)}) async-start(f32[4,1,8192]{2,1,0:T(1,128)} %reshape.382), calls=%async_computation.1 | async-start | bytes 262144 | tf_op jit(solution)/shard_map/all_to_all | solution.py:243
  42.4 23.1 %copy-start.15 = (f32[12,5,2048]{2,0,1:T(8,128)}, f32[12,5,2048]{2,0,1:T(8,128)S(1)}, u32[]{:S(2)}) copy-start(f32[12,5,2048]{2,0,1:T(8,128)S(1)} %pad_convert_fusion) | copy-start | bytes 1474564
  45.8 31.1 %copy-start.17 = (f32[12,5,16,64]{3,2,0,1:T(8,128)}, f32[12,5,16,64]{3,2,0,1:T(8,128)S(1)}, u32[]{:S(2)}) copy-start(f32[12,5,16,64]{3,2,0,1:T(8,128)S(1)} %reshape.323) | copy-start | bytes 737284
  61.3 36.3 %all-to-all-start.2 = ((f32[4,1,8192]{2,1,0:T(1,128)}), f32[4,1,8192]{2,1,0:T(1,128)S(1)}, u32[]{:S(2)}, u32[]{:S(2)}) async-start(f32[4,1,8192]{2,1,0:T(1,128)} %reshape.384), calls=%async_computation.2 | async-start | bytes 262144 | tf_op jit(solution)/shard_map/all_to_all | solution.py:250
  98.3 97.7 %all-to-all-start = ((f32[1,1024,1,2048]{1,2,0,3:T(1,128)}), f32[1,1024,1,2048]{1,2,0,3:T(1,128)}, u32[]{:S(2)}, u32[]{:S(2)}) async-start(f32[1,1024,1,2048]{1,2,0,3:T(1,128)} %copy.155), calls=%async_computation | async-start | bytes 16777216 | tf_op jit(solution)/shard_map/all_to_all | solution.py:257
  103.9 191.1 %all-gather.9.cloned.1.call-start = ((), (), s32[]{:S(2)}) async-start(), calls=%async_computation.21 | async-start | bytes 5242880 | tf_op jit(solution)/shard_map/all_gather | solution.py:307
  104.8 130.4 %copy-start.61 = (f32[1024]{0:T(1024)}, f32[1024]{0:T(1024)S(1)}, u32[]{:S(2)}) copy-start(f32[1024]{0:T(1024)S(1)} %convert_element_type.111) | copy-start | bytes 12292
  105.0 130.3 %copy-start.53 = (f32[1,1024]{1,0:T(1,128)}, f32[1,1024]{1,0:T(1,128)S(1)}, u32[]{:S(2)}) copy-start(f32[1,1024]{1,0:T(1,128)S(1)} %fusion.117) | copy-start | bytes 12292
  108.8 13.7 copy-start.18
  241.6 108.5 %all-gather.11.cloned.1.call-start = ((), (), s32[]{:S(2)}) async-start(), calls=%async_computation.22 | async-start | bytes 5242880 | tf_op jit(solution)/shard_map/all_gather | solution.py:308
  242.4 459.5 %reduce-scatter.14.cloned.1.call-start = ((), (), s32[]{:S(2)}) async-start(), calls=%async_computation.13 | async-start | bytes 10485760 | tf_op jit(solution)/shard_map/reduce_scatter | solution.py:360
  356.7 47.9 %copy-start.54 = (f32[1,1024]{1,0:T(1,128)S(1)}, f32[1,1024]{1,0:T(1,128)}, u32[]{:S(2)}) copy-start(f32[1,1024]{1,0:T(1,128)} %copy-done.53) | copy-start | bytes 12292
  408.6 50.8 %copy-start.13 = (f32[512,1024]{1,0:T(8,128)}, f32[512,1024]{1,0:T(8,128)S(1)}, u32[]{:S(2)}) copy-start(f32[512,1024]{1,0:T(8,128)S(1)} %get-tuple-element.307) | copy-start | bytes 6291460
  408.6 50.8 %copy-start.58 = (f32[512]{0:T(512)}, f32[512]{0:T(512)S(1)}, u32[]{:S(2)}) copy-start(f32[512]{0:T(512)S(1)} %broadcast_multiply_fusion.6) | copy-start | bytes 6148
  409.7 49.7 %copy-start.76 = (f32[512]{0:T(512)}, f32[512]{0:T(512)S(1)}, u32[]{:S(2)}) copy-start(f32[512]{0:T(512)S(1)} %add_rsqrt_fusion) | copy-start | bytes 6148
  409.7 25.8 %copy-start.36 = (bf16[1,512,1024]{2,1,0:T(8,128)(2,1)S(1)}, bf16[1,512,1024]{2,1,0:T(8,128)(2,1)}, u32[]{:S(2)}) copy-start(bf16[1,512,1024]{2,1,0:T(8,128)(2,1)} %param.39) | copy-start | bytes 3145732
  615.4 176.2 %reduce-scatter.12.cloned.1.call-start = ((), (), s32[]{:S(2)}) async-start(), calls=%async_computation.12 | async-start | bytes 10485760 | tf_op jit(solution)/shard_map/reduce_scatter | solution.py:359
  616.0 177.3 %copy-start.55 = (f32[1,1024]{1,0:T(1,128)S(1)}, f32[1,1024]{1,0:T(1,128)}, u32[]{:S(2)}) copy-start(f32[1,1024]{1,0:T(1,128)} %copy-done.53) | copy-start | bytes 12292
  616.0 177.3 %copy-start.57 = (f32[512]{0:T(512)S(1)}, f32[512]{0:T(512)}, u32[]{:S(2)}) copy-start(f32[512]{0:T(512)} %copy-done.56) | copy-start | bytes 6148
  616.0 177.3 %copy-start.62 = (f32[1024]{0:T(1024)S(1)}, f32[1024]{0:T(1024)}, u32[]{:S(2)}) copy-start(f32[1024]{0:T(1024)} %copy-done.61) | copy-start | bytes 12292
  616.0 177.3 %copy-start.70 = (f32[512]{0:T(512)S(1)}, f32[512]{0:T(512)}, u32[]{:S(2)}) copy-start(f32[512]{0:T(512)} %copy-done.69) | copy-start | bytes 6148
  616.0 248.5 %all-gather.13.cloned.1.call-start = ((), (), s32[]{:S(2)}) async-start(), calls=%async_computation.23 | async-start | bytes 5242880 | tf_op jit(solution)/shard_map/all_gather | solution.py:381
  703.7 98.6 %copy-start.32 = (bf16[512,1024]{0,1:T(8,128)(2,1)}, bf16[512,1024]{0,1:T(8,128)(2,1)S(1)}, u32[]{:S(2)}) copy-start(bf16[512,1024]{0,1:T(8,128)(2,1)S(1)} %convert_bitcast_fusion) | copy-start | bytes 3145732
  806.9 207.8 %reduce-scatter.16.cloned.1.call-start = ((), (), s32[]{:S(2)}) async-start(), calls=%async_computation.14 | async-start | bytes 81920 | tf_op jit(solution)/shard_map/reduce_scatter | solution.py:425
  871.4 10.4 copy-start.16
  871.4 10.4 copy-start.22
  889.5 11.2 copy-start.28
  893.1 121.7 %all-reduce.16.cloned.1.call-start = ((), (), s32[]{:S(2)}) async-start(), calls=%async_computation.24 | async-start | bytes 1572864
  903.8 126.8 %reduce-scatter.24.cloned.1.call-start = ((), (), s32[]{:S(2)}) async-start(), calls=%async_computation.18 | async-start | bytes 5242880 | tf_op jit(solution)/shard_map/reduce_scatter | solution.py:419
  909.1 178.1 %reduce-scatter.20.cloned.1.call-start = ((), (), s32[]{:S(2)}) async-start(), calls=%async_computation.16 | async-start | bytes 5242880 | tf_op jit(solution)/shard_map/reduce_scatter | solution.py:423
  914.1 229.2 %reduce-scatter.18.cloned.1.call-start = ((), (), s32[]{:S(2)}) async-start(), calls=%async_computation.15 | async-start | bytes 5242880 | tf_op jit(solution)/shard_map/reduce_scatter | solution.py:424
  918.8 381.6 %reduce-scatter.26.cloned.1.call-start = ((), (), s32[]{:S(2)}) async-start(), calls=%async_computation.19 | async-start | bytes 20971520 | tf_op jit(solution)/shard_map/reduce_scatter | solution.py:420
  932.5 525.1 %reduce-scatter.28.cloned.1.call-start = ((), (), s32[]{:S(2)}) async-start(), calls=%async_computation.20 | async-start | bytes 20971520 | tf_op jit(solution)/shard_map/reduce_scatter | solution.py:421
  944.2 637.5 %reduce-scatter.22.cloned.1.call-start = ((), (), s32[]{:S(2)}) async-start(), calls=%async_computation.17 | async-start | bytes 15728640 | tf_op jit(solution)/shard_map/reduce_scatter | solution.py:418
  955.8 37.0 %copy-start.68 = (f32[4096]{0:T(1024)S(1)}, f32[4096]{0:T(1024)}, u32[]{:S(2)}) copy-start(f32[4096]{0:T(1024)} %get-tuple-element.313) | copy-start | bytes 49156
  955.8 37.0 %copy-start.79 = (f32[1024]{0:T(1024)S(1)}, f32[1024]{0:T(1024)}, u32[]{:S(2)}) copy-start(f32[1024]{0:T(1024)} %get-tuple-element.232) | copy-start | bytes 12292
  955.8 37.0 %copy-start.80 = (f32[1024]{0:T(1024)S(1)}, f32[1024]{0:T(1024)}, u32[]{:S(2)}) copy-start(f32[1024]{0:T(1024)} %get-tuple-element.230) | copy-start | bytes 12292
  955.9 682.5 %all-reduce.18.cloned.1.call-start = ((), (), s32[]{:S(2)}) async-start(), calls=%async_computation.25 | async-start | bytes 194560 | tf_op jit(solution)/shard_map/psum | solution.py:433
  990.3 23.6 %collective-permute-start = (f32[12,1024]{1,0:T(8,128)S(1)}, f32[12,1024]{1,0:T(8,128)S(1)}, u32[]{:S(2)}, u32[]{:S(2)}) collective-permute-start(f32[12,1024]{1,0:T(8,128)S(1)} %slice.35), channel_id=1, source_target_pairs={{0,8},{8,16},{16,24},{1,9},{9,17},{17,25},{2,10},{10,18},{18,26},{... | collective-permute-start | bytes 147464
  1014.7 928.6 %all-reduce.20.cloned.1.call-start = ((), (), s32[]{:S(2)}) async-start(), calls=%async_computation.26 | async-start | bytes 29753344 | tf_op jit(solution)/shard_map/psum | solution.py:433
  1582.4 10.8 copy-start.46
  1582.4 10.8 copy-start.9
  1582.4 10.8 copy-start.50
  1638.4 314.1 %copy-start.75 = (f32[2,1024]{1,0:T(2,128)S(1)}, f32[2,1024]{1,0:T(2,128)}, u32[]{:S(2)}) copy-start(f32[2,1024]{1,0:T(2,128)} %get-tuple-element.478) | copy-start | bytes 24580
  1638.4 314.7 %copy-start.87 = (f32[256]{0:T(256)S(1)}, f32[256]{0:T(256)}, u32[]{:S(2)}) copy-start(f32[256]{0:T(256)} %get-tuple-element.479) | copy-start | bytes 3076
  (68 other events, 275.8 us)
Sparse Core Ops, SparseCore 0:
  241.8 53.2 all-gather.8
  297.4 52.6 all-gather.10
  615.5 86.3 reduce-scatter.13
  705.1 86.3 reduce-scatter.11
  807.0 57.5 all-gather.12
  893.3 23.5 reduce-scatter.15
  920.7 48.7 all-reduce.15
  972.5 58.0 reduce-scatter.23
  1034.4 52.6 reduce-scatter.19
  1090.6 52.6 reduce-scatter.17
  1146.6 153.7 reduce-scatter.25
  1303.7 153.7 reduce-scatter.27
  1461.0 120.6 reduce-scatter.21
  1585.8 52.5 all-reduce.17
  1641.7 301.5 all-reduce.19
where the time goes:
time: 1980 us; the launch traced here: 1970 us
  waiting for transfers between devices  1270 us (64%)
  matrix products  332 us (17%)
  local copies, waits for them, and re-layouts  153 us (8%)
  other arithmetic  102 us (5%)
  blocking collectives  73 us (4%)
    psum x2, waiting for transfers between devices, body(): lax.psum((parts_in[0], parts_in[1], parts_in[2], parts_in[3], parts_in[4]...  346 us
    reduce_scatter x1, waiting for transfers between devices, body(): lax.psum_scatter(grad_mlp_in, 'var', scatter_dimension=0, tiled=True)  157 us
    reduce_scatter x1, waiting for transfers between devices, body(): lax.psum_scatter(grad_mlp_out, 'var', scatter_dimension=0, tiled=True)  157 us
    reduce_scatter x1, waiting for transfers between devices, body(): lax.psum_scatter(grad_qkv, 'var', scatter_dimension=0, tiled=True)  124 us
    reduce_scatter x1, waiting for transfers between devices, body(): lax.psum_scatter(grad_keys_full, 'var', scatter_dimension=1, tiled=True)  87.9 us
    reduce_scatter x1, waiting for transfers between devices, body(): lax.psum_scatter(grad_values_full, 'var', scatter_dimension=1, tiled=True)  85.6 us
    all_to_all x1, waiting for transfers between devices, body(): lax.all_to_all(sums.reshape(1, width, samples_here, seq_len), 'var', spli...  70.6 us
    reduce_scatter x1, waiting for transfers between devices, body(): lax.psum_scatter(grad_agg_out, 'var', scatter_dimension=0, tiled=True)  56.6 us
  transfers between devices with their start and end apart: 19, of which 14 were waited for; matrix products, arithmetic and copies ran while one was open for 10% of the time, Pallas kernels for 0%

commit v1 on v0

v1 whole, which is shorter than its diff:
```python
from functools import partial

import jax
import jax.numpy as jnp
from jax import lax
from jax.experimental import pallas as pl
from jax.experimental.pallas import tpu as pltpu
from jax.sharding import PartitionSpec as P

HEADS = 16
PIX = 4
HEAD_DIM = 64

f32, bf16 = jnp.float32, jnp.bfloat16
highest = lax.Precision.HIGHEST
epsilon = 1e-05
NT = (((1,), (1,)), ((), ()))
TN = (((0,), (0,)), ((), ()))


def head_weights(pixels, key_ref, head):
    scores = key_ref[PIX, :, head : head + 1]
    for c in range(PIX):
        scores = scores + pixels[c] * key_ref[c, :, head : head + 1]
    soft = jnp.exp(scores - jnp.max(scores, axis=0, keepdims=True))
    return soft * (1.0 / jnp.sum(soft, axis=0, keepdims=True))


def weighted_pixels(soft, pixels):
    return jnp.concatenate(
        [(soft * pixels[c]).astype(bf16) for c in range(PIX)] + [soft.astype(bf16)], axis=0
    )


def front_kernel(
    member,
    pixel_ref,
    key_ref,
    value_ref,
    out_ref,
    lead_ref,
    gain_ref,
    wq_ref,
    wk_ref,
    wv_ref,
    hidden_ref,
    qkv_ref,
    resid_ref,
    att_ref,
    att_scratch,
):
    pixels = [pixel_ref[c].astype(f32) for c in range(PIX)]
    for head in range(HEADS):
        soft = head_weights(pixels, key_ref, head)
        span = slice(head * HEAD_DIM, (head + 1) * HEAD_DIM)
        att_scratch[span, :] = jnp.dot(
            value_ref[span, :], weighted_pixels(soft, pixels), preferred_element_type=f32
        ).astype(bf16)
    att = att_scratch[...]
    resid = lax.dot_general(att, out_ref[...], TN, preferred_element_type=f32) + lead_ref[...]
    centered = resid - jnp.mean(resid, axis=1, keepdims=True)
    inverse = lax.rsqrt(jnp.mean(centered * centered, axis=1, keepdims=True) + epsilon)
    hidden = (centered * inverse * gain_ref[...]).astype(bf16)
    hidden_ref[...] = hidden
    own = wq_ref.shape[1]
    for t, weight in enumerate((wq_ref, wk_ref, wv_ref)):
        qkv_ref[:, t * own : (t + 1) * own] = jnp.dot(
            hidden, weight[...], preferred_element_type=f32
        ).astype(bf16)

    @pl.when(pl.program_id(0) == 0)
    def _():
        resid_ref[...] = resid
        att_ref[...] = att


def front(member, pixels, key_rows, values_t, agg_out, lead_row, gain, attn_qkv, groups):
    width = agg_out.shape[0]
    own = width // groups
    channels, seq = pixels.shape[1:]
    rows = seq // groups
    spec = pltpu.PrefetchScalarGridSpec(
        num_scalar_prefetch=1,
        grid=(groups,),
        in_specs=[
            pl.BlockSpec((PIX, channels, rows), lambda i, m: (0, 0, m[0] ^ i)),
            pl.BlockSpec(key_rows.shape, lambda i, m: (0, 0, 0)),
            pl.BlockSpec(values_t.shape, lambda i, m: (0, 0)),
            pl.BlockSpec(agg_out.shape, lambda i, m: (0, 0)),
            pl.BlockSpec((1, width), lambda i, m: (0, 0)),
            pl.BlockSpec((1, width), lambda i, m: (0, 0)),
            pl.BlockSpec((width, own), lambda i, m: (0, m[0])),
            pl.BlockSpec((width, own), lambda i, m: (0, groups + m[0])),
            pl.BlockSpec((width, own), lambda i, m: (0, 2 * groups + m[0])),
        ],
        out_specs=[
            pl.BlockSpec((rows, width), lambda i, m: (i, 0)),
            pl.BlockSpec((rows, 3 * own), lambda i, m: (i, 0)),
            pl.BlockSpec((rows, width), lambda i, m: (0, 0)),
            pl.BlockSpec((width, rows), lambda i, m: (0, 0)),
        ],
        scratch_shapes=[pltpu.VMEM((width, rows), bf16)],
    )
    return pl.pallas_call(
        front_kernel,
        grid_spec=spec,
        out_shape=[
            jax.ShapeDtypeStruct((seq, width), bf16),
            jax.ShapeDtypeStruct((seq, 3 * own), bf16),
            jax.ShapeDtypeStruct((rows, width), f32),
            jax.ShapeDtypeStruct((width, rows), bf16),
        ],
        cost_estimate=pl.CostEstimate(
            flops=2 * seq * width * (width + 3 * own), bytes_accessed=16 << 20, transcendentals=seq * channels * HEADS
        ),
        name="front",
    )(member, pixels, key_rows, values_t, agg_out, lead_row, gain, attn_qkv, attn_qkv, attn_qkv)


def attend_kernel(q_ref, k_ref, v_ref, mixed_ref, lse_ref):
    rows = q_ref.shape[0]
    lane = lax.broadcasted_iota(jnp.int32, (1, 2 * HEAD_DIM), 1)
    queries = q_ref[...] * jnp.asarray(0.125, bf16)
    mixed = jnp.zeros((rows, 2 * HEAD_DIM), f32)
    for part in range(2):
        keep = (lane // HEAD_DIM) == part
        query = jnp.where(keep, queries, jnp.zeros_like(queries))
        scores = lax.dot_general(query, k_ref[...], NT, preferred_element_type=f32)
        top = jnp.max(scores, axis=1, keepdims=True)
        soft = jnp.exp(scores - top)
        total = jnp.sum(soft, axis=1, keepdims=True)
        out = jnp.dot(soft.astype(bf16), v_ref[...], preferred_element_type=f32)
        mixed = jnp.where(keep, out * (1.0 / total), mixed)
        lse = jnp.broadcast_to(top + jnp.log(total), (rows, 2 * HEAD_DIM))
        lse_ref[0, part : part + 1, :] = lse.T[0:1, :]
    mixed_ref[...] = mixed.astype(bf16)


def attend(qkv, slot, rows, block):
    seq = qkv.shape[0]
    pair = 2 * HEAD_DIM
    pairs = qkv.shape[1] // (3 * pair)
    steps = rows // block
    return pl.pallas_call(
        attend_kernel,
        grid=(pairs, steps),
        in_specs=[
            pl.BlockSpec((block, pair), lambda p, i: (slot * steps + i, p)),
            pl.BlockSpec((seq, pair), lambda p, i: (0, pairs + p)),
            pl.BlockSpec((seq, pair), lambda p, i: (0, 2 * pairs + p)),
        ],
        out_specs=[
            pl.BlockSpec((block, pair), lambda p, i: (i, p)),
            pl.BlockSpec((1, 2, block), lambda p, i: (p, 0, i)),
        ],
        out_shape=[
            jax.ShapeDtypeStruct((rows, pairs * pair), bf16),
            jax.ShapeDtypeStruct((pairs, 2, rows), f32),
        ],
        cost_estimate=pl.CostEstimate(
            flops=16 * rows * seq * pair * pairs, bytes_accessed=3 << 20, transcendentals=2 * rows * seq * pairs
        ),
        name="attend",
    )(qkv, qkv, qkv)


def attend_back_kernel(q_ref, k_ref, v_ref, g_ref, o_ref, lse_ref, out_ref, dk_acc, dv_acc, kt, *, chunk):
    i = pl.program_id(0)
    block = q_ref.shape[0]
    seq = k_ref.shape[0]
    pair = 2 * HEAD_DIM
    lane = lax.broadcasted_iota(jnp.int32, (1, pair), 1)
    side = lax.broadcasted_iota(jnp.int32, (pair, 1), 0)

    @pl.when(i == 0)
    def _():
        dk_acc[...] = jnp.zeros_like(dk_acc)
        dv_acc[...] = jnp.zeros_like(dv_acc)
        kt[...] = k_ref[...].T

    queries = q_ref[...] * jnp.asarray(0.125, bf16)
    grads = g_ref[...]
    product = (grads.astype(f32) * o_ref[...].astype(f32)).T
    grad_query = jnp.zeros((pair, block), f32)
    for part in range(2):
        keep = (lane // HEAD_DIM) == part
        query = jnp.where(keep, queries, jnp.zeros_like(queries))
        grad = jnp.where(keep, grads, jnp.zeros_like(grads))
        delta = jnp.sum(product[part * HEAD_DIM : (part + 1) * HEAD_DIM], axis=0, keepdims=True)
        lse = lse_ref[0, part : part + 1, :]
        total = jnp.zeros((pair, block), f32)
        for at in range(0, seq, chunk):
            span = pl.ds(at, chunk)
            scores = lax.dot_general(k_ref[span, :], query, NT, preferred_element_type=f32)
            soft = jnp.exp(scores - lse)
            through = lax.dot_general(v_ref[span, :], grad, NT, preferred_element_type=f32)
            grad_scores = (soft * (through - delta)).astype(bf16)
            dv_acc[span, :] += jnp.dot(soft.astype(bf16), grad, preferred_element_type=f32)
            dk_acc[span, :] += jnp.dot(grad_scores, query, preferred_element_type=f32)
            total += jnp.dot(kt[:, span], grad_scores, preferred_element_type=f32)
        grad_query = jnp.where((side // HEAD_DIM) == part, total, grad_query)
    out_ref[pl.ds(pl.multiple_of(i * block, block), block), 0:pair] = (grad_query.T * 0.125).astype(bf16)

    @pl.when(i == pl.num_programs(0) - 1)
    def _():
        out_ref[:, pair : 2 * pair] = dk_acc[...].astype(bf16)
        out_ref[:, 2 * pair : 3 * pair] = dv_acc[...].astype(bf16)


def attend_back(qkv, grads, mixed, lse, which, block, chunk):
    seq = qkv.shape[0]
    pair = 2 * HEAD_DIM
    pairs = qkv.shape[1] // (3 * pair)
    return pl.pallas_call(
        partial(attend_back_kernel, chunk=chunk),
        grid=(seq // block,),
        in_specs=[
            pl.BlockSpec((block, pair), lambda i: (i, which)),
            pl.BlockSpec((seq, pair), lambda i: (0, pairs + which)),
            pl.BlockSpec((seq, pair), lambda i: (0, 2 * pairs + which)),
            pl.BlockSpec((block, pair), lambda i: (i, which)),
            pl.BlockSpec((block, pair), lambda i: (i, which)),
            pl.BlockSpec((1, 2, block), lambda i: (which, 0, i)),
        ],
        out_specs=pl.BlockSpec((seq, 3 * pair), lambda i: (0, 0)),
        out_shape=jax.ShapeDtypeStruct((seq, 3 * pair), bf16),
        scratch_shapes=[pltpu.VMEM((seq, pair), f32), pltpu.VMEM((seq, pair), f32), pltpu.VMEM((pair, seq), bf16)],
        cost_estimate=pl.CostEstimate(
            flops=40 * seq * seq * pair, bytes_accessed=5 << 20, transcendentals=2 * seq * seq
        ),
        name="attend_back",
    )(qkv, qkv, qkv, grads, mixed, lse)


def aggregate_back_kernel(member, pixel_ref, key_ref, value_ref, grad_ref, field_ref, proj_ref, keys_ref):
    count, rows = pixel_ref.shape[1:]
    pair = 2 * HEAD_DIM
    pixels = [pixel_ref[c].astype(f32) for c in range(PIX)]
    lane = lax.broadcasted_iota(jnp.int32, (1, pair), 1)
    side = lax.broadcasted_iota(jnp.int32, (pair, 1), 0)
    field = [jnp.zeros((count, rows), f32) for _ in range(PIX)]
    keys = [jnp.zeros((count, pair), f32) for _ in range(PIX + 1)]
    for which in range(HEADS // 2):
        span = slice(which * pair, (which + 1) * pair)
        values, grads = value_ref[:, span], grad_ref[span, :]
        total = jnp.zeros(((PIX + 1) * count, pair), f32)
        for part in range(2):
            head = which * 2 + part
            grad = jnp.where((side // HEAD_DIM) == part, grads, jnp.zeros_like(grads))
            through = jnp.dot(values, grad, preferred_element_type=f32)
            kinds = [through[c * count : (c + 1) * count] for c in range(PIX + 1)]
            soft = head_weights(pixels, key_ref, head)
            grad_soft = kinds[PIX]
            for c in range(PIX):
                grad_soft = grad_soft + pixels[c] * kinds[c]
            weighed = soft * grad_soft
            grad_scores = weighed - soft * jnp.sum(weighed, axis=0, keepdims=True)
            for c in range(PIX):
                field[c] = field[c] + soft * kinds[c] + grad_scores * key_ref[c, :, head : head + 1]
                keys[c] = jnp.where(lane == head, jnp.sum(grad_scores * pixels[c], axis=1, keepdims=True), keys[c])
            keys[PIX] = jnp.where(lane == head, jnp.sum(grad_scores, axis=1, keepdims=True), keys[PIX])
            total = total + lax.dot_general(weighted_pixels(soft, pixels), grad, NT, preferred_element_type=f32)
        proj_ref[:, span] = total.astype(bf16)
    for c in range(PIX):
        field_ref[c] = field[c].astype(bf16)
    for c in range(PIX + 1):
        keys_ref[c] = keys[c]


def aggregate_back(member, pixels, key_rows, values, grads, groups):
    count, seq = pixels.shape[1:]
    rows = seq // groups
    width = values.shape[1]
    spec = pltpu.PrefetchScalarGridSpec(
        num_scalar_prefetch=1,
        grid=(1,),
        in_specs=[
            pl.BlockSpec((PIX, count, rows), lambda i, m: (0, 0, m[0])),
            pl.BlockSpec(key_rows.shape, lambda i, m: (0, 0, 0)),
            pl.BlockSpec(values.shape, lambda i, m: (0, 0)),
            pl.BlockSpec(grads.shape, lambda i, m: (0, 0)),
        ],
        out_specs=[
            pl.BlockSpec((PIX, count, rows), lambda i, m: (0, 0, 0)),
            pl.BlockSpec(((PIX + 1) * count, width), lambda i, m: (0, 0)),
            pl.BlockSpec((PIX + 1, count, 2 * HEAD_DIM), lambda i, m: (0, 0, 0)),
        ],
    )
    return pl.pallas_call(
        aggregate_back_kernel,
        grid_spec=spec,
        out_shape=[
            jax.ShapeDtypeStruct((PIX, count, rows), bf16),
            jax.ShapeDtypeStruct(((PIX + 1) * count, width), bf16),
            jax.ShapeDtypeStruct((PIX + 1, count, 2 * HEAD_DIM), f32),
        ],
        cost_estimate=pl.CostEstimate(
            flops=16 * (PIX + 1) * count * rows * width, bytes_accessed=3 << 20, transcendentals=rows * count * HEADS
        ),
        name="aggregate_back",
    )(member, pixels, key_rows, values, grads)


def layer_norm(inputs, gain):
    centered = inputs - jnp.mean(inputs, axis=-1, keepdims=True)
    inverse = lax.rsqrt(jnp.mean(centered * centered, axis=-1, keepdims=True) + epsilon)
    normed = centered * inverse
    return normed * gain, normed, inverse


def norm_back(grad_rows, normed, inverse, gain):
    grad_gain = jnp.sum(grad_rows * normed, axis=0)
    grad_normed = grad_rows * gain
    first_mean = jnp.mean(grad_normed, axis=-1, keepdims=True)
    second_mean = jnp.mean(grad_normed * normed, axis=-1, keepdims=True)
    return inverse * (grad_normed - first_mean - normed * second_mean), grad_gain


def swap(value, axis, bits):
    size = lax.axis_size(axis)
    return lax.ppermute(value, axis, [(s, s ^ bits) for s in range(size)])


def to_owners(pieces):
    total = pieces[0].astype(f32)
    for k in range(1, len(pieces)):
        total = total + swap(pieces[k], "var", k).astype(f32)
    return total.astype(bf16)


def from_all(own, groups):
    return [own] + [swap(own, "var", k) for k in range(1, groups)]


def patch_sum(value):
    size = lax.axis_size("patch")
    index = lax.axis_index("patch")
    bits = []
    bit = 2
    while bit < size:
        bits.append(bit)
        bit *= 2
    for bit in bits:
        half = value.shape[0] // 2
        high = (index // bit) % 2
        keep = lax.dynamic_slice_in_dim(value, high * half, half)
        send = lax.dynamic_slice_in_dim(value, (1 - high) * half, half)
        value = (keep.astype(f32) + swap(send, "patch", bit).astype(f32)).astype(bf16)
    for bit in reversed(bits):
        other = swap(value, "patch", bit)
        high = (index // bit) % 2
        value = jnp.where(
            high == 0, jnp.concatenate([value, other], axis=0), jnp.concatenate([other, value], axis=0)
        )
    return value


def join_cores(value, core):
    other = swap(value, "patch", 1)
    return jnp.where(
        core == 0, jnp.concatenate([value, other], axis=-1), jnp.concatenate([other, value], axis=-1)
    )


def all_sum(value):
    for axis in ("patch", "var"):
        bit = 1
        while bit < lax.axis_size(axis):
            value = value + swap(value, axis, bit)
            bit *= 2
    return value


def body(
    field_patches,
    var_ids,
    lead_bucket,
    patch_weight,
    var_embed,
    agg_query,
    agg_key,
    agg_value,
    agg_out,
    lead_table,
    ln1_gain,
    attn_qkv,
    attn_out,
    ln2_gain,
    mlp_in,
    mlp_in_bias,
    mlp_out,
    cotangent,
):
    groups = lax.axis_size("var")
    member = lax.axis_index("var")
    core = lax.axis_index("patch") % 2
    channels, pixel_count, samples, seq = field_patches.shape
    width = agg_key.shape[0]
    inner_width = mlp_in.shape[1]
    leads = lead_table.shape[0]
    vocab = var_embed.shape[0]
    rows = seq // groups
    own = width // groups
    count = channels * groups
    slots = [member ^ k for k in range(groups)]
    member_one = member.reshape(1).astype(jnp.int32)
    gain_one = ln1_gain.astype(f32)
    gain_two = ln2_gain.astype(f32)

    mine = jnp.concatenate(
        [
            field_patches.reshape(channels, pixel_count, seq).transpose(1, 0, 2),
            patch_weight.transpose(1, 0, 2),
        ],
        axis=2,
    )
    gathered = jnp.concatenate(from_all(mine, groups), axis=1)
    pixels = gathered[:, :, :seq]
    ids = jnp.concatenate([lax.dynamic_slice_in_dim(var_ids, slot * channels, channels) for slot in slots])
    table_pick = (ids[:, None] == jnp.arange(vocab, dtype=jnp.int32)[None, :]).astype(bf16)
    embeds = jnp.dot(table_pick, var_embed, preferred_element_type=f32).astype(bf16)
    stacked = jnp.concatenate([gathered[:, :, seq:], embeds[None]], axis=0).reshape(-1, width)
    head_of = jnp.arange(width, dtype=jnp.int32) // HEAD_DIM
    spread = head_of[:, None] == jnp.arange(HEADS, dtype=jnp.int32)[None, :]
    query_block = jnp.where(spread, agg_query[:, None], jnp.zeros((), bf16))
    query_keys = jnp.dot(agg_key, query_block, preferred_element_type=f32) * 0.125
    key_rows = jnp.dot(stacked.astype(f32), query_keys, precision=highest).reshape(PIX + 1, count, HEADS)
    values = jnp.dot(stacked, agg_value, preferred_element_type=f32).astype(bf16)
    values_t = values.T
    lead_row = lax.dynamic_slice_in_dim(lead_table, lead_bucket[0], 1).astype(f32)

    hidden_one, qkv, resid_zero, att_low = front(
        member_one, pixels, key_rows, values_t, agg_out, lead_row, gain_one[None], attn_qkv, groups
    )

    block = min(256, rows)
    mixed_parts, lse_parts, received = [None] * groups, [None] * groups, [None] * groups
    for k in reversed(range(groups)):
        mixed_parts[k], lse_parts[k] = attend(qkv, k, rows, block)
        received[k] = swap(mixed_parts[k], "var", k) if k else mixed_parts[k]
    mixed_heads = jnp.concatenate(mixed_parts, axis=0)
    lse = jnp.concatenate(lse_parts, axis=2)
    mixed = jnp.concatenate(received, axis=1)
    out_rows = jnp.concatenate([lax.dynamic_slice_in_dim(attn_out, slot * own, own) for slot in slots], axis=0)

    resid_one = resid_zero + jnp.dot(mixed, out_rows, preferred_element_type=f32)
    normed_two, plain_two, inverse_two = layer_norm(resid_one, gain_two)
    hidden_two = normed_two.astype(bf16)
    inner = jnp.dot(hidden_two, mlp_in, preferred_element_type=f32) + mlp_in_bias.astype(f32)
    activated = jax.nn.gelu(inner, approximate=False).astype(bf16)
    output = (resid_one + jnp.dot(activated, mlp_out, preferred_element_type=f32)).astype(bf16)
    output = output.reshape(samples, rows, width)

    grad_out = cotangent.reshape(rows, width)
    grad_act = jnp.einsum("rd,fd->rf", grad_out, mlp_out, preferred_element_type=f32)
    unused, gelu_back = jax.vjp(partial(jax.nn.gelu, approximate=False), inner)
    grad_inner = gelu_back(grad_act)[0].astype(bf16)
    grad_bias = jnp.sum(grad_inner.astype(f32), axis=0)
    grad_hidden_two = jnp.einsum("rf,df->rd", grad_inner, mlp_in, preferred_element_type=f32)
    grad_norm_two, grad_gain_two = norm_back(grad_hidden_two, plain_two, inverse_two, gain_two)
    grad_resid_one = grad_out.astype(f32) + grad_norm_two
    grad_branch = grad_resid_one.astype(bf16)
    grad_mixed = jnp.einsum("re,de->rd", grad_branch, out_rows, preferred_element_type=f32).astype(bf16)
    grad_heads = jnp.concatenate(
        [
            swap(grad_mixed[:, k * own : (k + 1) * own], "var", k) if k else grad_mixed[:, :own]
            for k in range(groups)
        ],
        axis=0,
    )

    def halves(grad):
        half = grad.shape[1] // 2
        return (
            lax.dynamic_slice_in_dim(grad, core * half, half, axis=1),
            lax.dynamic_slice_in_dim(grad, (1 - core) * half, half, axis=1),
        )

    def weight_sum(lefts, grad, dims):
        keep, send = halves(grad)
        pieces = []
        for left in lefts:
            theirs = lax.dot_general(left, send, dims, preferred_element_type=f32).astype(bf16)
            ours = lax.dot_general(left, keep, dims, preferred_element_type=f32)
            pieces.append((ours + swap(theirs, "patch", 1).astype(f32)).astype(bf16))
        return join_cores(patch_sum(to_owners(pieces)), core).astype(f32)

    part = inner_width // groups
    sum_mlp_out = weight_sum(
        [lax.dynamic_slice_in_dim(activated, slot * part, part, axis=1) for slot in slots], grad_out, TN
    )
    sum_mlp_in = weight_sum(
        [lax.dynamic_slice_in_dim(hidden_two, slot * own, own, axis=1) for slot in slots], grad_inner, TN
    )
    sum_attn_out = weight_sum(received, grad_branch, TN)

    pair = 2 * HEAD_DIM
    pairs = own // pair
    mine_qkv, weight_qkv = [], []
    arrived = [[None] * pairs for _ in range(groups)]
    for which in range(pairs):
        grads = attend_back(qkv, grad_heads, mixed_heads, lse, which, min(512, rows), 512)
        for k in range(groups):
            piece = grads[k * rows : (k + 1) * rows]
            arrived[k][which] = swap(piece, "var", k) if k else piece
        weight_qkv.append(lax.dot_general(hidden_one, grads, TN, preferred_element_type=f32).astype(bf16))
    grad_proj = jnp.zeros((3, rows, width), bf16)
    for k in range(groups):
        both = jnp.stack(
            [jnp.concatenate([p[:, t * pair : (t + 1) * pair] for p in arrived[k]], axis=1) for t in range(3)]
        )
        grad_proj = lax.dynamic_update_slice(grad_proj, both, (0, 0, slots[k] * own))
    grad_hidden_one = jnp.einsum("re,de->rd", grad_proj[0], attn_qkv[:, :width], preferred_element_type=f32)
    for t in range(1, 3):
        grad_hidden_one = grad_hidden_one + jnp.einsum(
            "re,de->rd", grad_proj[t], attn_qkv[:, t * width : (t + 1) * width], preferred_element_type=f32
        )
    normed_one, plain_one, inverse_one = layer_norm(resid_zero, gain_one)
    grad_norm_one, grad_gain_one = norm_back(grad_hidden_one, plain_one, inverse_one, gain_one)
    grad_resid_zero = grad_resid_one + grad_norm_one
    grad_agg = grad_resid_zero.astype(bf16)
    grad_att = jnp.einsum("re,de->dr", grad_agg, agg_out, preferred_element_type=f32).astype(bf16)

    both_cores = jnp.stack(weight_qkv)
    ours = lax.dynamic_slice_in_dim(both_cores, core, pairs // 2)
    theirs = lax.dynamic_slice_in_dim(both_cores, 1 - core, pairs // 2)
    core_qkv = (ours.astype(f32) + swap(theirs, "patch", 1).astype(f32)).astype(bf16).reshape(groups, own, 3 * pair)
    qkv_chunks = [lax.dynamic_index_in_dim(core_qkv, slot, 0, keepdims=False) for slot in slots]
    qkv_own = jnp.stack([swap(qkv_chunks[k], "var", k) if k else qkv_chunks[0] for k in range(groups)])
    qkv_own = patch_sum(qkv_own.transpose(1, 0, 2))
    qkv_other = swap(qkv_own, "patch", 1)
    ordered = jnp.where(
        core == 0, jnp.stack([qkv_own, qkv_other], axis=2), jnp.stack([qkv_other, qkv_own], axis=2)
    )
    ordered = ordered.reshape(own, groups, pairs, 3, pair).transpose(0, 3, 1, 2, 4).astype(f32)
    sum_qkv = jnp.zeros((own, 3, groups, pairs * pair), f32)
    for k in range(groups):
        sum_qkv = lax.dynamic_update_slice(
            sum_qkv, ordered[:, :, k].reshape(own, 3, 1, pairs * pair), (0, 0, slots[k], 0)
        )
    sum_qkv = sum_qkv.reshape(own, 3 * width)

    sum_agg_out = weight_sum(
        [lax.dynamic_slice_in_dim(att_low, slot * own, own) for slot in slots], grad_agg, (((1,), (0,)), ((), ()))
    )

    sample_sum = jnp.sum(grad_resid_zero, axis=0)
    lead_pick = (lead_bucket[:, None] == jnp.arange(leads, dtype=jnp.int32)[None, :]).astype(f32)
    grad_lead = lead_pick.reshape(leads, 1) * sample_sum[None, :]
    small = jnp.concatenate(
        [grad_bias.reshape(-1, width), grad_gain_two[None], grad_gain_one[None], grad_lead], axis=0
    )
    small = all_sum(small)
    bias_rows = inner_width // width
    sum_bias = lax.dynamic_slice_in_dim(small[:bias_rows].reshape(-1), member * part, part)
    sum_gain_two = lax.dynamic_slice_in_dim(small[bias_rows], member * own, own)
    sum_gain_one = lax.dynamic_slice_in_dim(small[bias_rows + 1], member * own, own)
    sum_lead = lax.dynamic_slice_in_dim(small[bias_rows + 2 :], member * (leads // groups), leads // groups)

    field_own, grad_values, grad_keys = aggregate_back(member_one, pixels, key_rows, values, grad_att, groups)
    field_slots = field_own.reshape(pixel_count, groups, channels, rows)
    field_parts = jnp.stack(
        [swap(field_slots[:, k], "var", k) if k else field_slots[:, 0] for k in range(groups)]
    )
    field_grad = jnp.zeros((channels, pixel_count, seq), f32)
    for k in range(groups):
        field_grad = lax.dynamic_update_slice(
            field_grad, field_parts[k].transpose(1, 0, 2).astype(f32), (0, 0, slots[k] * rows)
        )
    field_grad = field_grad.reshape(channels, pixel_count, samples, seq)

    keep, send = halves(grad_values)
    keys_low = grad_keys.reshape(-1, 2 * HEAD_DIM).astype(bf16)
    keep = jnp.concatenate([keep, keys_low], axis=1)
    send = jnp.concatenate([send, keys_low], axis=1)
    tail = (keep.astype(f32) + swap(send, "patch", 1).astype(f32)).astype(bf16)
    tail = tail.reshape(PIX + 1, groups, channels, -1)
    tail = to_owners([tail[:, k] for k in range(groups)])
    bit = 2
    while bit < lax.axis_size("patch"):
        tail = (tail.astype(f32) + swap(tail, "patch", bit).astype(f32)).astype(bf16)
        bit *= 2
    tail = jnp.stack(from_all(tail, groups), axis=1).reshape((PIX + 1) * count, -1)
    sum_values = join_cores(tail[:, : width // 2], core)
    sum_keys = tail[:, width // 2 : width // 2 + HEADS].astype(f32)

    by_kind = sum_values.reshape(PIX + 1, count, width)
    keys_kind = sum_keys.reshape(PIX + 1, count, HEADS)
    weight_rows = by_kind[:PIX, :channels].reshape(PIX * channels, width)
    weight_keys = keys_kind[:PIX, :channels].reshape(PIX * channels, HEADS)
    own_ids = member * (vocab // groups) + jnp.arange(vocab // groups, dtype=jnp.int32)
    own_pick = own_ids[:, None] == ids[None, :]
    embed_rows = jnp.dot(own_pick.astype(bf16), by_kind[PIX], preferred_element_type=f32).astype(bf16)
    embed_keys = jnp.dot(own_pick.astype(f32), keys_kind[PIX], precision=highest)
    both_rows = jnp.concatenate([weight_rows, embed_rows], axis=0)
    both_keys = jnp.concatenate([weight_keys, embed_keys], axis=0)
    grad_stacked = jnp.einsum("ve,de->vd", both_rows, agg_value, preferred_element_type=f32) + jnp.einsum(
        "vh,dh->vd", both_keys, query_keys, precision=highest
    )
    sum_patch = grad_stacked[: PIX * channels].reshape(pixel_count, channels, width).transpose(1, 0, 2)
    sum_table = grad_stacked[PIX * channels :]
    stacked_own = lax.dynamic_slice_in_dim(stacked, member * own, own, axis=1)
    sum_value = jnp.einsum("vd,ve->de", stacked_own, sum_values, preferred_element_type=f32)
    grad_query_keys = jnp.einsum("vd,vh->dh", stacked.astype(f32), sum_keys, precision=highest)
    own_query_keys = lax.dynamic_slice_in_dim(grad_query_keys, member * own, own)
    sum_key = (
        jnp.dot(own_query_keys, spread.T.astype(f32), precision=highest) * agg_query.astype(f32)[None, :] * 0.125
    )
    agg_key_own = lax.dynamic_slice_in_dim(agg_key, member * own, own, axis=1).astype(f32)
    spread_own = lax.dynamic_slice_in_dim(spread.astype(f32), member * own, own)
    sum_query = (
        jnp.sum(jnp.einsum("dc,dh->ch", agg_key_own, grad_query_keys, precision=highest) * spread_own, axis=1) * 0.125
    )
    return (
        output,
        field_grad,
        sum_patch,
        sum_table,
        sum_query,
        sum_key,
        sum_value,
        sum_agg_out,
        sum_lead,
        sum_gain_one,
        sum_qkv,
        sum_attn_out,
        sum_gain_two,
        sum_mlp_in,
        sum_bias,
        sum_mlp_out,
    )


def solution(mesh):
    placed = (
        P("var", None, "patch", None),
        P(),
        P("patch"),
        P("var", None, None),
        P(),
        P(),
        P(),
        P(),
        P(),
        P(),
        P(),
        P(),
        P(),
        P(),
        P(),
        P(),
        P(),
        P("patch", "var", None),
    )
    return jax.shard_map(
        body,
        mesh=mesh,
        in_specs=placed,
        out_specs=(
            P("patch", "var", None),
            P("var", None, "patch", None),
            P("var", None, None),
            P("var", None),
            P("var"),
            P("var", None),
            P("var", None),
            P("var", None),
            P("var", None),
            P("var"),
            P("var", None),
            P("var", None),
            P("var"),
            P("var", None),
            P("var"),
            P("var", None),
        ),
        check_vma=False,
    )
```

time: 1980 us -> 780 us (0.39)
  waiting for transfers between devices: 1270 us -> 233 us
  matrix products: 332 us -> 138 us
  Pallas kernels: 0 us -> 115 us
  blocking collectives: 73 us -> 0 us
  starting transfers between devices: 19.7 us -> 72.3 us
  other arithmetic: 102 us -> 69.2 us
    reduce_scatter x9 -> x0, waiting for transfers between devices: 739 us -> none  [the longest x1 157 us: body(): lax.psum_scatter(grad_mlp_in, 'var', scatter_dimension=0, tiled=True)]
    psum x2 -> x0, waiting for transfers between devices: 346 us -> none  [body(): lax.psum((parts_in[0], parts_in[1], parts_in[2], parts_in[3], parts_in[4]...]
    ppermute x0 -> x90, waiting for transfers between devices: none -> 233 us  [swap(): return lax.ppermute(value, axis, [(s, s ^ bits) for s in range(size)])]
    dot_general x63 -> x56, matrix products: 332 us -> 138 us  [the longest x16 28.6 us: weight_sum(): ours = lax.dot_general(left, keep, dims, preferred_element_type=f32)]
    all_gather x3 -> x0, waiting for transfers between devices: 115 us -> none  [the longest x1 49.8 us: body(): lax.all_gather(key_local, 'var', axis=1, tiled=True)]
    pallas_call x0 -> x8, Pallas kernels: none -> 115 us  [the longest x2 48.7 us: attend_back(): pl.pallas_call(partial(attend_back_kernel, chunk=chunk), grid=(seq // blo...]
    ppermute x0 -> x90, starting transfers between devices: none -> 72.3 us  [swap(): return lax.ppermute(value, axis, [(s, s ^ bits) for s in range(size)])]
    all_to_all x3 -> x0, waiting for transfers between devices: 70.6 us -> none  [the longest x1 70.6 us: body(): lax.all_to_all(sums.reshape(1, width, samples_here, seq_len), 'var', spli...]
  transfers between devices with their start and end apart: 19 -> 90, of which waited for: 14 -> 37; matrix products, arithmetic and copies ran while one was open for 10% -> 34% of each run, Pallas kernels for 0% -> 7%
where the time goes in v1:
time: 780 us; the launch traced here: 773 us
  waiting for transfers between devices  233 us (30%)
  local copies, waits for them, and re-layouts  142 us (18%)
  matrix products  138 us (18%)
  Pallas kernels  115 us (15%)
  starting transfers between devices  72.3 us (9%)
  other arithmetic  69.2 us (9%)
    ppermute x90, waiting for transfers between devices, swap(): return lax.ppermute(value, axis, [(s, s ^ bits) for s in range(size)])  233 us
    ppermute x90, starting transfers between devices, swap(): return lax.ppermute(value, axis, [(s, s ^ bits) for s in range(size)])  72.3 us
    dynamic_update_slice x4, local copies, waits for them, and re-layouts, body(): lax.dynamic_update_slice(sum_qkv, ordered[:, :, k].reshape(own, 3, 1, pai...  69.8 us
    pallas_call x2, Pallas kernels, attend_back(): pl.pallas_call(partial(attend_back_kernel, chunk=chunk), grid=(seq // blo...  48.7 us
    pallas_call x4, Pallas kernels, attend(): pl.pallas_call(attend_kernel, grid=(pairs, steps), in_specs=[pl.BlockSpec...  35.8 us
    dot_general x16, matrix products, weight_sum(): ours = lax.dot_general(left, keep, dims, preferred_element_type=f32)  28.6 us
    dot_general x16, matrix products, weight_sum(): lax.dot_general(left, send, dims, preferred_element_type=f32).astype(bf16)  24.5 us
    dot_general x1, matrix products, body(): jnp.dot(hidden_two, mlp_in, preferred_element_type=f32)  24.3 us
  transfers between devices with their start and end apart: 90, of which 37 were waited for; matrix products, arithmetic and copies ran while one was open for 34% of the time, Pallas kernels for 7%

profile of v1, /device:TPU:0, one launch (start us, length us, event | category | flops | bytes accessed | tf_op | source)
XLA Modules:
  0.0 773.3 jit_solution(4427809320360590003)
XLA Ops:
  3.6 3.9 collective-permute-start.2
  20.7 4.5 collective-permute-done.1
  31.8 23.6 %front.1 = (bf16[2048,1024]{1,0:T(8,128)(2,1)}, bf16[2048,768]{1,0:T(8,128)(2,1)}, f32[512,1024]{1,0:T(8,128)}, bf16[1024,512]{1,0:T(8,128)(2,1)}) custom-call(s32[1]{0:T(128)} %bitcast.member, bf16[4,48,2048]{2,1,0:T(8,128)(2,1)} %slice.276.pixel_ref, f32[5,48,16]{2,1,0:T(8,128)} %fusion.156.key_ref, bf16[1024,240]{1,0:T(8,128)(2,1)} %copy.82.value_ref, ...), custom_call_target="tpu_custom_call" | custom-call | flops 7516192768 | bytes 16777216 | tf_op jit(solution)/shard_map/front/pallas_call | solution.py:104
  55.5 8.9 %attend.7 = (bf16[512,256]{1,0:T(8,128)(2,1)}, f32[2,2,512]{2,1,0:T(2,128)}) custom-call(bf16[2048,768]{1,0:T(8,128)(2,1)} %get-tuple-element.32.q_ref.k_ref.v_ref, bf16[2048,768]{1,0:T(8,128)(2,1)} %get-tuple-element.32.q_ref.k_ref.v_ref, bf16[2048,768]{1,0:T(8,128)(2,1)} %get-tuple-element.32.q_ref.k_ref.v_ref), custom_call_target="tpu_custom_call" | custom-call | flops 4294967296 | bytes 3145728 | tf_op jit(solution)/shard_map/attend/pallas_call | solution.py:144
  64.4 8.9 %attend.6 = (bf16[512,256]{1,0:T(8,128)(2,1)}, f32[2,2,512]{2,1,0:T(2,128)}) custom-call(bf16[2048,768]{1,0:T(8,128)(2,1)} %get-tuple-element.32.q_ref.k_ref.v_ref, bf16[2048,768]{1,0:T(8,128)(2,1)} %get-tuple-element.32.q_ref.k_ref.v_ref, bf16[2048,768]{1,0:T(8,128)(2,1)} %get-tuple-element.32.q_ref.k_ref.v_ref), custom_call_target="tpu_custom_call" | custom-call | flops 4294967296 | bytes 3145728 | tf_op jit(solution)/shard_map/attend/pallas_call | solution.py:144
  73.3 8.9 %attend.5 = (bf16[512,256]{1,0:T(8,128)(2,1)}, f32[2,2,512]{2,1,0:T(2,128)}) custom-call(bf16[2048,768]{1,0:T(8,128)(2,1)} %get-tuple-element.32.q_ref.k_ref.v_ref, bf16[2048,768]{1,0:T(8,128)(2,1)} %get-tuple-element.32.q_ref.k_ref.v_ref, bf16[2048,768]{1,0:T(8,128)(2,1)} %get-tuple-element.32.q_ref.k_ref.v_ref), custom_call_target="tpu_custom_call" | custom-call | flops 4294967296 | bytes 3145728 | tf_op jit(solution)/shard_map/attend/pallas_call | solution.py:144
  82.2 9.1 %attend.4 = (bf16[512,256]{1,0:T(8,128)(2,1)}, f32[2,2,512]{2,1,0:T(2,128)}) custom-call(bf16[2048,768]{1,0:T(8,128)(2,1)} %get-tuple-element.32.q_ref.k_ref.v_ref, bf16[2048,768]{1,0:T(8,128)(2,1)} %get-tuple-element.32.q_ref.k_ref.v_ref, bf16[2048,768]{1,0:T(8,128)(2,1)} %get-tuple-element.32.q_ref.k_ref.v_ref), custom_call_target="tpu_custom_call" | custom-call | flops 4294967296 | bytes 3145728 | tf_op jit(solution)/shard_map/attend/pallas_call | solution.py:144
  101.9 4.0 collective-permute-done.4
  108.5 24.3 %multiply_convert_fusion = (bf16[512,4096]{1,0:T(8,128)(2,1)}, f32[512,4096]{1,0:T(8,128)}, f32[512,4096]{1,0:T(8,128)}) fusion(f32[4096]{0:T(1024)S(1)} %convert_element_type.485, bf16[512,1024]{1,0:T(8,128)(2,1)S(1)} %multiply_convert_fusion.1, bf16[1024,4096]{1,0:T(8,128)(2,1)S(1)} %bitcast.256), kind=kOutput, calls=%fused_computation.4 | convolution fusion | flops 4433379328 | bytes 30425088 | tf_op jit(solution)/shard_map/dot_general | solution.py:449
  132.7 13.4 %convert_reduce_fusion = (f32[4096]{0:T(1024)S(1)}, bf16[512,4096]{1,0:T(8,128)(2,1)S(1)}) fusion(f32[512,4096]{1,0:T(8,128)} %get-tuple-element.89, bf16[4096,1024]{1,0:T(8,128)(2,1)} %param.34, bf16[1,512,1024]{2,1,0:T(8,128)(2,1)S(1)} %copy-done.22, f32[512,4096]{1,0:T(8,128)} %get-tuple-element.153, f32[4096]{0:T(1024)S(1)} %convert_element_type.485), kind=kOutput, calls=%fused_computation.2 | convolution fusion | flops 4330614784 | bytes 30441472 | tf_op jit(solution)/shard_map/rd,fd->rf/dot_general | solution.py:455
  146.1 9.8 %multiply_reduce_fusion.1 = (f32[1024]{0:T(1024)}, f32[512]{0:T(512)S(1)}, f32[512]{0:T(512)S(1)}, f32[512,1024]{1,0:T(8,128)S(1)}) fusion(f32[512,1024]{1,0:T(8,128)S(1)} %get-tuple-element.152, f32[512]{0:T(512)S(1)} %add_rsqrt_fusion.1, f32[512]{0:T(512)S(1)} %broadcast_multiply_fusion.6, f32[1024]{0:T(1024)S(1)} %convert_element_type.483, ...), kind=kOutput, calls=%fused_computation.40 | convolution fusion | flops 4299159552 | bytes 16793600 | tf_op jit(solution)/shard_map/rf,df->rd/dot_general | solution.py:459
  162.9 8.2 %fusion.17 = bf16[1,512,1024]{2,1,0:T(8,128)(2,1)} fusion(f32[512,1024]{1,0:T(8,128)S(1)} %get-tuple-element.152, bf16[512,4096]{1,0:T(8,128)(2,1)S(1)} %copy-done.60, bf16[4096,1024]{1,0:T(8,128)(2,1)} %param.34), kind=kOutput, calls=%fused_computation.75 | convolution fusion | flops 4296015872 | bytes 15728640 | tf_op jit(solution)/shard_map/dot_general | solution.py:451
  183.6 3.2 convolution_convert_fusion.6
  198.0 24.5 %attend_back.3 = bf16[2048,384]{1,0:T(8,128)(2,1)} custom-call(bf16[2048,768]{1,0:T(8,128)(2,1)} %get-tuple-element.32.q_ref.k_ref.v_ref, bf16[2048,768]{1,0:T(8,128)(2,1)} %get-tuple-element.32.q_ref.k_ref.v_ref, bf16[2048,768]{1,0:T(8,128)(2,1)} %get-tuple-element.32.q_ref.k_ref.v_ref, bf16[2048,256]{1,0:T(8,128)(2,1)} %pad_maximum_fusion.2.g_ref, ...), custom_call_target="tpu_custom_call" | custom-call | flops 21474836480 | bytes 5242880 | tf_op jit(solution)/shard_map/attend_back/pallas_call | solution.py:214
  222.5 24.2 %attend_back.2 = bf16[2048,384]{1,0:T(8,128)(2,1)} custom-call(bf16[2048,768]{1,0:T(8,128)(2,1)} %get-tuple-element.32.q_ref.k_ref.v_ref, bf16[2048,768]{1,0:T(8,128)(2,1)} %get-tuple-element.32.q_ref.k_ref.v_ref, bf16[2048,768]{1,0:T(8,128)(2,1)} %get-tuple-element.32.q_ref.k_ref.v_ref, bf16[2048,256]{1,0:T(8,128)(2,1)} %pad_maximum_fusion.2.g_ref, ...), custom_call_target="tpu_custom_call" | custom-call | flops 21474836480 | bytes 5242880 | tf_op jit(solution)/shard_map/attend_back/pallas_call | solution.py:214
  248.9 5.2 fusion.39
  269.1 6.1 collective-permute-done.60
  282.2 5.6 collective-permute-done.9
  289.6 15.0 %collective-permute-done.12 = bf16[512,384]{1,0:T(8,128)(2,1)S(1)} collective-permute-done((bf16[512,384]{1,0:T(8,128)(2,1)S(1)}, bf16[512,384]{1,0:T(8,128)(2,1)S(1)}, u32[]{:S(2)}, u32[]{:S(2)}) %collective-permute-start.12) | collective-permute-done | bytes 393248 | tf_op jit(solution)/shard_map/ppermute | solution.py:321
  306.2 9.2 %collective-permute-done.11 = bf16[512,384]{1,0:T(8,128)(2,1)S(1)} collective-permute-done((bf16[512,384]{1,0:T(8,128)(2,1)S(1)}, bf16[512,384]{1,0:T(8,128)(2,1)S(1)}, u32[]{:S(2)}, u32[]{:S(2)}) %collective-permute-start.11) | collective-permute-done | bytes 393248 | tf_op jit(solution)/shard_map/ppermute | solution.py:321
  332.2 6.5 aggregate_back.1
  358.8 4.8 collective-permute-done.42
  373.4 4.7 collective-permute-done.64
  397.7 3.8 add_convert_fusion.7
  401.7 3.5 add_convert_fusion.8
  405.6 3.1 add_convert_fusion.9
  421.3 3.4 collective-permute-done.22
  435.0 4.2 collective-permute-done.23
  446.1 16.5 %collective-permute-done.26 = bf16[5,12,640]{2,1,0:T(8,128)(2,1)S(1)} collective-permute-done((bf16[5,12,640]{2,1,0:T(8,128)(2,1)S(1)}, bf16[5,12,640]{2,1,0:T(8,128)(2,1)S(1)}, u32[]{:S(2)}, u32[]{:S(2)}) %collective-permute-start.26) | collective-permute-done | bytes 76832 | tf_op jit(solution)/shard_map/ppermute | solution.py:321
  464.3 21.8 %collective-permute-done.25 = bf16[5,12,640]{2,1,0:T(8,128)(2,1)S(1)} collective-permute-done((bf16[5,12,640]{2,1,0:T(8,128)(2,1)S(1)}, bf16[5,12,640]{2,1,0:T(8,128)(2,1)S(1)}, u32[]{:S(2)}, u32[]{:S(2)}) %collective-permute-start.25) | collective-permute-done | bytes 76832 | tf_op jit(solution)/shard_map/ppermute | solution.py:321
  494.6 4.0 collective-permute-done.36
  499.3 4.6 collective-permute-done.37
  525.0 19.1 %collective-permute-done.84 = bf16[1024,512]{1,0:T(8,128)(2,1)S(1)} collective-permute-done((bf16[1024,512]{1,0:T(8,128)(2,1)}, bf16[1024,512]{1,0:T(8,128)(2,1)S(1)}, u32[]{:S(2)}, u32[]{:S(2)}) %collective-permute-start.84) | collective-permute-done | bytes 1048608 | tf_op jit(solution)/shard_map/ppermute | solution.py:321
  544.7 21.5 %collective-permute-done.82 = bf16[1024,512]{1,0:T(8,128)(2,1)S(1)} collective-permute-done((bf16[1024,512]{1,0:T(8,128)(2,1)}, bf16[1024,512]{1,0:T(8,128)(2,1)S(1)}, u32[]{:S(2)}, u32[]{:S(2)}) %collective-permute-start.82) | collective-permute-done | bytes 1048608 | tf_op jit(solution)/shard_map/ppermute | solution.py:321
  573.2 9.5 %collective-permute-done.74 = bf16[64,2048]{1,0:T(8,128)(2,1)} collective-permute-done((bf16[64,2048]{1,0:T(8,128)(2,1)}, bf16[64,2048]{1,0:T(8,128)(2,1)}, u32[]{:S(2)}, u32[]{:S(2)}) %collective-permute-start.74) | collective-permute-done | bytes 262176 | tf_op jit(solution)/shard_map/ppermute | solution.py:321
  583.9 10.7 %collective-permute-done.85 = bf16[512,512]{1,0:T(8,128)(2,1)} collective-permute-done((bf16[512,512]{1,0:T(8,128)(2,1)}, bf16[512,512]{1,0:T(8,128)(2,1)}, u32[]{:S(2)}, u32[]{:S(2)}) %collective-permute-start.85) | collective-permute-done | bytes 524320 | tf_op jit(solution)/shard_map/ppermute | solution.py:321
  596.0 14.7 %collective-permute-done.51 = bf16[64,4,384]{0,2,1:T(8,128)(2,1)} collective-permute-done((bf16[64,4,384]{0,2,1:T(8,128)(2,1)S(1)}, bf16[64,4,384]{0,2,1:T(8,128)(2,1)}, u32[]{:S(2)}, u32[]{:S(2)}) %collective-permute-start.51) | collective-permute-done | bytes 196640 | tf_op jit(solution)/shard_map/ppermute | solution.py:321
  612.4 4.0 collective-permute-done.75
  616.5 5.3 collective-permute-done.86
  622.7 13.3 %collective-permute-done.52 = bf16[128,4,384]{0,2,1:T(8,128)(2,1)S(1)} collective-permute-done((bf16[128,4,384]{0,2,1:T(8,128)(2,1)S(1)}, bf16[128,4,384]{0,2,1:T(8,128)(2,1)S(1)}, u32[]{:S(2)}, u32[]{:S(2)}) %collective-permute-start.52) | collective-permute-done | bytes 393248 | tf_op jit(solution)/shard_map/ppermute | solution.py:321
  653.7 4.7 collective-permute-done.88
  688.8 17.5 %dynamic_update_slice.48 = f32[256,3,4,256]{3,2,1,0:T(4,128)} dynamic-update-slice(f32[256,3,4,256]{3,2,1,0:T(4,128)} %broadcast_in_dim.31, f32[256,3,1,256]{3,2,1,0:T(1,128)} %copy.107, s32[]{:T(128)} %constant.210.clone.1, s32[]{:T(128)} %constant.210.clone.1, s32[]{:T(128)S(6)} %select_n.432, s32[]{:T(128)} %constant.210.clone.1) | dynamic-update-slice | bytes 1572868 | tf_op jit(solution)/shard_map/dynamic_update_slice | solution.py:538
  706.2 17.5 %dynamic_update_slice.49 = f32[256,3,4,256]{3,2,1,0:T(4,128)} dynamic-update-slice(f32[256,3,4,256]{3,2,1,0:T(4,128)} %dynamic_update_slice.48, f32[256,3,1,256]{3,2,1,0:T(1,128)} %copy.109, s32[]{:T(128)} %constant.210.clone.1, s32[]{:T(128)} %constant.210.clone.1, s32[]{:T(128)S(6)} %select_n.433, s32[]{:T(128)} %constant.210.clone.1) | dynamic-update-slice | bytes 1572868 | tf_op jit(solution)/shard_map/dynamic_update_slice | solution.py:538
  723.7 17.5 %dynamic_update_slice.50 = f32[256,3,4,256]{3,2,1,0:T(4,128)} dynamic-update-slice(f32[256,3,4,256]{3,2,1,0:T(4,128)} %dynamic_update_slice.49, f32[256,3,1,256]{3,2,1,0:T(1,128)} %copy.111, s32[]{:T(128)} %constant.210.clone.1, s32[]{:T(128)} %constant.210.clone.1, s32[]{:T(128)S(6)} %select_n.434, s32[]{:T(128)} %constant.210.clone.1) | dynamic-update-slice | bytes 1572868 | tf_op jit(solution)/shard_map/dynamic_update_slice | solution.py:538
  741.1 17.5 %dynamic_update_slice.51 = f32[256,3,4,256]{3,2,1,0:T(4,128)} dynamic-update-slice(f32[256,3,4,256]{3,2,1,0:T(4,128)} %dynamic_update_slice.50, f32[256,3,1,256]{3,2,1,0:T(1,128)} %copy.113, s32[]{:T(128)} %constant.210.clone.1, s32[]{:T(128)} %constant.210.clone.1, s32[]{:T(128)S(6)} %select_n.435, s32[]{:T(128)} %constant.210.clone.1) | dynamic-update-slice | bytes 1572868 | tf_op jit(solution)/shard_map/dynamic_update_slice | solution.py:538
  758.6 5.1 reshape.360
  763.7 4.3 fusion.6
  768.0 5.1 fusion.7
  (570 shorter events, 281.4 us)
Async XLA Ops:
  3.6 17.1 %collective-permute-start.2 = (bf16[4,12,3072]{2,1,0:T(8,128)(2,1)}, bf16[4,12,3072]{2,1,0:T(8,128)(2,1)S(1)}, u32[]{:S(2)}, u32[]{:S(2)}) collective-permute-start(bf16[4,12,3072]{2,1,0:T(8,128)(2,1)} %pad_maximum_fusion.11), channel_id=1, source_target_pairs={{0,24},{8,16},{16,8},{24,0},{1,25},{9,17},{17,9},{25,1},{2,26},{10... | collective-permute-start | bytes 884744 | tf_op jit(solution)/shard_map/ppermute | solution.py:321
  7.5 17.7 %collective-permute-start.1 = (bf16[4,12,3072]{2,1,0:T(8,128)(2,1)}, bf16[4,12,3072]{2,1,0:T(8,128)(2,1)S(1)}, u32[]{:S(2)}, u32[]{:S(2)}) collective-permute-start(bf16[4,12,3072]{2,1,0:T(8,128)(2,1)} %pad_maximum_fusion.11), channel_id=1, source_target_pairs={{0,16},{8,24},{16,0},{24,8},{1,17},{9,25},{17,1},{25,9},{2,18},{10... | collective-permute-start | bytes 884744 | tf_op jit(solution)/shard_map/ppermute | solution.py:321
  8.0 17.6 %collective-permute-start = (bf16[4,12,3072]{2,1,0:T(8,128)(2,1)}, bf16[4,12,3072]{2,1,0:T(8,128)(2,1)}, u32[]{:S(2)}, u32[]{:S(2)}) collective-permute-start(bf16[4,12,3072]{2,1,0:T(8,128)(2,1)} %pad_maximum_fusion.11), channel_id=1, source_target_pairs={{0,8},{8,0},{16,24},{24,16},{1,9},{9,1},{17,25},{25,17},{2,10},{10... | collective-permute-start | bytes 884744 | tf_op jit(solution)/shard_map/ppermute | solution.py:321
  175.5 19.8 %collective-permute-start.8 = (bf16[512,256]{1,0:T(8,128)(2,1)}, bf16[512,256]{1,0:T(8,128)(2,1)}, u32[]{:S(2)}, u32[]{:S(2)}) collective-permute-start(bf16[512,256]{1,0:T(8,128)(2,1)} %get-tuple-element.111), channel_id=1, source_target_pairs={{0,24},{8,16},{16,8},{24,0},{1,25},{9,17},{17,9},{25,1},{2,26},{10... | collective-permute-start | bytes 786440 | tf_op jit(solution)/shard_map/ppermute | solution.py:321
  177.0 18.2 %collective-permute-start.7 = (bf16[512,256]{1,0:T(8,128)(2,1)}, bf16[512,256]{1,0:T(8,128)(2,1)}, u32[]{:S(2)}, u32[]{:S(2)}) collective-permute-start(bf16[512,256]{1,0:T(8,128)(2,1)} %get-tuple-element.112), channel_id=1, source_target_pairs={{0,16},{8,24},{16,0},{24,8},{1,17},{9,25},{17,1},{25,9},{2,18},{10... | collective-permute-start | bytes 786440 | tf_op jit(solution)/shard_map/ppermute | solution.py:321
  178.5 17.2 %collective-permute-start.6 = (bf16[512,256]{1,0:T(8,128)(2,1)}, bf16[512,256]{1,0:T(8,128)(2,1)}, u32[]{:S(2)}, u32[]{:S(2)}) collective-permute-start(bf16[512,256]{1,0:T(8,128)(2,1)} %get-tuple-element.113), channel_id=1, source_target_pairs={{0,8},{8,0},{16,24},{24,16},{1,9},{9,1},{17,25},{25,17},{2,10},{10... | collective-permute-start | bytes 786440 | tf_op jit(solution)/shard_map/ppermute | solution.py:321
  182.0 74.6 %collective-permute-start.59 = (bf16[256,512]{1,0:T(8,128)(2,1)}, bf16[256,512]{1,0:T(8,128)(2,1)}, u32[]{:S(2)}, u32[]{:S(2)}) collective-permute-start(bf16[256,512]{1,0:T(8,128)(2,1)} %convolution_convert_fusion.13), channel_id=1, source_target_pairs={{0,1},{1,0},{2,3},{3,2},{4,5},{5,4},{6,7},{7,6},{8,9},{9,8},{10,11... | collective-permute-start | bytes 786440 | tf_op jit(solution)/shard_map/ppermute | solution.py:321
  183.1 76.6 %collective-permute-start.57 = (bf16[256,512]{1,0:T(8,128)(2,1)}, bf16[256,512]{1,0:T(8,128)(2,1)}, u32[]{:S(2)}, u32[]{:S(2)}) collective-permute-start(bf16[256,512]{1,0:T(8,128)(2,1)} %convolution_convert_fusion.14), channel_id=1, source_target_pairs={{0,1},{1,0},{2,3},{3,2},{4,5},{5,4},{6,7},{7,6},{8,9},{9,8},{10,11... | collective-permute-start | bytes 786440 | tf_op jit(solution)/shard_map/ppermute | solution.py:321
  195.2 67.2 %collective-permute-start.55 = (bf16[256,512]{1,0:T(8,128)(2,1)}, bf16[256,512]{1,0:T(8,128)(2,1)}, u32[]{:S(2)}, u32[]{:S(2)}) collective-permute-start(bf16[256,512]{1,0:T(8,128)(2,1)} %convolution_convert_fusion.15), channel_id=1, source_target_pairs={{0,1},{1,0},{2,3},{3,2},{4,5},{5,4},{6,7},{7,6},{8,9},{9,8},{10,11... | collective-permute-start | bytes 786440 | tf_op jit(solution)/shard_map/ppermute | solution.py:321
  195.3 69.6 %collective-permute-start.54 = (bf16[256,512]{1,0:T(8,128)(2,1)}, bf16[256,512]{1,0:T(8,128)(2,1)}, u32[]{:S(2)}, u32[]{:S(2)}) collective-permute-start(bf16[256,512]{1,0:T(8,128)(2,1)} %convolution_convert_fusion.16), channel_id=1, source_target_pairs={{0,1},{1,0},{2,3},{3,2},{4,5},{5,4},{6,7},{7,6},{8,9},{9,8},{10,11... | collective-permute-start | bytes 786440 | tf_op jit(solution)/shard_map/ppermute | solution.py:321
  195.8 201.5 %collective-permute-start.71 = (bf16[256,2048]{1,0:T(8,128)(2,1)}, bf16[256,2048]{1,0:T(8,128)(2,1)}, u32[]{:S(2)}, u32[]{:S(2)}) collective-permute-start(bf16[256,2048]{1,0:T(8,128)(2,1)} %convolution_convert_fusion), channel_id=1, source_target_pairs={{0,1},{1,0},{2,3},{3,2},{4,5},{5,4},{6,7},{7,6},{8,9},{9,8},{10,11... | collective-permute-start | bytes 3145736 | tf_op jit(solution)/shard_map/ppermute | solution.py:321
  256.6 24.9 %collective-permute-start.10 = (bf16[512,384]{1,0:T(8,128)(2,1)S(1)}, bf16[512,384]{1,0:T(8,128)(2,1)S(1)}, u32[]{:S(2)}, u32[]{:S(2)}) collective-permute-start(bf16[512,384]{1,0:T(8,128)(2,1)S(1)} %get-tuple-element.103), channel_id=1, source_target_pairs={{0,8},{8,0},{16,24},{24,16},{1,9},{9,1},{17,25},{25,17},{2,10},{10... | collective-permute-start | bytes 1179656 | tf_op jit(solution)/shard_map/ppermute | solution.py:321
  275.2 126.4 %collective-permute-start.69 = (bf16[256,2048]{1,0:T(8,128)(2,1)}, bf16[256,2048]{1,0:T(8,128)(2,1)}, u32[]{:S(2)}, u32[]{:S(2)}) collective-permute-start(bf16[256,2048]{1,0:T(8,128)(2,1)} %convolution_convert_fusion.1), channel_id=1, source_target_pairs={{0,1},{1,0},{2,3},{3,2},{4,5},{5,4},{6,7},{7,6},{8,9},{9,8},{10,11... | collective-permute-start | bytes 3145736 | tf_op jit(solution)/shard_map/ppermute | solution.py:321
  279.9 24.7 %collective-permute-start.12 = (bf16[512,384]{1,0:T(8,128)(2,1)S(1)}, bf16[512,384]{1,0:T(8,128)(2,1)S(1)}, u32[]{:S(2)}, u32[]{:S(2)}) collective-permute-start(bf16[512,384]{1,0:T(8,128)(2,1)S(1)} %get-tuple-element.102), channel_id=1, source_target_pairs={{0,16},{8,24},{16,0},{24,8},{1,17},{9,25},{17,1},{25,9},{2,18},{10... | collective-permute-start | bytes 1179656 | tf_op jit(solution)/shard_map/ppermute | solution.py:321
  281.6 33.8 %collective-permute-start.11 = (bf16[512,384]{1,0:T(8,128)(2,1)S(1)}, bf16[512,384]{1,0:T(8,128)(2,1)S(1)}, u32[]{:S(2)}, u32[]{:S(2)}) collective-permute-start(bf16[512,384]{1,0:T(8,128)(2,1)S(1)} %get-tuple-element.99), channel_id=1, source_target_pairs={{0,16},{8,24},{16,0},{24,8},{1,17},{9,25},{17,1},{25,9},{2,18},{10... | collective-permute-start | bytes 1179656 | tf_op jit(solution)/shard_map/ppermute | solution.py:321
  287.9 29.4 %collective-permute-start.14 = (bf16[512,384]{1,0:T(8,128)(2,1)S(1)}, bf16[512,384]{1,0:T(8,128)(2,1)S(1)}, u32[]{:S(2)}, u32[]{:S(2)}) collective-permute-start(bf16[512,384]{1,0:T(8,128)(2,1)S(1)} %get-tuple-element.101), channel_id=1, source_target_pairs={{0,24},{8,16},{16,8},{24,0},{1,25},{9,17},{17,9},{25,1},{2,26},{10... | collective-permute-start | bytes 1179656 | tf_op jit(solution)/shard_map/ppermute | solution.py:321
  315.4 29.4 %collective-permute-start.61 = (bf16[128,512]{1,0:T(8,128)(2,1)S(1)}, bf16[128,512]{1,0:T(8,128)(2,1)}, u32[]{:S(2)}, u32[]{:S(2)}) collective-permute-start(bf16[128,512]{1,0:T(8,128)(2,1)S(1)} %constant_dynamic-slice_fusion.6), channel_id=1, source_target_pairs={{0,2},{1,3},{2,0},{3,1},{4,6},{5,7},{6,4},{7,5},{8,10},{9,11},{10,... | collective-permute-start | bytes 393224 | tf_op jit(solution)/shard_map/ppermute | solution.py:321
  347.8 20.5 %collective-permute-start.33 = (bf16[256,512]{1,0:T(8,128)(2,1)S(1)}, bf16[256,512]{1,0:T(8,128)(2,1)S(1)}, u32[]{:S(2)}, u32[]{:S(2)}) collective-permute-start(bf16[256,512]{1,0:T(8,128)(2,1)S(1)} %copy-done.58), channel_id=1, source_target_pairs={{0,1},{1,0},{2,3},{3,2},{4,5},{5,4},{6,7},{7,6},{8,9},{9,8},{10,11... | collective-permute-start | bytes 786440 | tf_op jit(solution)/shard_map/ppermute | solution.py:321
  368.2 36.9 %collective-permute-start.67 = (bf16[256,2048]{1,0:T(8,128)(2,1)}, bf16[256,2048]{1,0:T(8,128)(2,1)}, u32[]{:S(2)}, u32[]{:S(2)}) collective-permute-start(bf16[256,2048]{1,0:T(8,128)(2,1)} %convolution_convert_fusion.2), channel_id=1, source_target_pairs={{0,1},{1,0},{2,3},{3,2},{4,5},{5,4},{6,7},{7,6},{8,9},{9,8},{10,11... | collective-permute-start | bytes 3145736 | tf_op jit(solution)/shard_map/ppermute | solution.py:321
  397.2 17.8 %collective-permute-start.81 = (bf16[1024,512]{1,0:T(8,128)(2,1)}, bf16[1024,512]{1,0:T(8,128)(2,1)S(1)}, u32[]{:S(2)}, u32[]{:S(2)}) collective-permute-start(bf16[1024,512]{1,0:T(8,128)(2,1)} %convolution_convert_fusion.7), channel_id=1, source_target_pairs={{0,1},{1,0},{2,3},{3,2},{4,5},{5,4},{6,7},{7,6},{8,9},{9,8},{10,11... | collective-permute-start | bytes 3145736 | tf_op jit(solution)/shard_map/ppermute | solution.py:321
  401.6 15.8 %collective-permute-start.79 = (bf16[1024,512]{1,0:T(8,128)(2,1)S(1)}, bf16[1024,512]{1,0:T(8,128)(2,1)S(1)}, u32[]{:S(2)}, u32[]{:S(2)}) collective-permute-start(bf16[1024,512]{1,0:T(8,128)(2,1)S(1)} %copy-done.86), channel_id=1, source_target_pairs={{0,1},{1,0},{2,3},{3,2},{4,5},{5,4},{6,7},{7,6},{8,9},{9,8},{10,11... | collective-permute-start | bytes 3145736 | tf_op jit(solution)/shard_map/ppermute | solution.py:321
  408.7 22.1 %collective-permute-start.34 = (bf16[256,512]{1,0:T(8,128)(2,1)}, bf16[256,512]{1,0:T(8,128)(2,1)}, u32[]{:S(2)}, u32[]{:S(2)}) collective-permute-start(bf16[256,512]{1,0:T(8,128)(2,1)} %add_convert_fusion.22), channel_id=1, source_target_pairs={{0,24},{8,16},{16,8},{24,0},{1,25},{9,17},{17,9},{25,1},{2,26},{10... | collective-permute-start | bytes 786440 | tf_op jit(solution)/shard_map/ppermute | solution.py:321
  411.9 19.4 %collective-permute-start.32 = (bf16[256,512]{1,0:T(8,128)(2,1)}, bf16[256,512]{1,0:T(8,128)(2,1)}, u32[]{:S(2)}, u32[]{:S(2)}) collective-permute-start(bf16[256,512]{1,0:T(8,128)(2,1)} %add_convert_fusion.23), channel_id=1, source_target_pairs={{0,16},{8,24},{16,0},{24,8},{1,17},{9,25},{17,1},{25,9},{2,18},{10... | collective-permute-start | bytes 786440 | tf_op jit(solution)/shard_map/ppermute | solution.py:321
  415.1 17.8 %collective-permute-start.30 = (bf16[256,512]{1,0:T(8,128)(2,1)}, bf16[256,512]{1,0:T(8,128)(2,1)}, u32[]{:S(2)}, u32[]{:S(2)}) collective-permute-start(bf16[256,512]{1,0:T(8,128)(2,1)} %add_convert_fusion.24), channel_id=1, source_target_pairs={{0,8},{8,0},{16,24},{24,16},{1,9},{9,1},{17,25},{25,17},{2,10},{10... | collective-permute-start | bytes 786440 | tf_op jit(solution)/shard_map/ppermute | solution.py:321
  424.7 16.0 %collective-permute-start.48 = (bf16[256,384]{0,1:T(8,128)(2,1)}, bf16[256,384]{0,1:T(8,128)(2,1)S(1)}, u32[]{:S(2)}, u32[]{:S(2)}) collective-permute-start(bf16[256,384]{0,1:T(8,128)(2,1)} %bitcast.242), channel_id=1, source_target_pairs={{0,24},{8,16},{16,8},{24,0},{1,25},{9,17},{17,9},{25,1},{2,26},{10... | collective-permute-start | bytes 589832 | tf_op jit(solution)/shard_map/ppermute | solution.py:321
  431.3 87.1 %collective-permute-start.72 = (bf16[256,2048]{1,0:T(8,128)(2,1)}, bf16[256,2048]{1,0:T(8,128)(2,1)}, u32[]{:S(2)}, u32[]{:S(2)}) collective-permute-start(bf16[256,2048]{1,0:T(8,128)(2,1)} %add_convert_fusion.7), channel_id=1, source_target_pairs={{0,24},{8,16},{16,8},{24,0},{1,25},{9,17},{17,9},{25,1},{2,26},{10... | collective-permute-start | bytes 3145736 | tf_op jit(solution)/shard_map/ppermute | solution.py:321
  439.2 80.9 %collective-permute-start.70 = (bf16[256,2048]{1,0:T(8,128)(2,1)}, bf16[256,2048]{1,0:T(8,128)(2,1)}, u32[]{:S(2)}, u32[]{:S(2)}) collective-permute-start(bf16[256,2048]{1,0:T(8,128)(2,1)} %add_convert_fusion.8), channel_id=1, source_target_pairs={{0,16},{8,24},{16,0},{24,8},{1,17},{9,25},{17,1},{25,9},{2,18},{10... | collective-permute-start | bytes 3145736 | tf_op jit(solution)/shard_map/ppermute | solution.py:321
  440.7 21.9 %collective-permute-start.26 = (bf16[5,12,640]{2,1,0:T(8,128)(2,1)S(1)}, bf16[5,12,640]{2,1,0:T(8,128)(2,1)S(1)}, u32[]{:S(2)}, u32[]{:S(2)}) collective-permute-start(bf16[5,12,640]{2,1,0:T(8,128)(2,1)S(1)} %add_convert_fusion.28), channel_id=1, source_target_pairs={{0,24},{8,16},{16,8},{24,0},{1,25},{9,17},{17,9},{25,1},{2,26},{10... | collective-permute-start | bytes 230408 | tf_op jit(solution)/shard_map/ppermute | solution.py:321
  442.4 43.7 %collective-permute-start.25 = (bf16[5,12,640]{2,1,0:T(8,128)(2,1)S(1)}, bf16[5,12,640]{2,1,0:T(8,128)(2,1)S(1)}, u32[]{:S(2)}, u32[]{:S(2)}) collective-permute-start(bf16[5,12,640]{2,1,0:T(8,128)(2,1)S(1)} %add_convert_fusion.28), channel_id=1, source_target_pairs={{0,16},{8,24},{16,0},{24,8},{1,17},{9,25},{17,1},{25,9},{2,18},{10... | collective-permute-start | bytes 230408 | tf_op jit(solution)/shard_map/ppermute | solution.py:321
  442.8 43.6 %collective-permute-start.24 = (bf16[5,12,640]{2,1,0:T(8,128)(2,1)S(1)}, bf16[5,12,640]{2,1,0:T(8,128)(2,1)S(1)}, u32[]{:S(2)}, u32[]{:S(2)}) collective-permute-start(bf16[5,12,640]{2,1,0:T(8,128)(2,1)S(1)} %add_convert_fusion.28), channel_id=1, source_target_pairs={{0,8},{8,0},{16,24},{24,16},{1,9},{9,1},{17,25},{25,17},{2,10},{10... | collective-permute-start | bytes 230408 | tf_op jit(solution)/shard_map/ppermute | solution.py:321
  462.6 59.1 %collective-permute-start.68 = (bf16[256,2048]{1,0:T(8,128)(2,1)}, bf16[256,2048]{1,0:T(8,128)(2,1)}, u32[]{:S(2)}, u32[]{:S(2)}) collective-permute-start(bf16[256,2048]{1,0:T(8,128)(2,1)} %add_convert_fusion.9), channel_id=1, source_target_pairs={{0,8},{8,0},{16,24},{24,16},{1,9},{9,1},{17,25},{25,17},{2,10},{10... | collective-permute-start | bytes 3145736 | tf_op jit(solution)/shard_map/ppermute | solution.py:321
  487.2 16.8 %collective-permute-start.27 = (bf16[240,512]{1,0:T(8,128)(2,1)S(1)}, bf16[240,512]{1,0:T(8,128)(2,1)S(1)}, u32[]{:S(2)}, u32[]{:S(2)}) collective-permute-start(bf16[240,512]{1,0:T(8,128)(2,1)S(1)} %slice.322), channel_id=1, source_target_pairs={{0,1},{1,0},{2,3},{3,2},{4,5},{5,4},{6,7},{7,6},{8,9},{9,8},{10,11... | collective-permute-start | bytes 737288 | tf_op jit(solution)/shard_map/ppermute | solution.py:321
  517.0 27.1 %collective-permute-start.84 = (bf16[1024,512]{1,0:T(8,128)(2,1)}, bf16[1024,512]{1,0:T(8,128)(2,1)S(1)}, u32[]{:S(2)}, u32[]{:S(2)}) collective-permute-start(bf16[1024,512]{1,0:T(8,128)(2,1)} %add_convert_fusion.2), channel_id=1, source_target_pairs={{0,24},{8,16},{16,8},{24,0},{1,25},{9,17},{17,9},{25,1},{2,26},{10... | collective-permute-start | bytes 3145736 | tf_op jit(solution)/shard_map/ppermute | solution.py:321
  518.5 47.7 %collective-permute-start.82 = (bf16[1024,512]{1,0:T(8,128)(2,1)}, bf16[1024,512]{1,0:T(8,128)(2,1)S(1)}, u32[]{:S(2)}, u32[]{:S(2)}) collective-permute-start(bf16[1024,512]{1,0:T(8,128)(2,1)} %add_convert_fusion.3), channel_id=1, source_target_pairs={{0,16},{8,24},{16,0},{24,8},{1,17},{9,25},{17,1},{25,9},{2,18},{10... | collective-permute-start | bytes 3145736 | tf_op jit(solution)/shard_map/ppermute | solution.py:321
  520.1 46.1 %collective-permute-start.80 = (bf16[1024,512]{1,0:T(8,128)(2,1)}, bf16[1024,512]{1,0:T(8,128)(2,1)S(1)}, u32[]{:S(2)}, u32[]{:S(2)}) collective-permute-start(bf16[1024,512]{1,0:T(8,128)(2,1)} %add_convert_fusion.4), channel_id=1, source_target_pairs={{0,8},{8,0},{16,24},{24,16},{1,9},{9,1},{17,25},{25,17},{2,10},{10... | collective-permute-start | bytes 3145736 | tf_op jit(solution)/shard_map/ppermute | solution.py:321
  524.5 42.4 %collective-permute-start.73 = (bf16[128,2048]{1,0:T(8,128)(2,1)S(1)}, bf16[128,2048]{1,0:T(8,128)(2,1)S(1)}, u32[]{:S(2)}, u32[]{:S(2)}) collective-permute-start(bf16[128,2048]{1,0:T(8,128)(2,1)S(1)} %constant_dynamic-slice_fusion.3), channel_id=1, source_target_pairs={{0,2},{1,3},{2,0},{3,1},{4,6},{5,7},{6,4},{7,5},{8,10},{9,11},{10,... | collective-permute-start | bytes 1572872 | tf_op jit(solution)/shard_map/ppermute | solution.py:321
  524.9 112.1 %collective-permute-start.39 = (bf16[256,512]{1,0:T(8,128)(2,1)}, bf16[256,512]{1,0:T(8,128)(2,1)}, u32[]{:S(2)}, u32[]{:S(2)}) collective-permute-start(bf16[256,512]{1,0:T(8,128)(2,1)} %maximum_select_fusion.14), channel_id=1, source_target_pairs={{0,1},{1,0},{2,3},{3,2},{4,5},{5,4},{6,7},{7,6},{8,9},{9,8},{10,11... | collective-permute-start | bytes 786440 | tf_op jit(solution)/shard_map/ppermute | solution.py:321
  544.1 27.0 %collective-permute-start.50 = (bf16[64,4,384]{0,2,1:T(8,128)(2,1)S(1)}, bf16[64,4,384]{0,2,1:T(8,128)(2,1)S(1)}, u32[]{:S(2)}, u32[]{:S(2)}) collective-permute-start(bf16[64,4,384]{0,2,1:T(8,128)(2,1)S(1)} %constant_dynamic-slice_fusion.7), channel_id=1, source_target_pairs={{0,4},{1,5},{2,6},{3,7},{4,0},{5,1},{6,2},{7,3},{8,12},{9,13},{10,... | collective-permute-start | bytes 589832 | tf_op jit(solution)/shard_map/ppermute | solution.py:321
  569.4 25.1 %collective-permute-start.85 = (bf16[512,512]{1,0:T(8,128)(2,1)}, bf16[512,512]{1,0:T(8,128)(2,1)}, u32[]{:S(2)}, u32[]{:S(2)}) collective-permute-start(bf16[512,512]{1,0:T(8,128)(2,1)} %constant_dynamic-slice_fusion.1), channel_id=1, source_target_pairs={{0,2},{1,3},{2,0},{3,1},{4,6},{5,7},{6,4},{7,5},{8,10},{9,11},{10,... | collective-permute-start | bytes 1572872 | tf_op jit(solution)/shard_map/ppermute | solution.py:321
  571.4 39.4 %collective-permute-start.51 = (bf16[64,4,384]{0,2,1:T(8,128)(2,1)S(1)}, bf16[64,4,384]{0,2,1:T(8,128)(2,1)}, u32[]{:S(2)}, u32[]{:S(2)}) collective-permute-start(bf16[64,4,384]{0,2,1:T(8,128)(2,1)S(1)} %add_convert_fusion.15), channel_id=1, source_target_pairs={{0,4},{1,5},{2,6},{3,7},{4,0},{5,1},{6,2},{7,3},{8,12},{9,13},{10,... | collective-permute-start | bytes 589832 | tf_op jit(solution)/shard_map/ppermute | solution.py:321
  583.8 32.5 %collective-permute-start.75 = (bf16[64,2048]{1,0:T(8,128)(2,1)S(1)}, bf16[64,2048]{1,0:T(8,128)(2,1)S(1)}, u32[]{:S(2)}, u32[]{:S(2)}) collective-permute-start(bf16[64,2048]{1,0:T(8,128)(2,1)S(1)} %add_convert_fusion.18), channel_id=1, source_target_pairs={{0,4},{1,5},{2,6},{3,7},{4,0},{5,1},{6,2},{7,3},{8,12},{9,13},{10,... | collective-permute-start | bytes 786440 | tf_op jit(solution)/shard_map/ppermute | solution.py:321
  595.8 26.1 %collective-permute-start.86 = (bf16[256,512]{1,0:T(8,128)(2,1)S(1)}, bf16[256,512]{1,0:T(8,128)(2,1)S(1)}, u32[]{:S(2)}, u32[]{:S(2)}) collective-permute-start(bf16[256,512]{1,0:T(8,128)(2,1)S(1)} %constant_dynamic-slice_fusion), channel_id=1, source_target_pairs={{0,4},{1,5},{2,6},{3,7},{4,0},{5,1},{6,2},{7,3},{8,12},{9,13},{10,... | collective-permute-start | bytes 786440 | tf_op jit(solution)/shard_map/ppermute | solution.py:321
  612.3 23.6 %collective-permute-start.52 = (bf16[128,4,384]{0,2,1:T(8,128)(2,1)S(1)}, bf16[128,4,384]{0,2,1:T(8,128)(2,1)S(1)}, u32[]{:S(2)}, u32[]{:S(2)}) collective-permute-start(bf16[128,4,384]{0,2,1:T(8,128)(2,1)S(1)} %maximum_select_fusion.13), channel_id=1, source_target_pairs={{0,2},{1,3},{2,0},{3,1},{4,6},{5,7},{6,4},{7,5},{8,10},{9,11},{10,... | collective-permute-start | bytes 1179656 | tf_op jit(solution)/shard_map/ppermute | solution.py:321
  616.5 30.8 %collective-permute-start.76 = (bf16[128,2048]{1,0:T(8,128)(2,1)S(1)}, bf16[128,2048]{1,0:T(8,128)(2,1)}, u32[]{:S(2)}, u32[]{:S(2)}) collective-permute-start(bf16[128,2048]{1,0:T(8,128)(2,1)S(1)} %maximum_select_fusion.10), channel_id=1, source_target_pairs={{0,2},{1,3},{2,0},{3,1},{4,6},{5,7},{6,4},{7,5},{8,10},{9,11},{10,... | collective-permute-start | bytes 1572872 | tf_op jit(solution)/shard_map/ppermute | solution.py:321
  622.6 18.0 %collective-permute-start.87 = (bf16[256,512]{1,0:T(8,128)(2,1)}, bf16[256,512]{1,0:T(8,128)(2,1)}, u32[]{:S(2)}, u32[]{:S(2)}) collective-permute-start(bf16[256,512]{1,0:T(8,128)(2,1)} %add_convert_fusion.17), channel_id=1, source_target_pairs={{0,4},{1,5},{2,6},{3,7},{4,0},{5,1},{6,2},{7,3},{8,12},{9,13},{10,... | collective-permute-start | bytes 786440 | tf_op jit(solution)/shard_map/ppermute | solution.py:321
  642.8 15.6 %collective-permute-start.88 = (bf16[512,512]{1,0:T(8,128)(2,1)}, bf16[512,512]{1,0:T(8,128)(2,1)}, u32[]{:S(2)}, u32[]{:S(2)}) collective-permute-start(bf16[512,512]{1,0:T(8,128)(2,1)} %maximum_select_fusion.11), channel_id=1, source_target_pairs={{0,2},{1,3},{2,0},{3,1},{4,6},{5,7},{6,4},{7,5},{8,10},{9,11},{10,... | collective-permute-start | bytes 1572872 | tf_op jit(solution)/shard_map/ppermute | solution.py:321
  649.2 114.5 %collective-permute-start.77 = (bf16[256,2048]{1,0:T(8,128)(2,1)S(1)}, bf16[256,2048]{1,0:T(8,128)(2,1)}, u32[]{:S(2)}, u32[]{:S(2)}) collective-permute-start(bf16[256,2048]{1,0:T(8,128)(2,1)S(1)} %maximum_select_fusion.4), channel_id=1, source_target_pairs={{0,1},{1,0},{2,3},{3,2},{4,5},{5,4},{6,7},{7,6},{8,9},{9,8},{10,11... | collective-permute-start | bytes 3145736 | tf_op jit(solution)/shard_map/ppermute | solution.py:321
  661.2 106.8 %collective-permute-start.89 = (bf16[1024,512]{1,0:T(8,128)(2,1)}, bf16[1024,512]{1,0:T(8,128)(2,1)}, u32[]{:S(2)}, u32[]{:S(2)}) collective-permute-start(bf16[1024,512]{1,0:T(8,128)(2,1)} %maximum_select_fusion.5), channel_id=1, source_target_pairs={{0,1},{1,0},{2,3},{3,2},{4,5},{5,4},{6,7},{7,6},{8,9},{9,8},{10,11... | collective-permute-start | bytes 3145736 | tf_op jit(solution)/shard_map/ppermute | solution.py:321
  (134 other events, 1371.8 us)

commit v2 on v1

v2 whole, which is shorter than its diff:
```python
from functools import partial

import jax
import jax.numpy as jnp
from jax import lax
from jax.experimental import pallas as pl
from jax.experimental.pallas import tpu as pltpu
from jax.sharding import PartitionSpec as P

HEADS = 16
PIX = 4
HEAD_DIM = 64
ORDER = (0, 2, 1, 3)
BLOCKS = tuple((k, 0) for k in range(4)) + tuple((k, 1) for k in ORDER)

f32, bf16 = jnp.float32, jnp.bfloat16
highest = lax.Precision.HIGHEST
epsilon = 1e-05
NT = (((1,), (1,)), ((), ()))
TN = (((0,), (0,)), ((), ()))


def head_weights(pixels, key_ref, head):
    scores = key_ref[PIX, :, head : head + 1]
    for c in range(PIX):
        scores = scores + pixels[c] * key_ref[c, :, head : head + 1]
    soft = jnp.exp(scores - jnp.max(scores, axis=0, keepdims=True))
    return soft * (1.0 / jnp.sum(soft, axis=0, keepdims=True))


def slot_spans(member, own):
    return [pl.ds(pl.multiple_of((member[0] ^ k) * own, own), own) for k in ORDER]


def weighted_pixels(soft, pixels):
    return jnp.concatenate(
        [(soft * pixels[c]).astype(bf16) for c in range(PIX)] + [soft.astype(bf16)], axis=0
    )


def front_kernel(
    member,
    pixel_ref,
    key_ref,
    value_ref,
    out_ref,
    lead_ref,
    gain_ref,
    wq_ref,
    wk_ref,
    wv_ref,
    hidden_ref,
    qkv_ref,
    resid_ref,
    att_ref,
    att_scratch,
):
    pixels = [pixel_ref[c].astype(f32) for c in range(PIX)]
    for head in range(HEADS):
        soft = head_weights(pixels, key_ref, head)
        span = slice(head * HEAD_DIM, (head + 1) * HEAD_DIM)
        att_scratch[span, :] = jnp.dot(
            value_ref[span, :], weighted_pixels(soft, pixels), preferred_element_type=f32
        ).astype(bf16)
    att = att_scratch[...]
    resid = lax.dot_general(att, out_ref[...], TN, preferred_element_type=f32) + lead_ref[...]
    centered = resid - jnp.mean(resid, axis=1, keepdims=True)
    inverse = lax.rsqrt(jnp.mean(centered * centered, axis=1, keepdims=True) + epsilon)
    hidden = (centered * inverse * gain_ref[...]).astype(bf16)
    own = wq_ref.shape[1]
    hidden_ref[...] = hidden.T
    for t, weight in enumerate((wq_ref, wk_ref, wv_ref)):
        qkv_ref[:, t * own : (t + 1) * own] = jnp.dot(
            hidden, weight[...], preferred_element_type=f32
        ).astype(bf16)

    @pl.when(pl.program_id(0) == member[0])
    def _():
        resid_ref[...] = resid
        att_ref[...] = att


def front(member, pixels, key_rows, values_t, agg_out, lead_row, gain, attn_qkv, groups):
    width = agg_out.shape[0]
    own = width // groups
    channels, seq = pixels.shape[1:]
    rows = seq // groups
    spec = pltpu.PrefetchScalarGridSpec(
        num_scalar_prefetch=1,
        grid=(groups,),
        in_specs=[
            pl.BlockSpec((PIX, channels, rows), lambda i, m: (0, 0, i)),
            pl.BlockSpec(key_rows.shape, lambda i, m: (0, 0, 0)),
            pl.BlockSpec(values_t.shape, lambda i, m: (0, 0)),
            pl.BlockSpec(agg_out.shape, lambda i, m: (0, 0)),
            pl.BlockSpec((1, width), lambda i, m: (0, 0)),
            pl.BlockSpec((1, width), lambda i, m: (0, 0)),
            pl.BlockSpec((width, own), lambda i, m: (0, m[0])),
            pl.BlockSpec((width, own), lambda i, m: (0, groups + m[0])),
            pl.BlockSpec((width, own), lambda i, m: (0, 2 * groups + m[0])),
        ],
        out_specs=[
            pl.BlockSpec((width, rows), lambda i, m: (0, i)),
            pl.BlockSpec((rows, 3 * own), lambda i, m: (i, 0)),
            pl.BlockSpec((rows, width), lambda i, m: (0, 0)),
            pl.BlockSpec((width, rows), lambda i, m: (0, 0)),
        ],
        scratch_shapes=[pltpu.VMEM((width, rows), bf16)],
    )
    return pl.pallas_call(
        front_kernel,
        grid_spec=spec,
        out_shape=[
            jax.ShapeDtypeStruct((width, seq), bf16),
            jax.ShapeDtypeStruct((seq, 3 * own), bf16),
            jax.ShapeDtypeStruct((rows, width), f32),
            jax.ShapeDtypeStruct((width, rows), bf16),
        ],
        cost_estimate=pl.CostEstimate(
            flops=2 * seq * width * (width + 3 * own), bytes_accessed=16 << 20, transcendentals=seq * channels * HEADS
        ),
        name="front",
    )(member, pixels, key_rows, values_t, agg_out, lead_row, gain, attn_qkv, attn_qkv, attn_qkv)


def attend_kernel(member, q_ref, k_ref, v_ref, mixed_ref, lse_ref):
    rows = q_ref.shape[0]
    lane = lax.broadcasted_iota(jnp.int32, (1, 2 * HEAD_DIM), 1)
    queries = q_ref[...] * jnp.asarray(0.125, bf16)
    mixed = jnp.zeros((rows, 2 * HEAD_DIM), f32)
    for part in range(2):
        keep = (lane // HEAD_DIM) == part
        query = jnp.where(keep, queries, jnp.zeros_like(queries))
        scores = lax.dot_general(query, k_ref[...], NT, preferred_element_type=f32)
        top = jnp.max(scores, axis=1, keepdims=True)
        soft = jnp.exp(scores - top)
        total = jnp.sum(soft, axis=1, keepdims=True)
        out = jnp.dot(soft.astype(bf16), v_ref[...], preferred_element_type=f32)
        mixed = jnp.where(keep, out * (1.0 / total), mixed)
        lse = jnp.broadcast_to(top + jnp.log(total), (rows, 2 * HEAD_DIM))
        lse_ref[0, part : part + 1, :] = lse.T[0:1, :]
    mixed_ref[...] = mixed.astype(bf16)


def attend(member, qkv, slot, rows, block):
    seq = qkv.shape[0]
    pair = 2 * HEAD_DIM
    pairs = qkv.shape[1] // (3 * pair)
    steps = rows // block
    spec = pltpu.PrefetchScalarGridSpec(
        num_scalar_prefetch=1,
        grid=(pairs, steps),
        in_specs=[
            pl.BlockSpec((block, pair), lambda p, i, m: ((m[0] ^ slot) * steps + i, p)),
            pl.BlockSpec((seq, pair), lambda p, i, m: (0, pairs + p)),
            pl.BlockSpec((seq, pair), lambda p, i, m: (0, 2 * pairs + p)),
        ],
        out_specs=[
            pl.BlockSpec((block, pair), lambda p, i, m: (i, p)),
            pl.BlockSpec((1, 2, block), lambda p, i, m: (p, 0, i)),
        ],
    )
    return pl.pallas_call(
        attend_kernel,
        grid_spec=spec,
        out_shape=[
            jax.ShapeDtypeStruct((rows, pairs * pair), bf16),
            jax.ShapeDtypeStruct((pairs, 2, rows), f32),
        ],
        cost_estimate=pl.CostEstimate(
            flops=16 * rows * seq * pair * pairs, bytes_accessed=3 << 20, transcendentals=2 * rows * seq * pairs
        ),
        name="attend",
    )(member, qkv, qkv, qkv)


def attend_back_kernel(member, q_ref, k_ref, v_ref, g_ref, *refs, chunk, groups):
    mixed_refs, lse_refs = refs[:groups], refs[groups : 2 * groups]
    out_ref, dk_acc, dv_acc, kt = refs[2 * groups :]
    i = pl.program_id(0)
    slot = i ^ member[0]
    mixed, lse_rows = mixed_refs[0][...], lse_refs[0][0]
    for k in range(1, groups):
        mixed = jnp.where(slot == k, mixed_refs[k][...], mixed)
        lse_rows = jnp.where(slot == k, lse_refs[k][0], lse_rows)
    block = q_ref.shape[0]
    seq = k_ref.shape[0]
    pair = 2 * HEAD_DIM
    lane = lax.broadcasted_iota(jnp.int32, (1, pair), 1)
    side = lax.broadcasted_iota(jnp.int32, (pair, 1), 0)

    @pl.when(i == 0)
    def _():
        dk_acc[...] = jnp.zeros_like(dk_acc)
        dv_acc[...] = jnp.zeros_like(dv_acc)
        kt[...] = k_ref[...].T

    queries = q_ref[...] * jnp.asarray(0.125, bf16)
    grads = g_ref[...]
    product = (grads.astype(f32) * mixed.astype(f32)).T
    grad_query = jnp.zeros((pair, block), f32)
    for part in range(2):
        keep = (lane // HEAD_DIM) == part
        query = jnp.where(keep, queries, jnp.zeros_like(queries))
        grad = jnp.where(keep, grads, jnp.zeros_like(grads))
        delta = jnp.sum(product[part * HEAD_DIM : (part + 1) * HEAD_DIM], axis=0, keepdims=True)
        lse = lse_rows[part : part + 1, :]
        total = jnp.zeros((pair, block), f32)
        for at in range(0, seq, chunk):
            span = pl.ds(at, chunk)
            scores = lax.dot_general(k_ref[span, :], query, NT, preferred_element_type=f32)
            soft = jnp.exp(scores - lse)
            through = lax.dot_general(v_ref[span, :], grad, NT, preferred_element_type=f32)
            grad_scores = (soft * (through - delta)).astype(bf16)
            dv_acc[span, :] += jnp.dot(soft.astype(bf16), grad, preferred_element_type=f32)
            dk_acc[span, :] += jnp.dot(grad_scores, query, preferred_element_type=f32)
            total += jnp.dot(kt[:, span], grad_scores, preferred_element_type=f32)
        grad_query = jnp.where((side // HEAD_DIM) == part, total, grad_query)
    out_ref[pl.ds(pl.multiple_of(i * block, block), block), 0:pair] = (grad_query.T * 0.125).astype(bf16)

    @pl.when(i == pl.num_programs(0) - 1)
    def _():
        out_ref[:, pair : 2 * pair] = dk_acc[...].astype(bf16)
        out_ref[:, 2 * pair : 3 * pair] = dv_acc[...].astype(bf16)


def attend_back(member, qkv, grads, mixed, lse, which, chunk):
    seq = qkv.shape[0]
    groups = len(mixed)
    rows = seq // groups
    pair = 2 * HEAD_DIM
    pairs = qkv.shape[1] // (3 * pair)
    spec = pltpu.PrefetchScalarGridSpec(
        num_scalar_prefetch=1,
        grid=(groups,),
        in_specs=[
            pl.BlockSpec((rows, pair), lambda i, m: (i, which)),
            pl.BlockSpec((seq, pair), lambda i, m: (0, pairs + which)),
            pl.BlockSpec((seq, pair), lambda i, m: (0, 2 * pairs + which)),
            pl.BlockSpec((rows, pair), lambda i, m: (i, which)),
        ]
        + [pl.BlockSpec((rows, pair), lambda i, m: (0, which))] * groups
        + [pl.BlockSpec((1, 2, rows), lambda i, m: (which, 0, 0))] * groups,
        out_specs=pl.BlockSpec((seq, 3 * pair), lambda i, m: (0, 0)),
        scratch_shapes=[pltpu.VMEM((seq, pair), f32), pltpu.VMEM((seq, pair), f32), pltpu.VMEM((pair, seq), bf16)],
    )
    return pl.pallas_call(
        partial(attend_back_kernel, chunk=min(chunk, seq), groups=groups),
        grid_spec=spec,
        out_shape=jax.ShapeDtypeStruct((seq, 3 * pair), bf16),
        cost_estimate=pl.CostEstimate(
            flops=40 * seq * seq * pair, bytes_accessed=5 << 20, transcendentals=2 * seq * seq
        ),
        name="attend_back",
    )(member, qkv, qkv, qkv, grads, *mixed, *lse)


def put_tail(tail, values, span):
    groups = len(ORDER)
    channels = values.shape[0] // ((PIX + 1) * groups)
    stride = tail.shape[0] // groups
    for at, k in enumerate(ORDER):
        for c in range(PIX + 1):
            row, source = at * stride + c * channels, (c * groups + k) * channels
            tail[row : row + channels, span] = values[source : source + channels]


def aggregate_back_kernel(
    member, core, pixel_ref, key_ref, value_ref, grad_ref, small_ref, field_ref, keep_ref, send_ref, tail
):
    count, rows = pixel_ref.shape[1:]
    pair = 2 * HEAD_DIM
    pixels = [pixel_ref[c].astype(f32) for c in range(PIX)]
    lane = lax.broadcasted_iota(jnp.int32, (1, pair), 1)
    side = lax.broadcasted_iota(jnp.int32, (pair, 1), 0)
    field = [jnp.zeros((count, rows), f32) for _ in range(PIX)]
    keys = [jnp.zeros((count, pair), f32) for _ in range(PIX + 1)]
    for which in range(HEADS // 2):
        span = slice(which * pair, (which + 1) * pair)
        values, grads = value_ref[:, span], grad_ref[span, :]
        total = jnp.zeros(((PIX + 1) * count, pair), f32)
        for part in range(2):
            head = which * 2 + part
            grad = jnp.where((side // HEAD_DIM) == part, grads, jnp.zeros_like(grads))
            through = jnp.dot(values, grad, preferred_element_type=f32)
            kinds = [through[c * count : (c + 1) * count] for c in range(PIX + 1)]
            soft = head_weights(pixels, key_ref, head)
            grad_soft = kinds[PIX]
            for c in range(PIX):
                grad_soft = grad_soft + pixels[c] * kinds[c]
            weighed = soft * grad_soft
            grad_scores = weighed - soft * jnp.sum(weighed, axis=0, keepdims=True)
            for c in range(PIX):
                field[c] = field[c] + soft * kinds[c] + grad_scores * key_ref[c, :, head : head + 1]
                keys[c] = jnp.where(lane == head, jnp.sum(grad_scores * pixels[c], axis=1, keepdims=True), keys[c])
            keys[PIX] = jnp.where(lane == head, jnp.sum(grad_scores, axis=1, keepdims=True), keys[PIX])
            total = total + lax.dot_general(weighted_pixels(soft, pixels), grad, NT, preferred_element_type=f32)
        put_tail(tail, total, span)
    for c in range(PIX):
        field_ref[c] = field[c].astype(bf16)
    width = value_ref.shape[1]
    put_tail(tail, jnp.concatenate(keys, axis=0), slice(width, width + pair))
    stride = tail.shape[0] // len(ORDER)
    free = small_ref.shape[0] // len(ORDER)
    for at in range(len(ORDER)):
        end = (at + 1) * stride
        tail[end - free : end, :width] = small_ref[at * free : (at + 1) * free, :]
        tail[end - free : end, width:] = jnp.zeros((free, pair), f32)
    half = width // 2
    for ref, which in ((keep_ref, core[0]), (send_ref, 1 - core[0])):
        ref[:, :half] = tail[:, pl.ds(pl.multiple_of(which * half, half), half)].astype(bf16)
        ref[:, half:] = tail[:, width:].astype(bf16)


def aggregate_back(member, core, pixels, key_rows, values, grads, small, groups):
    count, seq = pixels.shape[1:]
    rows = seq // groups
    width = values.shape[1]
    free = small.shape[0] // groups
    deep = (PIX + 1) * count + small.shape[0]
    wide = width // 2 + 2 * HEAD_DIM

    def whole(*shape):
        return pl.BlockSpec(shape, lambda i, m, c: (0,) * len(shape))

    spec = pltpu.PrefetchScalarGridSpec(
        num_scalar_prefetch=2,
        grid=(1,),
        in_specs=[
            pl.BlockSpec((PIX, count, rows), lambda i, m, c: (0, 0, m[0])),
            whole(*key_rows.shape),
            whole(*values.shape),
            whole(*grads.shape),
            whole(*small.shape),
        ],
        out_specs=[whole(PIX, count, rows), whole(deep, wide), whole(deep, wide)],
        scratch_shapes=[pltpu.VMEM((deep, width + 2 * HEAD_DIM), f32)],
    )
    return pl.pallas_call(
        aggregate_back_kernel,
        grid_spec=spec,
        out_shape=[
            jax.ShapeDtypeStruct((PIX, count, rows), bf16),
            jax.ShapeDtypeStruct((deep, wide), bf16),
            jax.ShapeDtypeStruct((deep, wide), bf16),
        ],
        cost_estimate=pl.CostEstimate(
            flops=16 * (PIX + 1) * count * rows * width, bytes_accessed=3 << 20, transcendentals=rows * count * HEADS
        ),
        name="aggregate_back",
    )(member, core, pixels, key_rows, values, grads, small)


def middle_kernel(
    member, core, mixed0, mixed1, mixed2, mixed3, wo_ref, resid_ref, gain_ref, w1_ref, b1_ref, w2_ref, ga_ref, g_ref,
    osend_ref, okeep_ref, isend_ref, ikeep_ref, bias_ref, out_ref, gres_ref, gm_ref, ggain_ref,
    normed, hidden, inverse, acc_out, acc_grad, hidden_t, mixed_t,
):
    j = pl.program_id(0)
    steps = pl.num_programs(0) - 1
    parts = (mixed0, mixed1, mixed2, mixed3)
    rows, own = mixed0.shape
    half = g_ref.shape[1] // 2

    def columns(ref, which):
        return ref[:, pl.ds(pl.multiple_of(which * half, half), half)]

    def owner(slot):
        return pl.ds(pl.multiple_of((member[0] ^ slot) * own, own), own)

    @pl.when(j == 0)
    def _():
        resid = resid_ref[...]
        for slot, part in enumerate(parts):
            resid = resid + jnp.dot(part[...], wo_ref[owner(slot), :], preferred_element_type=f32)
        centered = resid - jnp.mean(resid, axis=1, keepdims=True)
        scale = lax.rsqrt(jnp.mean(centered * centered, axis=1, keepdims=True) + epsilon)
        plain = centered * scale
        normed[...] = plain
        inverse[...] = jnp.broadcast_to(scale, inverse.shape)
        hidden[...] = (plain * gain_ref[...]).astype(bf16)
        acc_out[...] = resid
        acc_grad[...] = jnp.zeros_like(acc_grad)
        piece = own // 2
        for at, (slot, side) in enumerate(BLOCKS):
            start = pl.multiple_of((member[0] ^ slot) * own + side * piece, piece)
            hidden_t[at * piece : (at + 1) * piece, :] = hidden[:, pl.ds(start, piece)].T
            mixed_t[at * piece : (at + 1) * piece, :] = parts[slot][:, side * piece : (side + 1) * piece].T

    @pl.when(j < steps)
    def _():
        inner = jnp.dot(hidden[...], w1_ref[...], preferred_element_type=f32) + b1_ref[...]
        below = 0.5 + 0.5 * lax.erf(inner * 0.7071067811865476)
        act = (inner * below).astype(bf16)
        slope = below + inner * (jnp.exp(-0.5 * inner * inner) * 0.3989422804014327)
        gu = (slope * ga_ref[...].astype(f32)).astype(bf16)
        bias_ref[...] = jnp.sum(gu.astype(f32), axis=0, keepdims=True)
        acc_out[...] += jnp.dot(act, w2_ref[...], preferred_element_type=f32)
        acc_grad[...] += lax.dot_general(gu, w1_ref[...], NT, preferred_element_type=f32)
        act_t = act.T
        osend_ref[...] = jnp.dot(act_t, columns(g_ref, 1 - core[0]), preferred_element_type=f32).astype(bf16)
        okeep_ref[...] = jnp.dot(act_t, columns(g_ref, core[0]), preferred_element_type=f32).astype(bf16)
        grad_in = jnp.dot(hidden_t[...], gu, preferred_element_type=f32).astype(bf16)

        @pl.when(j < steps // 2)
        def _():
            isend_ref[...] = grad_in

        @pl.when(j >= steps // 2)
        def _():
            ikeep_ref[...] = grad_in

    @pl.when(j == steps)
    def _():
        out_ref[...] = acc_out[...].astype(bf16)
        grad, plain = acc_grad[...], normed[...]
        ggain_ref[...] = jnp.sum(grad * plain, axis=0, keepdims=True)
        grad = grad * gain_ref[...]
        first = jnp.mean(grad, axis=1, keepdims=True)
        second = jnp.mean(grad * plain, axis=1, keepdims=True)
        gres = g_ref[...].astype(f32) + inverse[:, :1] * (grad - first - plain * second)
        gres_ref[...] = gres
        gb = gres.astype(bf16)
        for p in range(len(parts)):
            gm_ref[p] = lax.dot_general(gb, wo_ref[p * own : (p + 1) * own, :], NT, preferred_element_type=f32).astype(
                bf16
            )
        both = jnp.dot(mixed_t[...], gb, preferred_element_type=f32).astype(bf16)
        for which in range(2):
            mine = both[:, which * half : (which + 1) * half]

            @pl.when(core[0] == which)
            def _():
                ikeep_ref[...] = mine

            @pl.when(core[0] != which)
            def _():
                isend_ref[...] = mine


def middle(member, core, mixed, attn_out, resid, gain, mlp_in, bias, mlp_out, grad_act, grad_out):
    rows, width = resid.shape
    inner = mlp_in.shape[1]
    groups = len(mixed)
    own = width // groups
    block = inner // (2 * groups)
    steps = 2 * groups
    half = width // 2
    assert half == block

    def natural(j, m, c):
        j = jnp.minimum(j, steps - 1)
        return ((j // groups) ^ (1 - c[0])) * groups + j % groups

    def place(j, m, c):
        n = natural(j, m, c)
        slot = (n // 2) ^ m[0]
        return jnp.where(n % 2 == 0, slot, 4 + (slot % 2) * 2 + slot // 2)

    def whole(*shape):
        return pl.BlockSpec(shape, lambda j, m, c: (0,) * len(shape))

    def shape(*dims, kind=bf16):
        return jax.ShapeDtypeStruct(dims, kind)

    spec = pltpu.PrefetchScalarGridSpec(
        num_scalar_prefetch=2,
        grid=(steps + 1,),
        in_specs=[whole(rows, own)] * groups
        + [
            whole(width, width),
            whole(rows, width),
            whole(1, width),
            pl.BlockSpec((width, block), lambda j, m, c: (0, natural(j, m, c))),
            pl.BlockSpec((1, block), lambda j, m, c: (0, natural(j, m, c))),
            pl.BlockSpec((block, width), lambda j, m, c: (natural(j, m, c), 0)),
            pl.BlockSpec((rows, block), lambda j, m, c: (0, natural(j, m, c))),
            whole(rows, width),
        ],
        out_specs=[
            pl.BlockSpec((block, half), lambda j, m, c: (place(j, m, c), 0)),
            pl.BlockSpec((block, half), lambda j, m, c: (place(j, m, c), 0)),
            pl.BlockSpec((width, block), lambda j, m, c: (0, jnp.minimum(j, groups))),
            pl.BlockSpec((width, block), lambda j, m, c: (0, jnp.maximum(j - groups, 0))),
            pl.BlockSpec((1, block), lambda j, m, c: (0, natural(j, m, c))),
            whole(rows, width),
            whole(rows, width),
            whole(groups, rows, own),
            whole(1, width),
        ],
        scratch_shapes=[
            pltpu.VMEM((rows, width), f32),
            pltpu.VMEM((rows, width), bf16),
            pltpu.VMEM((rows, 128), f32),
            pltpu.VMEM((rows, width), f32),
            pltpu.VMEM((rows, width), f32),
            pltpu.VMEM((width, rows), bf16),
            pltpu.VMEM((width, rows), bf16),
        ],
    )
    side = inner // 2 + half
    return pl.pallas_call(
        middle_kernel,
        grid_spec=spec,
        out_shape=[
            shape(inner, half),
            shape(inner, half),
            shape(width, side),
            shape(width, side),
            shape(1, inner, kind=f32),
            shape(rows, width),
            shape(rows, width, kind=f32),
            shape(groups, rows, own),
            shape(1, width, kind=f32),
        ],
        cost_estimate=pl.CostEstimate(
            flops=2 * rows * width * (5 * inner + 3 * width), bytes_accessed=48 << 20, transcendentals=2 * rows * inner
        ),
        name="middle",
    )(member, core, *mixed, attn_out, resid, gain, mlp_in, bias, mlp_out, grad_act, grad_out)


def join_kernel(first_ref, second_ref, wq, wk, wv, resid_ref, gain_ref, gres_ref, out_ref, *refs):
    ga_ref, gatt_ref, ggain_ref, sum_ref, total = refs
    i = pl.program_id(0)
    pair = 2 * HEAD_DIM

    @pl.when(i == 0)
    def _():
        total[...] = jnp.zeros_like(total)

    grad = total[...]
    for t, weight in enumerate((wq, wk, wv)):
        span = slice(t * pair, (t + 1) * pair)
        left = jnp.concatenate([first_ref[:, span], second_ref[:, span]], axis=1)
        grad = grad + lax.dot_general(left, weight[...], NT, preferred_element_type=f32)
    total[...] = grad

    @pl.when(i == pl.num_programs(0) - 1)
    def _():
        resid = resid_ref[...]
        centered = resid - jnp.mean(resid, axis=1, keepdims=True)
        scale = lax.rsqrt(jnp.mean(centered * centered, axis=1, keepdims=True) + epsilon)
        plain = centered * scale
        grad = total[...]
        ggain_ref[...] = jnp.sum(grad * plain, axis=0, keepdims=True)
        grad = grad * gain_ref[...]
        first = jnp.mean(grad, axis=1, keepdims=True)
        second = jnp.mean(grad * plain, axis=1, keepdims=True)
        gres = gres_ref[...] + scale * (grad - first - plain * second)
        sum_ref[...] = jnp.sum(gres, axis=0, keepdims=True)
        ga = gres.astype(bf16)
        ga_ref[...] = ga
        gatt_ref[...] = lax.dot_general(out_ref[...], ga, NT, preferred_element_type=f32).astype(bf16)


def join(first, second, attn_qkv, resid, gain, gres, agg_out):
    rows, width = resid.shape
    groups = first.shape[0] // rows
    own = width // groups
    cols = first.shape[1]

    def whole(*shape):
        return pl.BlockSpec(shape, lambda i: (0,) * len(shape))

    return pl.pallas_call(
        join_kernel,
        grid=(groups,),
        in_specs=[
            pl.BlockSpec((rows, cols), lambda i: (i, 0)),
            pl.BlockSpec((rows, cols), lambda i: (i, 0)),
            pl.BlockSpec((width, own), lambda i: (0, i)),
            pl.BlockSpec((width, own), lambda i: (0, groups + i)),
            pl.BlockSpec((width, own), lambda i: (0, 2 * groups + i)),
            whole(rows, width),
            whole(1, width),
            whole(rows, width),
            whole(width, width),
        ],
        out_specs=[whole(rows, width), whole(width, rows), whole(1, width), whole(1, width)],
        scratch_shapes=[pltpu.VMEM((rows, width), f32)],
        out_shape=[
            jax.ShapeDtypeStruct((rows, width), bf16),
            jax.ShapeDtypeStruct((width, rows), bf16),
            jax.ShapeDtypeStruct((1, width), f32),
            jax.ShapeDtypeStruct((1, width), f32),
        ],
        cost_estimate=pl.CostEstimate(flops=8 * rows * width * width, bytes_accessed=16 << 20, transcendentals=0),
        name="join",
    )(first, second, attn_qkv, attn_qkv, attn_qkv, resid, gain, gres, agg_out)


def add(a, b):
    return (a.astype(f32) + b.astype(f32)).astype(bf16)


def quarter_kernel(keep_ref, came_ref, *outs):
    i = pl.program_id(0)
    total = add(keep_ref[...], came_ref[...])
    for q, out in enumerate(outs):

        @pl.when(i // 2 == q)
        def _():
            out[...] = total


def quarters(keep, came):
    rows, cols = keep.shape
    block = rows // 8

    def at(q):
        return lambda i: (jnp.clip(i - 2 * q, 0, 1), 0)

    return pl.pallas_call(
        quarter_kernel,
        grid=(8,),
        in_specs=[pl.BlockSpec((block, cols), lambda i: (i, 0))] * 2,
        out_specs=[pl.BlockSpec((block, cols), at(q)) for q in range(4)],
        out_shape=[jax.ShapeDtypeStruct((rows // 4, cols), bf16)] * 4,
        cost_estimate=pl.CostEstimate(flops=rows * cols, bytes_accessed=6 * rows * cols, transcendentals=0),
        name="quarters",
    )(keep, came)


def halve_kernel(a_ref, b_ref, c_ref, d_ref, a_low, a_high, c_low, c_high):
    for x, y, low, high in ((a_ref, b_ref, a_low, a_high), (c_ref, d_ref, c_low, c_high)):
        half = low.shape[0]
        low[...] = add(x[:half, :], y[:half, :])
        high[...] = add(x[half:, :], y[half:, :])


def halve_both(a, b, c, d):
    rows, cols = a.shape
    return pl.pallas_call(
        halve_kernel,
        out_shape=[jax.ShapeDtypeStruct((rows // 2, cols), bf16)] * 4,
        cost_estimate=pl.CostEstimate(flops=rows * cols, bytes_accessed=12 * rows * cols, transcendentals=0),
        name="halve_both",
    )(a, b, c, d)


def choose_kernel(high, a_ref, b_ref, c_ref, d_ref, keep, send):
    first, second = add(a_ref[...], b_ref[...]), add(c_ref[...], d_ref[...])
    keep[...] = jnp.where(high[0] == 0, first, second)
    send[...] = jnp.where(high[0] == 0, second, first)


def whole_blocks(shapes):
    return [pl.BlockSpec(shape, lambda i, *_, n=len(shape): (0,) * n) for shape in shapes]


def choose(high, a, b, c, d):
    spec = pltpu.PrefetchScalarGridSpec(
        num_scalar_prefetch=1, grid=(1,), in_specs=whole_blocks([a.shape] * 4), out_specs=whole_blocks([a.shape] * 2)
    )
    return pl.pallas_call(
        choose_kernel,
        grid_spec=spec,
        out_shape=[jax.ShapeDtypeStruct(a.shape, bf16)] * 2,
        cost_estimate=pl.CostEstimate(flops=a.size, bytes_accessed=12 * a.size, transcendentals=0),
        name="choose",
    )(high, a, b, c, d)


def part_kernel(high, a_ref, b_ref, keep, send):
    half = keep.shape[0]
    for out, which in ((keep, high[0]), (send, 1 - high[0])):
        span = pl.ds(pl.multiple_of(which * half, half), half)
        out[...] = add(a_ref[span, :], b_ref[span, :])


def part(high, a, b):
    shape = (a.shape[0] // 2, a.shape[1])
    spec = pltpu.PrefetchScalarGridSpec(
        num_scalar_prefetch=1, grid=(1,), in_specs=whole_blocks([a.shape] * 2), out_specs=whole_blocks([shape] * 2)
    )
    return pl.pallas_call(
        part_kernel,
        grid_spec=spec,
        out_shape=[jax.ShapeDtypeStruct(shape, bf16)] * 2,
        cost_estimate=pl.CostEstimate(flops=a.size, bytes_accessed=6 * a.size, transcendentals=0),
        name="part",
    )(high, a, b)


def gather_sources_kernel(high, came_ref, keep, send, *, cols):
    groups, half = came_ref.shape[0], keep.shape[0]
    for out, which in ((keep, high[0]), (send, 1 - high[0])):
        span = pl.ds(pl.multiple_of(which * half, half), half)
        total = jnp.zeros((half, came_ref.shape[2] - cols), f32)
        for p in range(groups):
            out[:, p * cols : (p + 1) * cols] = came_ref[p, span, :cols]
            total = total + came_ref[p, span, cols:].astype(f32)
        out[:, groups * cols :] = total.astype(bf16)


def gather_sources(high, came, cols):
    groups, rows, wide = came.shape
    shape = (rows // 2, groups * cols + wide - cols)
    spec = pltpu.PrefetchScalarGridSpec(
        num_scalar_prefetch=1, grid=(1,), in_specs=whole_blocks([came.shape]), out_specs=whole_blocks([shape] * 2)
    )
    return pl.pallas_call(
        partial(gather_sources_kernel, cols=cols),
        grid_spec=spec,
        out_shape=[jax.ShapeDtypeStruct(shape, bf16)] * 2,
        cost_estimate=pl.CostEstimate(flops=came.size, bytes_accessed=4 * came.size, transcendentals=0),
        name="gather_sources",
    )(high, came)


def place_kernel(high, core, *refs, spans):
    pieces, outs = refs[:4], refs[4:]
    rows = pieces[0].shape[0]
    for ref, upper, which in (
        (pieces[0], high[0], core[0]),
        (pieces[1], 1 - high[0], core[0]),
        (pieces[2], high[0], 1 - core[0]),
        (pieces[3], 1 - high[0], 1 - core[0]),
    ):
        at = pl.ds(pl.multiple_of(upper * rows, rows), rows)
        for number, source, target, scale, size in spans:
            start = pl.multiple_of(target + which * scale, 128)
            outs[number][at, pl.ds(start, size)] = ref[:, source : source + size].astype(f32)


def place(high, core, pieces, spans, widths):
    rows = 2 * pieces[0].shape[0]
    shapes = [(rows, wide) for wide in widths]
    spec = pltpu.PrefetchScalarGridSpec(
        num_scalar_prefetch=2,
        grid=(1,),
        in_specs=whole_blocks([p.shape for p in pieces]),
        out_specs=whole_blocks(shapes),
    )
    return pl.pallas_call(
        partial(place_kernel, spans=spans),
        grid_spec=spec,
        out_shape=[jax.ShapeDtypeStruct(shape, f32) for shape in shapes],
        cost_estimate=pl.CostEstimate(flops=0, bytes_accessed=6 * rows * sum(widths), transcendentals=0),
        name="place",
    )(high, core, *pieces)


def field_kernel(member, *refs):
    pieces, out = refs[:-1], refs[-1]
    kinds, channels, rows = pieces[0].shape
    for k, piece in enumerate(pieces):
        at = pl.ds(pl.multiple_of((member[0] ^ k) * rows, rows), rows)
        for c in range(kinds):
            out[:, c, at] = piece[c].astype(f32)


def place_field(member, pieces):
    kinds, channels, rows = pieces[0].shape
    shape = (channels, kinds, rows * len(pieces))
    spec = pltpu.PrefetchScalarGridSpec(
        num_scalar_prefetch=1,
        grid=(1,),
        in_specs=whole_blocks([p.shape for p in pieces]),
        out_specs=whole_blocks([shape])[0],
    )
    return pl.pallas_call(
        field_kernel, grid_spec=spec, out_shape=jax.ShapeDtypeStruct(shape, f32), name="place_field"
    )(member, *pieces)


def tail_kernel(member, *refs, groups):
    tails = refs[:groups]
    stacked_ref, pick_ref, value_ref, qk_ref, key_ref, query_ref = refs[groups : groups + 6]
    gvalue_ref, gkey_ref, gquery_ref, rows_ref, gqk = refs[groups + 6 :]
    width = value_ref.shape[0]
    own = gvalue_ref.shape[0]
    at = pl.ds(pl.multiple_of(member[0] * own, own), own)
    tail = jnp.concatenate([t[...] for t in tails], axis=0)
    values, keys = tail[:, :width], tail[:, width:]
    gvalue_ref[...] = lax.dot_general(stacked_ref[:, at], values, TN, preferred_element_type=f32)
    gqk[...] = lax.dot_general(stacked_ref[...], keys, TN, preferred_element_type=f32)
    head = lax.broadcasted_iota(jnp.int32, (keys.shape[1], width), 0)
    column = lax.broadcasted_iota(jnp.int32, (keys.shape[1], width), 1) // HEAD_DIM
    spread = jnp.where(head == column, 1.0, 0.0)
    gkey_ref[...] = (
        jnp.dot(gqk[at, :], spread, precision=highest, preferred_element_type=f32) * (query_ref[...] * 0.125)
    )
    by_head = lax.dot_general(gqk[...], key_ref[...].astype(f32), TN, precision=highest, preferred_element_type=f32)
    head = lax.broadcasted_iota(jnp.int32, by_head.shape, 0)
    column = (lax.broadcasted_iota(jnp.int32, by_head.shape, 1) + member[0] * own) // HEAD_DIM
    gquery_ref[...] = jnp.sum(jnp.where(head == column, by_head, 0.0), axis=0, keepdims=True) * 0.125
    own_rows = tails[0].shape[0]
    table = jnp.dot(pick_ref[...], tail, preferred_element_type=f32).astype(bf16)
    rows = jnp.concatenate([tail[:own_rows], table], axis=0)
    rows_ref[...] = lax.dot_general(rows[:, :width], value_ref[...], NT, preferred_element_type=f32) + lax.dot_general(
        rows[:, width:].astype(f32), qk_ref[...], NT, precision=highest, preferred_element_type=f32
    )


def finish_tail(member, tails, stacked, pick, agg_value, query_keys, agg_key, agg_query):
    groups = len(tails)
    width = agg_value.shape[0]
    own = width // groups
    deep = tails[0].shape[0] + pick.shape[0]
    args = [*tails, stacked, pick, agg_value, query_keys]
    spec = pltpu.PrefetchScalarGridSpec(
        num_scalar_prefetch=1,
        grid=(1,),
        in_specs=whole_blocks([x.shape for x in args])
        + [pl.BlockSpec((width, own), lambda i, m: (0, m[0])), pl.BlockSpec((1, width), lambda i, m: (0, 0))],
        out_specs=whole_blocks([(own, width), (own, width), (1, own), (deep, width)]),
        scratch_shapes=[pltpu.VMEM((width, query_keys.shape[1]), f32)],
    )
    return pl.pallas_call(
        partial(tail_kernel, groups=groups),
        grid_spec=spec,
        out_shape=[
            jax.ShapeDtypeStruct((own, width), f32),
            jax.ShapeDtypeStruct((own, width), f32),
            jax.ShapeDtypeStruct((1, own), f32),
            jax.ShapeDtypeStruct((deep, width), f32),
        ],
        cost_estimate=pl.CostEstimate(flops=1 << 30, bytes_accessed=8 << 20, transcendentals=0),
        name="finish_tail",
    )(member, *args, agg_key, agg_query)


def fence(*values):
    return lax.optimization_barrier(values)


def swap(value, axis, bits):
    size = lax.axis_size(axis)
    return lax.ppermute(value, axis, [(s, s ^ bits) for s in range(size)])


def from_all(own, groups):
    return [own] + [swap(own, "var", k) for k in range(1, groups)]


def exchange(value):
    return lax.all_to_all(value, "var", split_axis=0, concat_axis=0, tiled=True)


def patch_bits():
    bits, bit = [], 2
    while bit < lax.axis_size("patch"):
        bits.append(bit)
        bit *= 2
    return bits


def is_high(bit):
    return ((lax.axis_index("patch") // bit) % 2).reshape(1).astype(jnp.int32)


def sum_over_chips(keep, send):
    bits = patch_bits()
    for bit in bits[1:]:
        keep, send = part(is_high(bit), keep, swap(send, "patch", bit // 2))
    value = add(keep, swap(send, "patch", bits[-1]))
    for bit in reversed(bits[1:]):
        other = swap(value, "patch", bit)
        high = is_high(bit)[0] == 1
        value = jnp.concatenate([jnp.where(high, other, value), jnp.where(high, value, other)], axis=0)
    return value, swap(value, "patch", bits[0])


def with_core(halves):
    return [*halves, *(swap(value, "patch", 1) for value in halves)]


def body(
    field_patches,
    var_ids,
    lead_bucket,
    patch_weight,
    var_embed,
    agg_query,
    agg_key,
    agg_value,
    agg_out,
    lead_table,
    ln1_gain,
    attn_qkv,
    attn_out,
    ln2_gain,
    mlp_in,
    mlp_in_bias,
    mlp_out,
    cotangent,
):
    groups = lax.axis_size("var")
    member = lax.axis_index("var")
    core = lax.axis_index("patch") % 2
    channels, pixel_count, samples, seq = field_patches.shape
    width = agg_key.shape[0]
    inner_width = mlp_in.shape[1]
    leads = lead_table.shape[0]
    vocab = var_embed.shape[0]
    rows = seq // groups
    own = width // groups
    count = channels * groups
    slots = [member ^ k for k in range(groups)]
    member_one = member.reshape(1).astype(jnp.int32)
    core_one = core.reshape(1).astype(jnp.int32)
    high = is_high(2)
    gain_one = ln1_gain.astype(f32)
    gain_two = ln2_gain.astype(f32)

    mine = jnp.concatenate(
        [
            field_patches.reshape(channels, pixel_count, seq).transpose(1, 0, 2),
            patch_weight.transpose(1, 0, 2),
        ],
        axis=2,
    )
    grad_out = cotangent.reshape(rows, width)
    grad_act = lax.dot_general(grad_out, mlp_out, NT, preferred_element_type=f32).astype(bf16)
    ids = jnp.concatenate([lax.dynamic_slice_in_dim(var_ids, slot * channels, channels) for slot in slots])
    table_pick = (ids[:, None] == jnp.arange(vocab, dtype=jnp.int32)[None, :]).astype(bf16)
    embeds = jnp.dot(table_pick, var_embed, preferred_element_type=f32).astype(bf16)
    head_of = jnp.arange(width, dtype=jnp.int32) // HEAD_DIM
    spread = head_of[:, None] == jnp.arange(2 * HEAD_DIM, dtype=jnp.int32)[None, :]
    query_block = jnp.where(spread, agg_query[:, None], jnp.zeros((), bf16))
    query_keys = jnp.dot(agg_key, query_block, preferred_element_type=f32) * 0.125
    lead_row = lax.dynamic_slice_in_dim(lead_table, lead_bucket[0], 1).astype(f32)
    arrived, grad_act, embeds, query_keys, lead_row = fence(
        from_all(mine, groups), grad_act, embeds, query_keys, lead_row
    )
    pixels = jnp.concatenate([value[:, :, :seq] for value in arrived], axis=1)
    stacked = jnp.concatenate([value[:, :, seq:] for value in arrived], axis=1)
    stacked = jnp.concatenate([stacked, embeds[None]], axis=0).reshape(-1, width)
    key_rows = jnp.dot(stacked.astype(f32), query_keys, precision=highest).reshape(PIX + 1, count, 2 * HEAD_DIM)
    values = jnp.dot(stacked, agg_value, preferred_element_type=f32).astype(bf16)
    values_t = values.T

    hidden_t, qkv, resid_zero, att_low = front(
        member_one, pixels, key_rows, values_t, agg_out, lead_row, gain_one[None], attn_qkv, groups
    )

    block = min(256, rows)
    mixed_parts, lse_parts, received = [None] * groups, [None] * groups, [None] * groups
    for k in reversed(range(groups)):
        mixed_parts[k], lse_parts[k] = attend(member_one, qkv, k, rows, block)
        if k + 1 < groups:
            received[k + 1], mixed_parts[k], qkv = fence(received[k + 1], mixed_parts[k], qkv)
        received[k] = swap(mixed_parts[k], "var", k) if k else mixed_parts[k]

    out_send, out_keep, in_send, in_keep, grad_bias, output, grad_resid_one, grad_mixed, grad_gain_two = middle(
        member_one,
        core_one,
        received,
        attn_out,
        resid_zero,
        gain_two[None],
        mlp_in,
        mlp_in_bias.astype(f32)[None],
        mlp_out,
        grad_act,
        grad_out,
    )
    output = output.reshape(samples, rows, width)

    grad_heads = exchange(grad_mixed).reshape(seq, own)
    out_came = swap(out_send, "patch", 1)
    in_came = swap(in_send, "patch", 1)
    out_y, out_y_send, out_x, out_x_send = quarters(out_keep, out_came)
    in_y, in_y_send, in_x, in_x_send = quarters(in_keep, in_came)
    grad_heads, out_y_send, out_x_send, in_y, in_y_send, in_x, in_x_send = fence(
        grad_heads, out_y_send, out_x_send, in_y, in_y_send, in_x, in_x_send
    )

    pair = 2 * HEAD_DIM
    pairs = own // pair
    assert pairs == 2
    out_y_came, out_x_came = swap(out_y_send, "var", 2), swap(out_x_send, "var", 1)
    first = attend_back(member_one, qkv, grad_heads, mixed_parts, lse_parts, 0, 512)
    first, out_y_came, out_x_came, in_y_send, in_x_send = fence(first, out_y_came, out_x_came, in_y_send, in_x_send)
    out_y, out_y_send, out_x, out_x_send = halve_both(out_y, out_y_came, out_x, out_x_came)
    first, out_y_send, out_x_send, qkv = fence(first, out_y_send, out_x_send, qkv)
    out_y_came, out_x_came = swap(out_y_send, "var", 1), swap(out_x_send, "var", 2)
    first_came = exchange(first)
    second = attend_back(member_one, qkv, grad_heads, mixed_parts, lse_parts, 1, 512)
    first_came, second, out_y_came, out_x_came, in_y_send, in_x_send = fence(
        first_came, second, out_y_came, out_x_came, in_y_send, in_x_send
    )
    second_came = exchange(second)
    in_y_came, in_x_came = swap(in_y_send, "var", 2), swap(in_x_send, "var", 1)
    out_keep, out_send = choose(high, out_y, out_y_came, out_x, out_x_came)
    weight_qkv = [
        jnp.dot(hidden_t, grads, preferred_element_type=f32).astype(bf16) for grads in (first, second)
    ]
    second_came, weight_qkv, out_send = fence(second_came, weight_qkv, out_send)
    out_halves = sum_over_chips(out_keep, out_send)
    grad_agg, grad_att, grad_gain_one, sample_sum = join(
        first_came, second_came, attn_qkv, resid_zero, gain_one[None], grad_resid_one, agg_out
    )

    def half_of(grad, which):
        half = grad.shape[1] // 2
        return lax.dynamic_slice_in_dim(grad, which * half, half, axis=1)

    last_send = jnp.concatenate(
        [
            jnp.where(core == 0, weight_qkv[1], weight_qkv[0]),
            jnp.dot(att_low, half_of(grad_agg, 1 - core), preferred_element_type=f32).astype(bf16),
        ],
        axis=1,
    )
    last_keep = jnp.concatenate(
        [
            jnp.where(core == 0, weight_qkv[0], weight_qkv[1]),
            jnp.dot(att_low, half_of(grad_agg, core), preferred_element_type=f32).astype(bf16),
        ],
        axis=1,
    )
    last_came = exchange(add(last_keep, swap(last_send, "patch", 1)).reshape(groups, own, -1))
    last_keep, last_send = gather_sources(high, last_came, 3 * pair)
    last_halves = sum_over_chips(last_keep, last_send)

    lead_pick = (lead_bucket[:, None] == jnp.arange(leads, dtype=jnp.int32)[None, :]).astype(f32)
    grad_lead = lead_pick.reshape(leads, 1) * sample_sum
    small = jnp.concatenate(
        [
            grad_bias.reshape(groups, -1),
            grad_gain_two.reshape(groups, own),
            grad_gain_one.reshape(groups, own),
            grad_lead.reshape(groups, -1),
        ],
        axis=1,
    )
    small_size = small.shape[1]
    free = 4
    small = jnp.pad(small, ((0, 0), (0, free * width - small_size))).reshape(groups, free, width)
    small = jnp.concatenate([lax.dynamic_index_in_dim(small, slots[k], 0, keepdims=False) for k in ORDER])

    field_own, tail, tail_send = aggregate_back(
        member_one, core_one, pixels, key_rows, values, grad_att, small, groups
    )
    tail_came = swap(tail_send, "patch", 1)
    field_slots = field_own.reshape(pixel_count, groups, channels, rows)
    field_parts = [swap(field_slots[:, k], "var", k) if k else field_slots[:, 0] for k in range(groups)]
    field_grad = place_field(member_one, field_parts).reshape(channels, pixel_count, samples, seq)

    tail = add(tail, tail_came)
    for bit in (1, 2):
        deep = tail.shape[0] // 2
        tail = add(tail[:deep], swap(tail[deep:], "var", bit))
    for bit in patch_bits():
        tail = add(tail, swap(tail, "patch", bit))
    half = width // 2
    other = swap(tail, "patch", 1)
    low, up = jnp.where(core == 0, tail, other), jnp.where(core == 0, other, tail)
    tail = jnp.concatenate([low[:, :half], up], axis=1)
    tails = from_all(tail, groups)
    stride = tail.shape[0]
    per_slot = (PIX + 1) * channels
    small_sum = tail[per_slot:, :width].astype(f32).reshape(-1)
    part_size = inner_width // groups
    sum_bias = small_sum[:part_size]
    sum_gain_two = small_sum[part_size : part_size + own]
    sum_gain_one = small_sum[part_size + own : part_size + 2 * own]
    sum_lead = small_sum[part_size + 2 * own : small_size].reshape(leads // groups, width)

    by_slot = stacked.reshape(PIX + 1, groups, channels, width).transpose(1, 0, 2, 3).reshape(groups, per_slot, width)
    by_slot = jnp.pad(by_slot, ((0, 0), (0, stride - per_slot), (0, 0))).reshape(groups * stride, width)
    own_ids = member * (vocab // groups) + jnp.arange(16, dtype=jnp.int32)
    own_pick = jnp.where(jnp.arange(16)[:, None] < vocab // groups, own_ids[:, None] == ids[None, :], False)
    own_pick = jnp.pad(
        own_pick.reshape(16, groups, channels), ((0, 0), (0, 0), (PIX * channels, stride - per_slot))
    ).reshape(16, groups * stride)
    sum_value, sum_key, sum_query, sum_rows = finish_tail(
        member_one,
        tails,
        by_slot,
        own_pick.astype(bf16),
        agg_value,
        query_keys,
        agg_key,
        agg_query.astype(f32)[None],
    )
    sum_query = sum_query.reshape(own)
    sum_patch = sum_rows[: PIX * channels].reshape(pixel_count, channels, width).transpose(1, 0, 2)
    sum_table = sum_rows[stride : stride + vocab // groups]

    in_y, in_y_send, in_x, in_x_send = halve_both(in_y, in_y_came, in_x, in_x_came)
    in_y_came, in_x_came = swap(in_y_send, "var", 1), swap(in_x_send, "var", 2)
    in_keep, in_send = choose(high, in_y, in_y_came, in_x, in_x_came)
    in_halves = sum_over_chips(in_keep, in_send)
    (sum_mlp_out,) = place(high, core_one, with_core(out_halves), [(0, 0, 0, half, half)], [width])
    half_in = inner_width // 2
    sum_mlp_in, sum_attn_out = place(
        high,
        core_one,
        with_core(in_halves),
        [(0, 0, 0, half_in, half_in), (1, half_in, 0, half, half)],
        [inner_width, width],
    )
    sum_qkv, sum_agg_out = place(
        high,
        core_one,
        with_core(last_halves),
        [(0, p * 3 * pair + t * pair, t * width + p * own, pair, pair) for p in range(groups) for t in range(3)]
        + [(1, groups * 3 * pair, 0, half, half)],
        [3 * width, width],
    )
    return (
        output,
        field_grad,
        sum_patch,
        sum_table,
        sum_query,
        sum_key,
        sum_value,
        sum_agg_out,
        sum_lead,
        sum_gain_one,
        sum_qkv,
        sum_attn_out,
        sum_gain_two,
        sum_mlp_in,
        sum_bias,
        sum_mlp_out,
    )


def solution(mesh):
    placed = (
        P("var", None, "patch", None),
        P(),
        P("patch"),
        P("var", None, None),
        P(),
        P(),
        P(),
        P(),
        P(),
        P(),
        P(),
        P(),
        P(),
        P(),
        P(),
        P(),
        P(),
        P("patch", "var", None),
    )
    return jax.shard_map(
        body,
        mesh=mesh,
        in_specs=placed,
        out_specs=(
            P("patch", "var", None),
            P("var", None, "patch", None),
            P("var", None, None),
            P("var", None),
            P("var"),
            P("var", None),
            P("var", None),
            P("var", None),
            P("var", None),
            P("var"),
            P("var", None),
            P("var", None),
            P("var"),
            P("var", None),
            P("var"),
            P("var", None),
        ),
        check_vma=False,
    )
```

time: 780 us -> 523 us (0.67)
  Pallas kernels: 115 us -> 231 us
  local copies, waits for them, and re-layouts: 142 us -> 33.2 us
  matrix products: 138 us -> 29.7 us
  waiting for transfers between devices: 233 us -> 135 us
  other arithmetic: 69.2 us -> 21.8 us
  starting transfers between devices: 72.3 us -> 61.9 us
    pallas_call x6 -> x23, Pallas kernels: 84.5 us -> 201 us  [the longest x2 49 us: attend_back(): pl.pallas_call(partial(attend_back_kernel, chunk=min(chunk, seq), groups=...]
    dot_general x52 -> x5, matrix products: 133 us -> 26.7 us  [the longest x2 11.3 us: body(): jnp.dot(hidden_t, grads, preferred_element_type=f32).astype(bf16)]
    ppermute x90 -> x47, waiting for transfers between devices: 233 us -> 133 us  [swap(): return lax.ppermute(value, axis, [(s, s ^ bits) for s in range(size)])]
    dynamic_update_slice x8 -> x0, local copies, waits for them, and re-layouts: 70.3 us -> none  [the longest x4 69.8 us: body(): lax.dynamic_update_slice(sum_qkv, ordered[:, :, k].reshape(own, 3, 1, pai...]
    ppermute x90 -> x47, starting transfers between devices: 72.3 us -> 47 us  [swap(): return lax.ppermute(value, axis, [(s, s ^ bits) for s in range(size)])]
    convert_element_type x31 -> x11, other arithmetic: 34.1 us -> 8.8 us  [the longest x9 8.71 us: add(): return (a.astype(f32) + b.astype(f32)).astype(bf16)]
    all_to_all x0 -> x4, starting transfers between devices: none -> 14.9 us  [exchange(): return lax.all_to_all(value, 'var', split_axis=0, concat_axis=0, tiled=True)]
    another operation x6 -> x0, local copies, waits for them, and re-layouts: 14.5 us -> none  [the longest x4 12.2 us: body(): ordered[:, :, k].reshape(own, 3, 1, pairs * pair)]
  transfers between devices with their start and end apart: 90 -> 51, of which waited for: 37 -> 18; matrix products, arithmetic and copies ran while one was open for 34% -> 12% of each run, Pallas kernels for 7% -> 26%
where the time goes in v2:
time: 523 us; the launch traced here: 515 us
  Pallas kernels  231 us (44%)
  waiting for transfers between devices  135 us (26%)
  starting transfers between devices  61.9 us (12%)
  local copies, waits for them, and re-layouts  33.2 us (6%)
  matrix products  29.7 us (6%)
  other arithmetic  21.8 us (4%)
    ppermute x47, waiting for transfers between devices, swap(): return lax.ppermute(value, axis, [(s, s ^ bits) for s in range(size)])  133 us
    pallas_call x2, Pallas kernels, attend_back(): pl.pallas_call(partial(attend_back_kernel, chunk=min(chunk, seq), groups=...  49 us
    ppermute x47, starting transfers between devices, swap(): return lax.ppermute(value, axis, [(s, s ^ bits) for s in range(size)])  47 us
    pallas_call x1, Pallas kernels, middle(): pl.pallas_call(middle_kernel, grid_spec=spec, out_shape=[shape(inner, hal...  42.2 us
    pallas_call x4, Pallas kernels, attend(): pl.pallas_call(attend_kernel, grid_spec=spec, out_shape=[jax.ShapeDtypeSt...  35.6 us
    pallas_call x1, Pallas kernels, front(): pl.pallas_call(front_kernel, grid_spec=spec, out_shape=[jax.ShapeDtypeStr...  23.4 us
    pallas_call x2, Pallas kernels, quarters(): pl.pallas_call(quarter_kernel, grid=(8,), in_specs=[pl.BlockSpec((block,...  18.2 us
    unnamed x130, local copies, waits for them, and re-layouts  17.8 us
  transfers between devices with their start and end apart: 51, of which 18 were waited for; matrix products, arithmetic and copies ran while one was open for 12% of the time, Pallas kernels for 26%

profile of v2, /device:TPU:0, one launch (start us, length us, event | category | flops | bytes accessed | tf_op | source)
XLA Modules:
  0.0 515.4 jit_solution(13219317192877493784)
XLA Ops:
  2.7 4.0 collective-permute-start.2
  9.3 10.4 %convolution_convert_fusion.ga_ref = bf16[512,4096]{1,0:T(8,128)(2,1)} fusion(bf16[4096,1024]{1,0:T(8,128)(2,1)} %w2_ref.1, bf16[1,512,1024]{2,1,0:T(8,128)(2,1)} %param.35), kind=kOutput, calls=%fused_computation | convolution fusion | flops 4297064448 | bytes 13631488 | tf_op jit(solution)/shard_map/dot_general | solution.py:916
  31.1 23.4 %front.1 = (bf16[1024,2048]{1,0:T(8,128)(2,1)}, bf16[2048,768]{1,0:T(8,128)(2,1)}, f32[512,1024]{1,0:T(8,128)}, bf16[1024,512]{1,0:T(8,128)(2,1)}) custom-call(s32[1]{0:T(128)} %bitcast.member, bf16[4,48,2048]{2,1,0:T(8,128)(2,1)} %pad_maximum_fusion.1.pixel_ref, f32[5,48,128]{2,1,0:T(8,128)} %fusion.1.key_ref, bf16[1024,240]{1,0:T(8,128)(2,1)} %copy.47.value_ref, ...), custom_call_target="tpu_custom_call" | custom-call | flops 7516192768 | bytes 16777216 | tf_op jit(solution)/shard_map/front/pallas_call | solution.py:110
  54.5 8.9 %attend.4 = (bf16[512,256]{1,0:T(8,128)(2,1)}, f32[2,2,512]{2,1,0:T(2,128)}) custom-call(s32[1]{0:T(128)} %bitcast.member, bf16[2048,768]{1,0:T(8,128)(2,1)} %get-tuple-element.175.q_ref.k_ref.v_ref, bf16[2048,768]{1,0:T(8,128)(2,1)} %get-tuple-element.175.q_ref.k_ref.v_ref, bf16[2048,768]{1,0:T(8,128)(2,1)} %get-tuple-element.175.q_ref.k_ref.v_ref), custom_call_target="tpu_custom_call" | custom-call | flops 4294967296 | bytes 3145728 | tf_op jit(solution)/shard_map/attend/pallas_call | solution.py:163
  65.6 8.9 %attend.5 = (bf16[512,256]{1,0:T(8,128)(2,1)}, f32[2,2,512]{2,1,0:T(2,128)}) custom-call(s32[1]{0:T(128)} %bitcast.member, bf16[2048,768]{1,0:T(8,128)(2,1)} %get-tuple-element.175.q_ref.k_ref.v_ref, bf16[2048,768]{1,0:T(8,128)(2,1)} %get-tuple-element.175.q_ref.k_ref.v_ref, bf16[2048,768]{1,0:T(8,128)(2,1)} %get-tuple-element.175.q_ref.k_ref.v_ref), custom_call_target="tpu_custom_call" | custom-call | flops 4294967296 | bytes 3145728 | tf_op jit(solution)/shard_map/attend/pallas_call | solution.py:163
  75.3 8.9 %attend.6 = (bf16[512,256]{1,0:T(8,128)(2,1)}, f32[2,2,512]{2,1,0:T(2,128)}) custom-call(s32[1]{0:T(128)} %bitcast.member, bf16[2048,768]{1,0:T(8,128)(2,1)} %get-tuple-element.175.q_ref.k_ref.v_ref, bf16[2048,768]{1,0:T(8,128)(2,1)} %get-tuple-element.175.q_ref.k_ref.v_ref, bf16[2048,768]{1,0:T(8,128)(2,1)} %get-tuple-element.175.q_ref.k_ref.v_ref), custom_call_target="tpu_custom_call" | custom-call | flops 4294967296 | bytes 3145728 | tf_op jit(solution)/shard_map/attend/pallas_call | solution.py:163
  84.8 8.9 %attend.7 = (bf16[512,256]{1,0:T(8,128)(2,1)}, f32[2,2,512]{2,1,0:T(2,128)}) custom-call(s32[1]{0:T(128)} %bitcast.member, bf16[2048,768]{1,0:T(8,128)(2,1)} %get-tuple-element.175.q_ref.k_ref.v_ref, bf16[2048,768]{1,0:T(8,128)(2,1)} %get-tuple-element.175.q_ref.k_ref.v_ref, bf16[2048,768]{1,0:T(8,128)(2,1)} %get-tuple-element.175.q_ref.k_ref.v_ref), custom_call_target="tpu_custom_call" | custom-call | flops 4294967296 | bytes 3145728 | tf_op jit(solution)/shard_map/attend/pallas_call | solution.py:163
  94.4 42.2 %middle.1 = (bf16[4096,512]{1,0:T(8,128)(2,1)}, bf16[4096,512]{1,0:T(8,128)(2,1)}, bf16[1024,2560]{1,0:T(8,128)(2,1)}, bf16[1024,2560]{1,0:T(8,128)(2,1)}, f32[1...) custom-call(s32[1]{0:T(128)} %bitcast.member, ...), custom_call_target="tpu_custom_call" | custom-call | flops 24696061952 | bytes 50331648 | tf_op jit(solution)/shard_map/middle/pallas_call | solution.py:502
  137.1 3.5 all-to-all-start
  140.7 11.0 %collective-permute-done.6.came_ref = bf16[4096,512]{1,0:T(8,128)(2,1)} collective-permute-done((bf16[4096,512]{1,0:T(8,128)(2,1)}, bf16[4096,512]{1,0:T(8,128)(2,1)}, u32[]{:S(2)}, u32[]{:S(2)}) %collective-permute-start.6) | collective-permute-done | bytes 4194336 | tf_op jit(solution)/shard_map/ppermute | solution.py:831
  151.6 8.6 %quarters.2 = (bf16[1024,512]{1,0:T(8,128)(2,1)}, bf16[1024,512]{1,0:T(8,128)(2,1)}, bf16[1024,512]{1,0:T(8,128)(2,1)}, bf16[1024,512]{1,0:T(8,128)(2,1)}) custom-call(bf16[4096,512]{1,0:T(8,128)(2,1)} %get-tuple-element.148.keep_ref, bf16[4096,512]{1,0:T(8,128)(2,1)} %collective-permute-done.6.came_ref), custom_call_target="tpu_custom_call" | custom-call | flops 2097152 | bytes 12582912 | tf_op jit(solution)/shard_map/quarters/pallas_call | solution.py:614
  160.2 9.6 %quarters.3 = (bf16[256,2560]{1,0:T(8,128)(2,1)}, bf16[256,2560]{1,0:T(8,128)(2,1)}, bf16[256,2560]{1,0:T(8,128)(2,1)}, bf16[256,2560]{1,0:T(8,128)(2,1)}) custom-call(bf16[1024,2560]{1,0:T(8,128)(2,1)} %get-tuple-element.152.keep_ref, bf16[1024,2560]{1,0:T(8,128)(2,1)} %collective-permute-done.7.came_ref), custom_call_target="tpu_custom_call" | custom-call | flops 2621440 | bytes 15728640 | tf_op jit(solution)/shard_map/quarters/pallas_call | solution.py:614
  172.7 24.5 %attend_back.2 = bf16[2048,384]{1,0:T(8,128)(2,1)} custom-call(s32[1]{0:T(128)} %bitcast.member, bf16[2048,768]{1,0:T(8,128)(2,1)} %get-tuple-element.175.q_ref.k_ref.v_ref, bf16[2048,768]{1,0:T(8,128)(2,1)} %get-tuple-element.175.q_ref.k_ref.v_ref, bf16[2048,768]{1,0:T(8,128)(2,1)} %get-tuple-element.175.q_ref.k_ref.v_ref, bf16[2048,256]{1,0:T(8,128)(2,1)} %bitcast.104, ...), custom_call_target="tpu_custom_call" | custom-call | flops 21474836480 | bytes 5242880 | tf_op jit(solution)/shard_map/attend_back/pallas_call | solution.py:247
  198.2 3.7 halve_both.2
  201.8 3.9 all-to-all-start.1
  209.2 24.5 %attend_back.3 = bf16[2048,384]{1,0:T(8,128)(2,1)} custom-call(s32[1]{0:T(128)} %bitcast.member, bf16[2048,768]{1,0:T(8,128)(2,1)} %get-tuple-element.175.q_ref.k_ref.v_ref, bf16[2048,768]{1,0:T(8,128)(2,1)} %get-tuple-element.175.q_ref.k_ref.v_ref, bf16[2048,768]{1,0:T(8,128)(2,1)} %get-tuple-element.175.q_ref.k_ref.v_ref, bf16[2048,256]{1,0:T(8,128)(2,1)} %bitcast.105, ...), custom_call_target="tpu_custom_call" | custom-call | flops 21474836480 | bytes 5242880 | tf_op jit(solution)/shard_map/attend_back/pallas_call | solution.py:247
  237.1 3.6 all-to-all-start.2
  242.8 5.9 %convolution_convert_fusion.4 = bf16[1024,384]{1,0:T(8,128)(2,1)} fusion(bf16[1024,2048]{1,0:T(8,128)(2,1)} %get-tuple-element.182, bf16[2048,384]{1,0:T(8,128)(2,1)} %attend_back.2), kind=kOutput, calls=%fused_computation.6 | convolution fusion | flops 1611005952 | bytes 6553600 | tf_op jit(solution)/shard_map/dot_general | solution.py:989
  248.7 2.9 choose.2
  251.6 5.4 %convolution_convert_fusion.3 = bf16[1024,384]{1,0:T(8,128)(2,1)} fusion(bf16[1024,2048]{1,0:T(8,128)(2,1)} %get-tuple-element.182, bf16[2048,384]{1,0:T(8,128)(2,1)S(1)} %copy-done.11), kind=kOutput, calls=%fused_computation.5 | convolution fusion | flops 1611005952 | bytes 6553600 | tf_op jit(solution)/shard_map/dot_general | solution.py:989
  260.4 12.9 %join.1 = (bf16[512,1024]{1,0:T(8,128)(2,1)}, bf16[1024,512]{1,0:T(8,128)(2,1)}, f32[1,1024]{1,0:T(1,128)}, f32[1,1024]{1,0:T(1,128)}) custom-call(bf16[2048,384]{1,0:T(8,128)(2,1)} %bitcast.94, bf16[2048,384]{1,0:T(8,128)(2,1)} %bitcast.95, bf16[1024,3072]{1,0:T(8,128)(2,1)} %wv.1, bf16[1024,3072]{1,0:T(8,128)(2,1)} %wv.1, bf16[1024,3072]{1,0:T(8,128)(2,1)} %wv.1, ...), custom_call_target="tpu_custom_call" | custom-call | flops 4294967296 | bytes 16777216 | tf_op jit(solution)/shard_map/join/pallas_call | solution.py:566
  281.2 6.4 %aggregate_back.1 = (bf16[4,48,512]{2,1,0:T(8,128)(2,1)}, bf16[256,640]{1,0:T(8,128)(2,1)}, bf16[256,640]{1,0:T(8,128)(2,1)}) custom-call(s32[1]{0:T(128)} %bitcast.member, s32[1]{0:T(128)} %bitcast.1.core, bf16[4,48,2048]{2,1,0:T(8,128)(2,1)} %pad_maximum_fusion.1.pixel_ref, f32[5,48,128]{2,1,0:T(8,128)} %fusion.1.key_ref, bf16[240,1024]{1,0:T(8,128)(2,1)} %copy-done.37, ...), custom_call_target="tpu_custom_call" | custom-call | flops 2013265920 | bytes 3145728 | tf_op jit(solution)/shard_map/aggregate_back/pallas_call | solution.py:339
  294.4 29.4 %collective-permute-done.16 = bf16[128,640]{1,0:T(8,128)(2,1)S(1)} collective-permute-done((bf16[128,640]{1,0:T(8,128)(2,1)S(1)}, bf16[128,640]{1,0:T(8,128)(2,1)S(1)}, u32[]{:S(2)}, u32[]{:S(2)}) %collective-permute-start.16) | collective-permute-done | bytes 163872 | tf_op jit(solution)/shard_map/ppermute | solution.py:831
  324.5 3.8 collective-permute-done.17
  330.0 3.1 convolution_convert_fusion.2
  335.3 4.1 halve_both.3
  344.2 2.6 collective-permute-start.42
  348.2 2.6 add_convert_fusion
  350.8 2.5 copy.59
  353.3 4.0 all-to-all-start.3
  362.8 3.1 choose.3
  368.6 2.6 collective-permute-start.43
  371.2 14.6 %collective-permute-done.35.b_ref = bf16[128,2560]{1,0:T(8,128)(2,1)S(1)} collective-permute-done((bf16[128,2560]{1,0:T(8,128)(2,1)}, bf16[128,2560]{1,0:T(8,128)(2,1)S(1)}, u32[]{:S(2)}, u32[]{:S(2)}) %collective-permute-start.35) | collective-permute-done | bytes 655392 | tf_op jit(solution)/shard_map/ppermute | solution.py:831
  390.7 2.6 gather_sources.1
  393.3 6.3 %collective-permute-done.36 = bf16[64,2560]{1,0:T(8,128)(2,1)S(1)} collective-permute-done((bf16[64,2560]{1,0:T(8,128)(2,1)}, bf16[64,2560]{1,0:T(8,128)(2,1)S(1)}, u32[]{:S(2)}, u32[]{:S(2)}) %collective-permute-start.36) | collective-permute-done | bytes 327712 | tf_op jit(solution)/shard_map/ppermute | solution.py:831
  404.8 11.3 %collective-permute-done.25.b_ref = bf16[128,2048]{1,0:T(8,128)(2,1)S(1)} collective-permute-done((bf16[128,2048]{1,0:T(8,128)(2,1)}, bf16[128,2048]{1,0:T(8,128)(2,1)S(1)}, u32[]{:S(2)}, u32[]{:S(2)}) %collective-permute-start.25) | collective-permute-done | bytes 524320 | tf_op jit(solution)/shard_map/ppermute | solution.py:831
  416.1 2.8 collective-permute-start.23
  421.0 2.6 collective-permute-start.26
  423.6 9.5 %collective-permute-done.26 = bf16[64,2048]{1,0:T(8,128)(2,1)S(1)} collective-permute-done((bf16[64,2048]{1,0:T(8,128)(2,1)}, bf16[64,2048]{1,0:T(8,128)(2,1)S(1)}, u32[]{:S(2)}, u32[]{:S(2)}) %collective-permute-start.26) | collective-permute-done | bytes 262176 | tf_op jit(solution)/shard_map/ppermute | solution.py:831
  434.4 12.5 %collective-permute-done.27 = bf16[64,2048]{1,0:T(8,128)(2,1)S(1)} collective-permute-done((bf16[64,2048]{1,0:T(8,128)(2,1)S(1)}, bf16[64,2048]{1,0:T(8,128)(2,1)S(1)}, u32[]{:S(2)}, u32[]{:S(2)}) %collective-permute-start.27) | collective-permute-done | bytes 262176 | tf_op jit(solution)/shard_map/ppermute | solution.py:831
  454.2 3.1 collective-permute-done.21.refs_1_
  457.3 7.9 %collective-permute-done.38.refs_1_ = bf16[128,2560]{1,0:T(8,128)(2,1)S(1)} collective-permute-done((bf16[128,2560]{1,0:T(8,128)(2,1)S(1)}, bf16[128,2560]{1,0:T(8,128)(2,1)S(1)}, u32[]{:S(2)}, u32[]{:S(2)}) %collective-permute-start.38) | collective-permute-done | bytes 655392 | tf_op jit(solution)/shard_map/ppermute | solution.py:831
  465.7 10.8 %collective-permute-done.44.refs_1_ = bf16[512,512]{1,0:T(8,128)(2,1)} collective-permute-done((bf16[512,512]{1,0:T(8,128)(2,1)S(1)}, bf16[512,512]{1,0:T(8,128)(2,1)}, u32[]{:S(2)}, u32[]{:S(2)}) %collective-permute-start.44) | collective-permute-done | bytes 524320 | tf_op jit(solution)/shard_map/ppermute | solution.py:831
  477.1 7.2 %collective-permute-done.28.refs_1_ = bf16[128,2048]{1,0:T(8,128)(2,1)} collective-permute-done((bf16[128,2048]{1,0:T(8,128)(2,1)S(1)}, bf16[128,2048]{1,0:T(8,128)(2,1)}, u32[]{:S(2)}, u32[]{:S(2)}) %collective-permute-start.28) | collective-permute-done | bytes 524320 | tf_op jit(solution)/shard_map/ppermute | solution.py:831
  492.5 6.2 %finish_tail.1 = (f32[256,1024]{1,0:T(8,128)}, f32[256,1024]{1,0:T(8,128)}, f32[1,256]{1,0:T(1,128)}, f32[80,1024]{1,0:T(8,128)}) custom-call(s32[1]{0:T(128)} %bitcast.member, bf16[64,1152]{1,0:T(8,128)(2,1)} %copy-done.31, bf16[64,1152]{1,0:T(8,128)(2,1)} %collective-permute-done.21.refs_1_, bf16[64,1152]{1,0:T(8,128)(2,1)} %copy-done.46, ...), custom_call_target="tpu_custom_call" | custom-call | flops 1073741824 | bytes 8388608 | tf_op jit(solution)/shard_map/finish_tail/pallas_call | solution.py:811
  502.0 3.8 place.5
  505.8 4.4 place.4
  511.0 4.0 place.3
  (300 shorter events, 103.4 us)
Async XLA Ops:
  2.7 21.0 %collective-permute-start.2 = (bf16[4,12,3072]{2,1,0:T(8,128)(2,1)S(1)}, bf16[4,12,3072]{2,1,0:T(8,128)(2,1)}, u32[]{:S(2)}, u32[]{:S(2)}) collective-permute-start(bf16[4,12,3072]{2,1,0:T(8,128)(2,1)S(1)} %pad_maximum_fusion.6), channel_id=1, source_target_pairs={{0,24},{8,16},{16,8},{24,0},{1,25},{9,17},{17,9},{25,1},{2,26},{10... | collective-permute-start | bytes 884744 | tf_op jit(solution)/shard_map/ppermute | solution.py:831
  6.7 17.5 %collective-permute-start.1 = (bf16[4,12,3072]{2,1,0:T(8,128)(2,1)S(1)}, bf16[4,12,3072]{2,1,0:T(8,128)(2,1)S(1)}, u32[]{:S(2)}, u32[]{:S(2)}) collective-permute-start(bf16[4,12,3072]{2,1,0:T(8,128)(2,1)S(1)} %pad_maximum_fusion.6), channel_id=1, source_target_pairs={{0,16},{8,24},{16,0},{24,8},{1,17},{9,25},{17,1},{25,9},{2,18},{10... | collective-permute-start | bytes 884744 | tf_op jit(solution)/shard_map/ppermute | solution.py:831
  7.2 17.3 %collective-permute-start = (bf16[4,12,3072]{2,1,0:T(8,128)(2,1)S(1)}, bf16[4,12,3072]{2,1,0:T(8,128)(2,1)S(1)}, u32[]{:S(2)}, u32[]{:S(2)}) collective-permute-start(bf16[4,12,3072]{2,1,0:T(8,128)(2,1)S(1)} %pad_maximum_fusion.6), channel_id=1, source_target_pairs={{0,8},{8,0},{16,24},{24,16},{1,9},{9,1},{17,25},{25,17},{2,10},{10... | collective-permute-start | bytes 884744 | tf_op jit(solution)/shard_map/ppermute | solution.py:831
  63.4 11.1 %collective-permute-start.3 = (bf16[512,256]{1,0:T(8,128)(2,1)}, bf16[512,256]{1,0:T(8,128)(2,1)S(1)}, u32[]{:S(2)}, u32[]{:S(2)}) collective-permute-start(bf16[512,256]{1,0:T(8,128)(2,1)} %get-tuple-element.131.refs_3_), channel_id=1, source_target_pairs={{0,24},{8,16},{16,8},{24,0},{1,25},{9,17},{17,9},{25,1},{2,26},{10... | collective-permute-start | bytes 786440 | tf_op jit(solution)/shard_map/ppermute | solution.py:831
  74.5 9.8 %collective-permute-start.4 = (bf16[512,256]{1,0:T(8,128)(2,1)}, bf16[512,256]{1,0:T(8,128)(2,1)S(1)}, u32[]{:S(2)}, u32[]{:S(2)}) collective-permute-start(bf16[512,256]{1,0:T(8,128)(2,1)} %get-tuple-element.133.refs_2_), channel_id=1, source_target_pairs={{0,16},{8,24},{16,0},{24,8},{1,17},{9,25},{17,1},{25,9},{2,18},{10... | collective-permute-start | bytes 786440 | tf_op jit(solution)/shard_map/ppermute | solution.py:831
  84.2 9.4 %collective-permute-start.5 = (bf16[512,256]{1,0:T(8,128)(2,1)}, bf16[512,256]{1,0:T(8,128)(2,1)S(1)}, u32[]{:S(2)}, u32[]{:S(2)}) collective-permute-start(bf16[512,256]{1,0:T(8,128)(2,1)} %get-tuple-element.136.refs_1_), channel_id=1, source_target_pairs={{0,8},{8,0},{16,24},{24,16},{1,9},{9,1},{17,25},{25,17},{2,10},{10... | collective-permute-start | bytes 786440 | tf_op jit(solution)/shard_map/ppermute | solution.py:831
  136.6 23.7 %collective-permute-start.7 = (bf16[1024,2560]{1,0:T(8,128)(2,1)}, bf16[1024,2560]{1,0:T(8,128)(2,1)}, u32[]{:S(2)}, u32[]{:S(2)}) collective-permute-start(bf16[1024,2560]{1,0:T(8,128)(2,1)} %get-tuple-element.153), channel_id=1, source_target_pairs={{0,1},{1,0},{2,3},{3,2},{4,5},{5,4},{6,7},{7,6},{8,9},{9,8},{10,11... | collective-permute-start | bytes 15728648 | tf_op jit(solution)/shard_map/ppermute | solution.py:831
  136.6 15.0 %collective-permute-start.6 = (bf16[4096,512]{1,0:T(8,128)(2,1)}, bf16[4096,512]{1,0:T(8,128)(2,1)}, u32[]{:S(2)}, u32[]{:S(2)}) collective-permute-start(bf16[4096,512]{1,0:T(8,128)(2,1)} %get-tuple-element.149), channel_id=1, source_target_pairs={{0,1},{1,0},{2,3},{3,2},{4,5},{5,4},{6,7},{7,6},{8,9},{9,8},{10,11... | collective-permute-start | bytes 12582920 | tf_op jit(solution)/shard_map/ppermute | solution.py:831
  137.1 32.7 %all-to-all-start = ((bf16[4,512,256]{2,1,0:T(8,128)(2,1)}), bf16[4,512,256]{2,1,0:T(8,128)(2,1)S(1)}, u32[]{:S(2)}, u32[]{:S(2)}) async-start(bf16[4,512,256]{2,1,0:T(8,128)(2,1)} %get-tuple-element.147), calls=%async_computation | async-start | bytes 2097152 | tf_op jit(solution)/shard_map/all_to_all | solution.py:839
  169.9 27.3 %collective-permute-start.8 = (bf16[1024,512]{1,0:T(8,128)(2,1)}, bf16[1024,512]{1,0:T(8,128)(2,1)S(1)}, u32[]{:S(2)}, u32[]{:S(2)}) collective-permute-start(bf16[1024,512]{1,0:T(8,128)(2,1)} %get-tuple-element.163), channel_id=1, source_target_pairs={{0,16},{8,24},{16,0},{24,8},{1,17},{9,25},{17,1},{25,9},{2,18},{10... | collective-permute-start | bytes 3145736 | tf_op jit(solution)/shard_map/ppermute | solution.py:831
  171.5 25.7 %collective-permute-start.9 = (bf16[1024,512]{1,0:T(8,128)(2,1)}, bf16[1024,512]{1,0:T(8,128)(2,1)}, u32[]{:S(2)}, u32[]{:S(2)}) collective-permute-start(bf16[1024,512]{1,0:T(8,128)(2,1)} %get-tuple-element.164), channel_id=1, source_target_pairs={{0,8},{8,0},{16,24},{24,16},{1,9},{9,1},{17,25},{25,17},{2,10},{10... | collective-permute-start | bytes 3145736 | tf_op jit(solution)/shard_map/ppermute | solution.py:831
  201.8 34.3 %all-to-all-start.1 = ((bf16[4,512,384]{2,1,0:T(8,128)(2,1)}), bf16[4,512,384]{2,1,0:T(8,128)(2,1)S(1)}, u32[]{:S(2)}, u32[]{:S(2)}) async-start(bf16[4,512,384]{2,1,0:T(8,128)(2,1)} %bitcast.17), calls=%async_computation.1 | async-start | bytes 3145728 | tf_op jit(solution)/shard_map/all_to_all | solution.py:839
  205.7 30.5 %collective-permute-start.10 = (bf16[512,512]{1,0:T(8,128)(2,1)}, bf16[512,512]{1,0:T(8,128)(2,1)S(1)}, u32[]{:S(2)}, u32[]{:S(2)}) collective-permute-start(bf16[512,512]{1,0:T(8,128)(2,1)} %get-tuple-element.176), channel_id=1, source_target_pairs={{0,8},{8,0},{16,24},{24,16},{1,9},{9,1},{17,25},{25,17},{2,10},{10... | collective-permute-start | bytes 1572872 | tf_op jit(solution)/shard_map/ppermute | solution.py:831
  207.8 28.4 %collective-permute-start.11 = (bf16[512,512]{1,0:T(8,128)(2,1)S(1)}, bf16[512,512]{1,0:T(8,128)(2,1)S(1)}, u32[]{:S(2)}, u32[]{:S(2)}) collective-permute-start(bf16[512,512]{1,0:T(8,128)(2,1)S(1)} %copy-done.54), channel_id=1, source_target_pairs={{0,16},{8,24},{16,0},{24,8},{1,17},{9,25},{17,1},{25,9},{2,18},{10... | collective-permute-start | bytes 1572872 | tf_op jit(solution)/shard_map/ppermute | solution.py:831
  237.1 22.1 %all-to-all-start.2 = ((bf16[4,512,384]{2,1,0:T(8,128)(2,1)}), bf16[4,512,384]{2,1,0:T(8,128)(2,1)S(1)}, u32[]{:S(2)}, u32[]{:S(2)}) async-start(bf16[4,512,384]{2,1,0:T(8,128)(2,1)} %bitcast.99), calls=%async_computation.2 | async-start | bytes 3145728 | tf_op jit(solution)/shard_map/all_to_all | solution.py:839
  280.6 67.6 %collective-permute-start.24 = (bf16[1024,896]{0,1:T(8,128)(2,1)}, bf16[1024,896]{0,1:T(8,128)(2,1)}, u32[]{:S(2)}, u32[]{:S(2)}) collective-permute-start(bf16[1024,896]{0,1:T(8,128)(2,1)} %pad_maximum_fusion), channel_id=1, source_target_pairs={{0,1},{1,0},{2,3},{3,2},{4,5},{5,4},{6,7},{7,6},{8,9},{9,8},{10,11... | collective-permute-start | bytes 5505032 | tf_op jit(solution)/shard_map/ppermute | solution.py:831
  288.1 46.1 %collective-permute-start.31 = (bf16[256,2560]{1,0:T(8,128)(2,1)}, bf16[256,2560]{1,0:T(8,128)(2,1)S(1)}, u32[]{:S(2)}, u32[]{:S(2)}) collective-permute-start(bf16[256,2560]{1,0:T(8,128)(2,1)} %get-tuple-element.213), channel_id=1, source_target_pairs={{0,16},{8,24},{16,0},{24,8},{1,17},{9,25},{17,1},{25,9},{2,18},{10... | collective-permute-start | bytes 3932168 | tf_op jit(solution)/shard_map/ppermute | solution.py:831
  289.6 44.6 %collective-permute-start.32 = (bf16[256,2560]{1,0:T(8,128)(2,1)}, bf16[256,2560]{1,0:T(8,128)(2,1)}, u32[]{:S(2)}, u32[]{:S(2)}) collective-permute-start(bf16[256,2560]{1,0:T(8,128)(2,1)} %get-tuple-element.215), channel_id=1, source_target_pairs={{0,8},{8,0},{16,24},{24,16},{1,9},{9,1},{17,25},{25,17},{2,10},{10... | collective-permute-start | bytes 3932168 | tf_op jit(solution)/shard_map/ppermute | solution.py:831
  291.2 32.5 %collective-permute-start.16 = (bf16[128,640]{1,0:T(8,128)(2,1)S(1)}, bf16[128,640]{1,0:T(8,128)(2,1)S(1)}, u32[]{:S(2)}, u32[]{:S(2)}) collective-permute-start(bf16[128,640]{1,0:T(8,128)(2,1)S(1)} %slice.105), channel_id=1, source_target_pairs={{0,8},{8,0},{16,24},{24,16},{1,9},{9,1},{17,25},{25,17},{2,10},{10... | collective-permute-start | bytes 491528 | tf_op jit(solution)/shard_map/ppermute | solution.py:831
  292.8 48.6 %collective-permute-start.41 = (bf16[512,512]{1,0:T(8,128)(2,1)}, bf16[512,512]{1,0:T(8,128)(2,1)S(1)}, u32[]{:S(2)}, u32[]{:S(2)}) collective-permute-start(bf16[512,512]{1,0:T(8,128)(2,1)} %get-tuple-element.227), channel_id=1, source_target_pairs={{0,2},{1,3},{2,0},{3,1},{4,6},{5,7},{6,4},{7,5},{8,10},{9,11},{10,... | collective-permute-start | bytes 1572872 | tf_op jit(solution)/shard_map/ppermute | solution.py:831
  328.4 18.5 %collective-permute-start.18 = (bf16[64,640]{1,0:T(8,128)(2,1)S(1)}, bf16[64,640]{1,0:T(8,128)(2,1)}, u32[]{:S(2)}, u32[]{:S(2)}) collective-permute-start(bf16[64,640]{1,0:T(8,128)(2,1)S(1)} %add_convert_fusion.8), channel_id=1, source_target_pairs={{0,2},{1,3},{2,0},{3,1},{4,6},{5,7},{6,4},{7,5},{8,10},{9,11},{10,... | collective-permute-start | bytes 245768 | tf_op jit(solution)/shard_map/ppermute | solution.py:831
  339.4 21.9 %collective-permute-start.33 = (bf16[128,2560]{1,0:T(8,128)(2,1)}, bf16[128,2560]{1,0:T(8,128)(2,1)}, u32[]{:S(2)}, u32[]{:S(2)}) collective-permute-start(bf16[128,2560]{1,0:T(8,128)(2,1)} %get-tuple-element.217), channel_id=1, source_target_pairs={{0,8},{8,0},{16,24},{24,16},{1,9},{9,1},{17,25},{25,17},{2,10},{10... | collective-permute-start | bytes 1966088 | tf_op jit(solution)/shard_map/ppermute | solution.py:831
  339.9 22.8 %collective-permute-start.34 = (bf16[128,2560]{1,0:T(8,128)(2,1)}, bf16[128,2560]{1,0:T(8,128)(2,1)}, u32[]{:S(2)}, u32[]{:S(2)}) collective-permute-start(bf16[128,2560]{1,0:T(8,128)(2,1)} %get-tuple-element.219), channel_id=1, source_target_pairs={{0,16},{8,24},{16,0},{24,8},{1,17},{9,25},{17,1},{25,9},{2,18},{10... | collective-permute-start | bytes 1966088 | tf_op jit(solution)/shard_map/ppermute | solution.py:831
  344.2 23.0 %collective-permute-start.42 = (bf16[256,512]{1,0:T(8,128)(2,1)}, bf16[256,512]{1,0:T(8,128)(2,1)}, u32[]{:S(2)}, u32[]{:S(2)}) collective-permute-start(bf16[256,512]{1,0:T(8,128)(2,1)} %get-tuple-element.229), channel_id=1, source_target_pairs={{0,4},{1,5},{2,6},{3,7},{4,0},{5,1},{6,2},{7,3},{8,12},{9,13},{10,... | collective-permute-start | bytes 786440 | tf_op jit(solution)/shard_map/ppermute | solution.py:831
  347.8 18.1 %collective-permute-start.19 = (bf16[64,640]{1,0:T(8,128)(2,1)S(1)}, bf16[64,640]{1,0:T(8,128)(2,1)}, u32[]{:S(2)}, u32[]{:S(2)}) collective-permute-start(bf16[64,640]{1,0:T(8,128)(2,1)S(1)} %add_convert_fusion.7), channel_id=1, source_target_pairs={{0,4},{1,5},{2,6},{3,7},{4,0},{5,1},{6,2},{7,3},{8,12},{9,13},{10,... | collective-permute-start | bytes 245768 | tf_op jit(solution)/shard_map/ppermute | solution.py:831
  353.3 36.2 %all-to-all-start.3 = ((bf16[4,256,896]{2,1,0:T(8,128)(2,1)}), bf16[4,256,896]{2,1,0:T(8,128)(2,1)S(1)}, u32[]{:S(2)}, u32[]{:S(2)}) async-start(bf16[4,256,896]{2,1,0:T(8,128)(2,1)} %bitcast.41), calls=%async_computation.3 | async-start | bytes 3670016 | tf_op jit(solution)/shard_map/all_to_all | solution.py:839
  359.3 88.2 %collective-permute-start.12 = (bf16[4,12,512]{2,1,0:T(8,128)(2,1)}, bf16[4,12,512]{2,1,0:T(8,128)(2,1)}, u32[]{:S(2)}, u32[]{:S(2)}) collective-permute-start(bf16[4,12,512]{2,1,0:T(8,128)(2,1)} %bitcast.86), channel_id=1, source_target_pairs={{0,8},{8,0},{16,24},{24,16},{1,9},{9,1},{17,25},{25,17},{2,10},{10... | collective-permute-start | bytes 147464 | tf_op jit(solution)/shard_map/ppermute | solution.py:831
  361.3 86.4 %collective-permute-start.13 = (bf16[4,12,512]{2,1,0:T(8,128)(2,1)}, bf16[4,12,512]{2,1,0:T(8,128)(2,1)}, u32[]{:S(2)}, u32[]{:S(2)}) collective-permute-start(bf16[4,12,512]{2,1,0:T(8,128)(2,1)} %bitcast.85), channel_id=1, source_target_pairs={{0,16},{8,24},{16,0},{24,8},{1,17},{9,25},{17,1},{25,9},{2,18},{10... | collective-permute-start | bytes 147464 | tf_op jit(solution)/shard_map/ppermute | solution.py:831
  362.7 85.0 %collective-permute-start.14 = (bf16[4,12,512]{2,1,0:T(8,128)(2,1)}, bf16[4,12,512]{2,1,0:T(8,128)(2,1)}, u32[]{:S(2)}, u32[]{:S(2)}) collective-permute-start(bf16[4,12,512]{2,1,0:T(8,128)(2,1)} %bitcast.84), channel_id=1, source_target_pairs={{0,24},{8,16},{16,8},{24,0},{1,25},{9,17},{17,9},{25,1},{2,26},{10... | collective-permute-start | bytes 147464 | tf_op jit(solution)/shard_map/ppermute | solution.py:831
  365.9 19.9 %collective-permute-start.35 = (bf16[128,2560]{1,0:T(8,128)(2,1)}, bf16[128,2560]{1,0:T(8,128)(2,1)S(1)}, u32[]{:S(2)}, u32[]{:S(2)}) collective-permute-start(bf16[128,2560]{1,0:T(8,128)(2,1)} %get-tuple-element.221), channel_id=1, source_target_pairs={{0,2},{1,3},{2,0},{3,1},{4,6},{5,7},{6,4},{7,5},{8,10},{9,11},{10,... | collective-permute-start | bytes 1966088 | tf_op jit(solution)/shard_map/ppermute | solution.py:831
  368.6 32.8 %collective-permute-start.43 = (bf16[256,512]{1,0:T(8,128)(2,1)S(1)}, bf16[256,512]{1,0:T(8,128)(2,1)}, u32[]{:S(2)}, u32[]{:S(2)}) collective-permute-start(bf16[256,512]{1,0:T(8,128)(2,1)S(1)} %add_convert_fusion.3), channel_id=1, source_target_pairs={{0,4},{1,5},{2,6},{3,7},{4,0},{5,1},{6,2},{7,3},{8,12},{9,13},{10,... | collective-permute-start | bytes 786440 | tf_op jit(solution)/shard_map/ppermute | solution.py:831
  388.8 10.7 %collective-permute-start.36 = (bf16[64,2560]{1,0:T(8,128)(2,1)}, bf16[64,2560]{1,0:T(8,128)(2,1)S(1)}, u32[]{:S(2)}, u32[]{:S(2)}) collective-permute-start(bf16[64,2560]{1,0:T(8,128)(2,1)} %get-tuple-element.223), channel_id=1, source_target_pairs={{0,4},{1,5},{2,6},{3,7},{4,0},{5,1},{6,2},{7,3},{8,12},{9,13},{10,... | collective-permute-start | bytes 983048 | tf_op jit(solution)/shard_map/ppermute | solution.py:831
  400.3 15.8 %collective-permute-start.25 = (bf16[128,2048]{1,0:T(8,128)(2,1)}, bf16[128,2048]{1,0:T(8,128)(2,1)S(1)}, u32[]{:S(2)}, u32[]{:S(2)}) collective-permute-start(bf16[128,2048]{1,0:T(8,128)(2,1)} %get-tuple-element.207), channel_id=1, source_target_pairs={{0,2},{1,3},{2,0},{3,1},{4,6},{5,7},{6,4},{7,5},{8,10},{9,11},{10,... | collective-permute-start | bytes 1572872 | tf_op jit(solution)/shard_map/ppermute | solution.py:831
  401.4 19.6 %collective-permute-start.37 = (bf16[64,2560]{1,0:T(8,128)(2,1)S(1)}, bf16[64,2560]{1,0:T(8,128)(2,1)S(1)}, u32[]{:S(2)}, u32[]{:S(2)}) collective-permute-start(bf16[64,2560]{1,0:T(8,128)(2,1)S(1)} %add_convert_fusion.1), channel_id=1, source_target_pairs={{0,4},{1,5},{2,6},{3,7},{4,0},{5,1},{6,2},{7,3},{8,12},{9,13},{10,... | collective-permute-start | bytes 983048 | tf_op jit(solution)/shard_map/ppermute | solution.py:831
  416.1 33.7 %collective-permute-start.23 = (bf16[64,1152]{1,0:T(8,128)(2,1)S(1)}, bf16[64,1152]{1,0:T(8,128)(2,1)}, u32[]{:S(2)}, u32[]{:S(2)}) collective-permute-start(bf16[64,1152]{1,0:T(8,128)(2,1)S(1)} %pad_maximum_fusion.8.refs_0_), channel_id=1, source_target_pairs={{0,24},{8,16},{16,8},{24,0},{1,25},{9,17},{17,9},{25,1},{2,26},{10... | collective-permute-start | bytes 442376 | tf_op jit(solution)/shard_map/ppermute | solution.py:831
  421.0 12.2 %collective-permute-start.26 = (bf16[64,2048]{1,0:T(8,128)(2,1)}, bf16[64,2048]{1,0:T(8,128)(2,1)S(1)}, u32[]{:S(2)}, u32[]{:S(2)}) collective-permute-start(bf16[64,2048]{1,0:T(8,128)(2,1)} %get-tuple-element.209), channel_id=1, source_target_pairs={{0,4},{1,5},{2,6},{3,7},{4,0},{5,1},{6,2},{7,3},{8,12},{9,13},{10,... | collective-permute-start | bytes 786440 | tf_op jit(solution)/shard_map/ppermute | solution.py:831
  434.3 12.6 %collective-permute-start.27 = (bf16[64,2048]{1,0:T(8,128)(2,1)S(1)}, bf16[64,2048]{1,0:T(8,128)(2,1)S(1)}, u32[]{:S(2)}, u32[]{:S(2)}) collective-permute-start(bf16[64,2048]{1,0:T(8,128)(2,1)S(1)} %add_convert_fusion.4), channel_id=1, source_target_pairs={{0,4},{1,5},{2,6},{3,7},{4,0},{5,1},{6,2},{7,3},{8,12},{9,13},{10,... | collective-permute-start | bytes 786440 | tf_op jit(solution)/shard_map/ppermute | solution.py:831
  446.9 5.1 collective-permute-start.22
  447.5 17.7 %collective-permute-start.38 = (bf16[128,2560]{1,0:T(8,128)(2,1)S(1)}, bf16[128,2560]{1,0:T(8,128)(2,1)S(1)}, u32[]{:S(2)}, u32[]{:S(2)}) collective-permute-start(bf16[128,2560]{1,0:T(8,128)(2,1)S(1)} %pad_maximum_fusion.2.refs_0_), channel_id=1, source_target_pairs={{0,2},{1,3},{2,0},{3,1},{4,6},{5,7},{6,4},{7,5},{8,10},{9,11},{10,... | collective-permute-start | bytes 1966088 | tf_op jit(solution)/shard_map/ppermute | solution.py:831
  447.7 28.9 %collective-permute-start.45 = (bf16[512,512]{1,0:T(8,128)(2,1)S(1)}, bf16[512,512]{1,0:T(8,128)(2,1)}, u32[]{:S(2)}, u32[]{:S(2)}) collective-permute-start(bf16[512,512]{1,0:T(8,128)(2,1)S(1)} %pad_maximum_fusion.4.refs_0_), channel_id=1, source_target_pairs={{0,1},{1,0},{2,3},{3,2},{4,5},{5,4},{6,7},{7,6},{8,9},{9,8},{10,11... | collective-permute-start | bytes 1572872 | tf_op jit(solution)/shard_map/ppermute | solution.py:831
  447.8 28.8 %collective-permute-start.44 = (bf16[512,512]{1,0:T(8,128)(2,1)S(1)}, bf16[512,512]{1,0:T(8,128)(2,1)}, u32[]{:S(2)}, u32[]{:S(2)}) collective-permute-start(bf16[512,512]{1,0:T(8,128)(2,1)S(1)} %pad_maximum_fusion.4.refs_0_), channel_id=1, source_target_pairs={{0,2},{1,3},{2,0},{3,1},{4,6},{5,7},{6,4},{7,5},{8,10},{9,11},{10,... | collective-permute-start | bytes 1572872 | tf_op jit(solution)/shard_map/ppermute | solution.py:831
  449.8 34.5 %collective-permute-start.28 = (bf16[128,2048]{1,0:T(8,128)(2,1)S(1)}, bf16[128,2048]{1,0:T(8,128)(2,1)}, u32[]{:S(2)}, u32[]{:S(2)}) collective-permute-start(bf16[128,2048]{1,0:T(8,128)(2,1)S(1)} %pad_maximum_fusion.3.refs_0_), channel_id=1, source_target_pairs={{0,2},{1,3},{2,0},{3,1},{4,6},{5,7},{6,4},{7,5},{8,10},{9,11},{10,... | collective-permute-start | bytes 1572872 | tf_op jit(solution)/shard_map/ppermute | solution.py:831
  452.0 5.2 %collective-permute-start.21 = (bf16[64,1152]{1,0:T(8,128)(2,1)S(1)}, bf16[64,1152]{1,0:T(8,128)(2,1)}, u32[]{:S(2)}, u32[]{:S(2)}) collective-permute-start(bf16[64,1152]{1,0:T(8,128)(2,1)S(1)} %pad_maximum_fusion.8.refs_0_), channel_id=1, source_target_pairs={{0,8},{8,0},{16,24},{24,16},{1,9},{9,1},{17,25},{25,17},{2,10},{10... | collective-permute-start | bytes 442376 | tf_op jit(solution)/shard_map/ppermute | solution.py:831
  457.3 48.5 %collective-permute-start.39 = (bf16[128,2560]{1,0:T(8,128)(2,1)S(1)}, bf16[128,2560]{1,0:T(8,128)(2,1)}, u32[]{:S(2)}, u32[]{:S(2)}) collective-permute-start(bf16[128,2560]{1,0:T(8,128)(2,1)S(1)} %pad_maximum_fusion.2.refs_0_), channel_id=1, source_target_pairs={{0,1},{1,0},{2,3},{3,2},{4,5},{5,4},{6,7},{7,6},{8,9},{9,8},{10,11... | collective-permute-start | bytes 1966088 | tf_op jit(solution)/shard_map/ppermute | solution.py:831
  465.2 40.6 %collective-permute-start.40 = (bf16[128,2560]{1,0:T(8,128)(2,1)S(1)}, bf16[128,2560]{1,0:T(8,128)(2,1)}, u32[]{:S(2)}, u32[]{:S(2)}) collective-permute-start(bf16[128,2560]{1,0:T(8,128)(2,1)S(1)} %collective-permute-done.38.refs_1_), channel_id=1, source_target_pairs={{0,1},{1,0},{2,3},{3,2},{4,5},{5,4},{6,7},{7,6},{8,9},{9,8},{10,11... | collective-permute-start | bytes 1966088 | tf_op jit(solution)/shard_map/ppermute | solution.py:831
  476.6 25.4 %collective-permute-start.46 = (bf16[512,512]{1,0:T(8,128)(2,1)}, bf16[512,512]{1,0:T(8,128)(2,1)}, u32[]{:S(2)}, u32[]{:S(2)}) collective-permute-start(bf16[512,512]{1,0:T(8,128)(2,1)} %collective-permute-done.44.refs_1_), channel_id=1, source_target_pairs={{0,1},{1,0},{2,3},{3,2},{4,5},{5,4},{6,7},{7,6},{8,9},{9,8},{10,11... | collective-permute-start | bytes 1572872 | tf_op jit(solution)/shard_map/ppermute | solution.py:831
  476.6 33.6 %collective-permute-start.29 = (bf16[128,2048]{1,0:T(8,128)(2,1)S(1)}, bf16[128,2048]{1,0:T(8,128)(2,1)S(1)}, u32[]{:S(2)}, u32[]{:S(2)}) collective-permute-start(bf16[128,2048]{1,0:T(8,128)(2,1)S(1)} %pad_maximum_fusion.3.refs_0_), channel_id=1, source_target_pairs={{0,1},{1,0},{2,3},{3,2},{4,5},{5,4},{6,7},{7,6},{8,9},{9,8},{10,11... | collective-permute-start | bytes 1572872 | tf_op jit(solution)/shard_map/ppermute | solution.py:831
  484.3 25.9 %collective-permute-start.30 = (bf16[128,2048]{1,0:T(8,128)(2,1)}, bf16[128,2048]{1,0:T(8,128)(2,1)}, u32[]{:S(2)}, u32[]{:S(2)}) collective-permute-start(bf16[128,2048]{1,0:T(8,128)(2,1)} %collective-permute-done.28.refs_1_), channel_id=1, source_target_pairs={{0,1},{1,0},{2,3},{3,2},{4,5},{5,4},{6,7},{7,6},{8,9},{9,8},{10,11... | collective-permute-start | bytes 1572872 | tf_op jit(solution)/shard_map/ppermute | solution.py:831
  (63 other events, 731.5 us)
